TPU v7x, 128 devices: a whole 4x4x4 slice. The times are simulated.
128 devices in a mesh: row: 8 (over x_hi, z), col: 8 (over x_lo, y), layer: 2 (over core).
Axes of the slice: x: 4 (x_hi: 2, x_lo: 2; x = x_hi * 2 + x_lo), y: 4, z: 4, core: 2. Of those that a mesh axis runs over, the one named last changes fastest.
Arguments:
- matrix: float32 [32, 512, 32, 512], P('row', None, 'col', 'layer'), may hold values from -40 to 40, as said below
- transforms: float32 [1, 16, 1024, 1024], P(None, 'row', ('col', 'layer')), may hold values from -0.1875 to 0.1875
Outputs:
- swept: float32 [32, 512, 32, 512], P('row', None, 'col', 'layer')
Inputs may be any that keep to these rules, and one draw needn't show every extreme that they name: `matrix`: symmetric: entry [i, a, j, b] equals entry [j, b, i, a].
All inputs are finite; a program needn't handle non-finite values.
Results may differ from a plain program's by a relative error of at most 0.0001.
Values sent between devices are 32-bit elements; how exact they have to be, the bound alone decides.
No kernel may reach another device: no remote copies, remote signals or barrier semaphores. Data moves between devices by JAX's collectives and lax.ppermute only.
A program may use at most 192 MiB of HBM per device.

v0:
```python
import jax
import jax.numpy as jnp
from jax import lax
from jax.sharding import PartitionSpec as P

exact_mode = lax.Precision.HIGHEST


def broadcast(x, axis, root):
    mine = lax.axis_index(axis) == root
    return lax.psum(jnp.where(mine, x, jnp.zeros_like(x)), axis)


def cut_along(x, dim, count):
    before, after = (x.shape[:dim], x.shape[dim + 1 :])
    return jnp.moveaxis(x.reshape(*before, count, -1, *after), dim, 0)


def sum_at_owner(x, axis, dim):
    count = lax.axis_size(axis)
    blocks = lax.all_to_all(cut_along(x, dim, count), axis, 0, 0, tiled=True)
    return jnp.sum(blocks, axis=0)


def passed_along(block, axis, distance):
    devices = range(lax.axis_size(axis))
    route = [(i - distance, i) for i in devices if i - distance in devices]
    return lax.ppermute(block, axis, route)


def split_slots(array, axis_dim):
    return [
        lax.index_in_dim(array, index, axis_dim, keepdims=False)
        for index in range(array.shape[axis_dim])
    ]


def leading(slots):
    width = len(slots)
    return slots[width - 2]


def rearranged(slots, from_prev, from_next, position, count):
    width = len(slots)
    result = [jnp.where(position == 0, slots[0], from_prev)]
    for local in range(1, width):
        if local % 2 == 1:
            if local == width - 1:
                result.append(jnp.where(position == count - 1, slots[width - 2], from_next))
            else:
                result.append(slots[local + 2])
        else:
            result.append(jnp.where(position == 0, slots[1], slots[0]))
    return result


def shards(matrix, transforms):
    pair_dev = matrix.shape[0] // 2
    block_size = matrix.shape[1]
    half_width = matrix.shape[3]
    width = 2 * pair_dev
    pairs_row = lax.axis_size("row")
    pairs_col = lax.axis_size("col")
    row_pos = lax.axis_index("row")
    col_pos = lax.axis_index("col")
    layer_pos = lax.axis_index("layer")
    current = matrix
    left_panel = lax.all_gather(transforms[0], ("col", "layer"), axis=1, tiled=True)
    shaped = left_panel.reshape(pair_dev, 2, block_size, 2 * block_size)
    selected = lax.dynamic_slice_in_dim(shaped, layer_pos * half_width, half_width, 2)
    right_part = broadcast(selected, "row", col_pos)
    grouped = current.reshape(pair_dev, 2 * block_size, width * half_width)
    partial_rows = jnp.einsum(
        "pka,pkc->pac",
        left_panel,
        grouped,
        precision=exact_mode,
        preferred_element_type=jnp.float32,
    )
    partial_rows = partial_rows.reshape(pair_dev, 2 * block_size, pair_dev, 2, half_width)
    term_pairs = jnp.einsum(
        "paqmh,qmhb->paqb",
        partial_rows,
        right_part,
        precision=exact_mode,
        preferred_element_type=jnp.float32,
    )
    term_pairs = term_pairs.reshape(pair_dev, 2 * block_size, pair_dev, 2, 2, half_width)
    rotated = sum_at_owner(term_pairs, "layer", 4)
    rotated = rotated.reshape(width, block_size, width, half_width)
    rows = split_slots(rotated, 0)
    upward = passed_along(leading(rows), "row", 1)
    downward = passed_along(rows[1], "row", -1)
    moved = jnp.stack(rearranged(rows, upward, downward, row_pos, pairs_row), 0)
    cols = split_slots(moved, 2)
    upward_cols = passed_along(leading(cols), "col", 1)
    downward_cols = passed_along(cols[1], "col", -1)
    current = jnp.stack(rearranged(cols, upward_cols, downward_cols, col_pos, pairs_col), 2)
    return current


def solution(mesh):
    return jax.shard_map(
        shards,
        mesh=mesh,
        in_specs=(P("row", None, "col", "layer"), P(None, "row", ("col", "layer"), None)),
        out_specs=P("row", None, "col", "layer"),
        check_vma=False,
    )
```

profile of v0, /device:TPU:6, one launch (start us, length us, event | category | flops | bytes accessed | tf_op | source)
XLA Modules:
  0.0 410.4 jit_solution(15162404626442989335)
XLA Ops:
  7.3 56.1 %all-gather.3.cloned.1.call-done = f32[1,2,1024,1024]{3,2,1,0:T(8,128)} async-done(((f32[1,2,64,1024]{3,2,1,0:T(8,128)}), f32[1,2,1024,1024]{3,2,1,0:T(8,128)}) %all-gather.3.cloned.1.call-update) | async-done | bytes 8388624 | tf_op jit(solution)/shard_map/all_gather | solution.py:68
  63.4 4.8 %constant_dynamic-slice_fusion = f32[2,2,256,1024]{3,2,1,0:T(8,128)} fusion(f32[2,2,512,1024]{3,2,1,0:T(8,128)} %bitcast.73, s32[]{:T(128)S(6)} %select_n.56), kind=kLoop, calls=%fused_computation.23 | loop fusion | bytes 8388612 | tf_op jit(solution)/shard_map/dynamic_slice | solution.py:70
  68.2 5.4 %copy.45 = f32[2,2,256,1024]{2,3,1,0:T(8,128)} copy(f32[2,2,256,1024]{3,2,1,0:T(8,128)} %constant_dynamic-slice_fusion) | data formatting | bytes 8388608
  73.6 4.5 %broadcast_select_fusion = f32[2,2,256,1024]{2,3,1,0:T(8,128)} fusion(f32[2,2,256,1024]{2,3,1,0:T(8,128)} %copy.45, pred[]{:T(512)S(6)} %eq.19), kind=kLoop, calls=%fused_computation.20 | loop fusion | flops 1048576 | bytes 8388609 | tf_op jit(solution)/shard_map/jit(_where)/select_n | solution.py:11
  78.1 10.7 %reshape.15 = f32[2,1024,1024]{2,1,0:T(8,128)} reshape(f32[4,512,4,256]{3,2,1,0:T(4,128)} %param.2) | data formatting | bytes 16777216 | tf_op jit(solution)/shard_map/reshape | solution.py:72
  88.8 31.5 %fusion.2 = f32[2,1024,1024]{1,2,0:T(8,128)} fusion(f32[2,1024,1024]{2,1,0:T(8,128)} %reshape.15, f32[1,2,1024,1024]{3,2,1,0:T(8,128)} %all-gather.3.cloned.1.call-done), kind=kOutput, calls=%fused_computation.5 | convolution fusion | flops 25769803776 | bytes 25165824 | tf_op jit(solution)/shard_map/pka,pkc->pac/dot_general | solution.py:73
  120.3 67.2 %all-reduce.2.cloned.1.call-done = f32[2,2,256,1024]{2,3,1,0:T(8,128)} async-done(((f32[2,2,256,1024]{2,3,1,0:T(8,128)}), f32[2,2,256,1024]{2,3,1,0:T(8,128)}) %all-reduce.2.cloned.1.call-update) | async-done | bytes 4194320 | tf_op jit(solution)/shard_map/psum | solution.py:11
  187.5 31.1 %fusion = f32[2,1024,2,1024,1]{3,1,4,2,0:T(8,128)S(1)} fusion(f32[2,1024,2,2,256]{1,4,3,2,0:T(8,128)} %bitcast.72, f32[2,2,256,1024]{2,3,1,0:T(8,128)} %all-reduce.2.cloned.1.call-done), kind=kOutput, calls=%fused_computation.3 | convolution fusion | flops 25769803776 | bytes 29360128 | tf_op jit(solution)/shard_map/paqmh,qmhb->paqb/dot_general | solution.py:81
  218.6 2.9 copy.55
  221.5 19.0 %all_to_all.5 = f32[2,2,1024,2,2,1,256]{2,6,4,1,3,5,0:T(8,128)} all-to-all(f32[2,2,1024,2,2,1,256]{2,6,4,1,3,5,0:T(8,128)S(1)} %bitcast.68), channel_id=1, replica_groups=mesh['row'=8,'col'=8,'layer'=2] {'layer'}, dimensions={0} | all-to-all | bytes 33554432 | tf_op jit(solution)/shard_map/all_to_all | solution.py:21
  240.6 12.2 %reduce_sum.9 = f32[2,1024,2,2,256]{1,4,3,0,2:T(8,128)} reduce(f32[2,2,1024,2,2,1,256]{2,6,4,1,3,5,0:T(8,128)} %all_to_all.5, f32[]{:T(128)} %constant.21.clone.1), dimensions={0,5}, to_apply=%region_1.2 | reduce | flops 2097152 | bytes 25165828 | tf_op jit(solution)/shard_map/reduce_sum | solution.py:22
  252.8 8.7 %copy.29 = f32[2,1024,2,2,256]{4,1,0,3,2:T(8,128)} copy(f32[2,1024,2,2,256]{1,4,3,0,2:T(8,128)} %reduce_sum.9) | data formatting | bytes 16777216 | tf_op jit(solution)/shard_map/reduce_sum | solution.py:22
  261.5 5.4 %slice_bitcast_fusion.3 = (f32[512,4,256]{2,0,1:T(8,128)}, f32[512,4,256]{2,0,1:T(8,128)}, f32[1,512,4,256]{3,1,2,0:T(8,128)S(1)}) fusion(f32[4,512,4,256]{3,1,0,2:T(8,128)} %bitcast.69), kind=kLoop, calls=%fused_computation.11 | loop fusion | bytes 12582912 | tf_op jit(solution)/shard_map/squeeze | solution.py:33
  268.8 7.5 %collective-permute-start.1 = (f32[512,4,256]{2,0,1:T(8,128)}, f32[512,4,256]{2,0,1:T(8,128)}, u32[]{:S(2)}, u32[]{:S(2)}) collective-permute-start(f32[512,4,256]{2,0,1:T(8,128)} %get-tuple-element.13), channel_id=1, source_target_pairs={{16,0},{32,16},{48,32},{64,48},{80,64},{96,80},{112,96},{17,1},{33... | collective-permute-start | bytes 6291464 | tf_op jit(solution)/shard_map/ppermute | solution.py:28
  278.9 41.5 %collective-permute-done = f32[512,4,256]{2,0,1:T(8,128)} collective-permute-done((f32[512,4,256]{2,0,1:T(8,128)}, f32[512,4,256]{2,0,1:T(8,128)}, u32[]{:S(2)}, u32[]{:S(2)}) %collective-permute-start) | collective-permute-done | bytes 2097184 | tf_op jit(solution)/shard_map/ppermute | solution.py:28
  321.5 4.2 %fusion.6 = (f32[1,512,4,256]{3,1,2,0:T(8,128)S(1)}, f32[1,512,4,256]{3,1,2,0:T(8,128)S(1)}) fusion(f32[512,4,256]{2,0,1:T(8,128)} %collective-permute-done, f32[4,512,4,256]{3,1,0,2:T(8,128)} %bitcast.71, pred[]{:T(512)S(6)} %eq.18, f32[512,4,256]{2,0,1:T(8,128)} %collective-permute-done.1, pred[]{:T(512)S(6)} %eq.20), kind=kLoop, calls=%fused_computation.16 | loop fusion | flops 1048576 | bytes 12582914 | tf_op jit(solution)/shard_map/stack | solution.py:94
  326.8 3.0 slice_bitcast_fusion.1
  331.4 3.4 collective-permute-start.2
  334.8 4.6 %collective-permute-start.3 = (f32[4,512,256]{2,1,0:T(8,128)}, f32[4,512,256]{2,1,0:T(8,128)}, u32[]{:S(2)}, u32[]{:S(2)}) collective-permute-start(f32[4,512,256]{2,1,0:T(8,128)} %get-tuple-element.8), channel_id=1, source_target_pairs={{2,0},{4,2},{6,4},{8,6},{10,8},{12,10},{14,12},{3,1},{5,3},{7,5},{... | collective-permute-start | bytes 6291464 | tf_op jit(solution)/shard_map/ppermute | solution.py:28
  339.4 2.5 bitcast_select_fusion.1
  341.9 40.3 %collective-permute-done.2 = f32[4,512,256]{2,1,0:T(8,128)} collective-permute-done((f32[4,512,256]{2,1,0:T(8,128)}, f32[4,512,256]{2,1,0:T(8,128)}, u32[]{:S(2)}, u32[]{:S(2)}) %collective-permute-start.2) | collective-permute-done | bytes 2097184 | tf_op jit(solution)/shard_map/ppermute | solution.py:28
  383.5 4.2 %fusion.5 = (f32[4,512,1,256]{3,1,0,2:T(8,128)S(1)}, f32[4,512,1,256]{3,1,0,2:T(8,128)S(1)}) fusion(f32[4,512,256]{2,1,0:T(8,128)} %collective-permute-done.2, f32[4,512,4,256]{3,1,2,0:T(8,128)} %copy-done, pred[]{:T(512)S(6)} %eq.17, f32[4,512,256]{2,1,0:T(8,128)} %collective-permute-done.3, pred[]{:T(512)S(6)} %eq.21), kind=kLoop, calls=%fused_computation.13 | loop fusion | flops 1048576 | bytes 12582914 | tf_op jit(solution)/shard_map/stack | solution.py:98
  387.7 3.7 pad_maximum_fusion.1
  391.4 12.2 %copy.38 = f32[4,512,4,256]{3,2,1,0:T(4,128)} copy(f32[4,512,4,256]{3,1,0,2:T(8,128)} %pad_maximum_fusion.1) | data formatting | bytes 16777216 | tf_op jit(solution)/shard_map/stack | solution.py:98
  (11 shorter events, 10.2 us)
Async XLA Ops:
  6.5 56.9 %all-gather.3.cloned.1.call-start = ((), (), s32[]{:S(2)}) async-start(), calls=%async_computation.2 | async-start | bytes 8912896 | tf_op jit(solution)/shard_map/all_gather | solution.py:68
  7.3 180.2 %all-reduce.2.cloned.1.call-start = ((), (), s32[]{:S(2)}) async-start(), calls=%async_computation.1 | async-start | bytes 8388608 | tf_op jit(solution)/shard_map/psum | solution.py:11
  266.9 53.5 %collective-permute-start = (f32[512,4,256]{2,0,1:T(8,128)}, f32[512,4,256]{2,0,1:T(8,128)}, u32[]{:S(2)}, u32[]{:S(2)}) collective-permute-start(f32[512,4,256]{2,0,1:T(8,128)} %get-tuple-element.12), channel_id=1, source_target_pairs={{0,16},{16,32},{32,48},{48,64},{64,80},{80,96},{96,112},{1,17},{17... | collective-permute-start | bytes 6291464 | tf_op jit(solution)/shard_map/ppermute | solution.py:28
  268.8 52.7 %collective-permute-start.1 = (f32[512,4,256]{2,0,1:T(8,128)}, f32[512,4,256]{2,0,1:T(8,128)}, u32[]{:S(2)}, u32[]{:S(2)}) collective-permute-start(f32[512,4,256]{2,0,1:T(8,128)} %get-tuple-element.13), channel_id=1, source_target_pairs={{16,0},{32,16},{48,32},{64,48},{80,64},{96,80},{112,96},{17,1},{33... | collective-permute-start | bytes 6291464 | tf_op jit(solution)/shard_map/ppermute | solution.py:28
  326.8 4.7 %copy-start = (f32[4,512,4,256]{3,1,2,0:T(8,128)}, f32[4,512,4,256]{3,1,2,0:T(8,128)S(1)}, u32[]{:S(2)}) copy-start(f32[4,512,4,256]{3,1,2,0:T(8,128)S(1)} %pad_maximum_fusion) | copy-start | bytes 25165828
  331.4 50.8 %collective-permute-start.2 = (f32[4,512,256]{2,1,0:T(8,128)}, f32[4,512,256]{2,1,0:T(8,128)}, u32[]{:S(2)}, u32[]{:S(2)}) collective-permute-start(f32[4,512,256]{2,1,0:T(8,128)} %get-tuple-element.7), channel_id=1, source_target_pairs={{0,2},{2,4},{4,6},{6,8},{8,10},{10,12},{12,14},{1,3},{3,5},{5,7},{... | collective-permute-start | bytes 6291464 | tf_op jit(solution)/shard_map/ppermute | solution.py:28
  334.8 48.6 %collective-permute-start.3 = (f32[4,512,256]{2,1,0:T(8,128)}, f32[4,512,256]{2,1,0:T(8,128)}, u32[]{:S(2)}, u32[]{:S(2)}) collective-permute-start(f32[4,512,256]{2,1,0:T(8,128)} %get-tuple-element.8), channel_id=1, source_target_pairs={{2,0},{4,2},{6,4},{8,6},{10,8},{12,10},{14,12},{3,1},{5,3},{7,5},{... | collective-permute-start | bytes 6291464 | tf_op jit(solution)/shard_map/ppermute | solution.py:28
Sparse Core Ops, SparseCore 0:
  9.0 54.3 all-gather.2
  78.2 109.2 all-reduce.1
where the time goes:
time: 414 us; the launch traced here: 410 us
  waiting for transfers between devices  208 us (50%)
  matrix products  62.6 us (15%)
  local copies, waits for them, and re-layouts  54.7 us (13%)
  other arithmetic  34.9 us (8%)
  blocking collectives  19 us (5%)
  starting transfers between devices  17.4 us (4%)
  between operations  13.5 us (3%)
    ppermute x4, waiting for transfers between devices, passed_along(): return lax.ppermute(block, axis, route)  84.2 us
    psum x1, waiting for transfers between devices, broadcast(): return lax.psum(jnp.where(mine, x, jnp.zeros_like(x)), axis)  67.2 us
    all_gather x1, waiting for transfers between devices, shards(): lax.all_gather(transforms[0], ('col', 'layer'), axis=1, tiled=True)  56.1 us
    dot_general x1, matrix products, shards(): jnp.einsum('pka,pkc->pac', left_panel, grouped, precision=exact_mode, pre...  31.5 us
    dot_general x1, matrix products, shards(): jnp.einsum('paqmh,qmhb->paqb', partial_rows, right_part, precision=exact_...  31.1 us
    all_to_all x1, blocking collectives, sum_at_owner(): blocks = lax.all_to_all(cut_along(x, dim, count), axis, 0, 0, tiled=True)  19 us
    ppermute x4, starting transfers between devices, passed_along(): return lax.ppermute(block, axis, route)  17.4 us
    reduce_sum x1, other arithmetic, sum_at_owner(): return jnp.sum(blocks, axis=0)  12.2 us
  transfers between devices with their start and end apart: 6, of which 6 were waited for; matrix products, arithmetic and copies ran while one was open for 12% of the time, Pallas kernels for 0%

commit v1 on v0

v1 whole, which is shorter than its diff:
```python
import jax
import jax.numpy as jnp
from jax import lax
from jax.experimental import pallas as pl
from jax.experimental.pallas import tpu as pltpu
from jax.sharding import PartitionSpec as P

F32 = jnp.float32
BF16 = jnp.bfloat16
AXES = ("row", "col", "layer")
VMEM_LIMIT = 56 * 1024 * 1024


def route(place):
    pairs = []
    for r in range(8):
        for c in range(8):
            for l in range(2):
                to = place(r, c, l)
                if to is not None:
                    pairs.append(((r * 8 + c) * 2 + l, (to[0] * 8 + to[1]) * 2 + to[2]))
    return pairs


def send(x, place):
    return lax.ppermute(x, AXES, route(place))


def split(x):
    high = x.astype(BF16)
    return high, (x - high.astype(F32)).astype(BF16)


def product(ah, al, bh, bl):
    def dot(a, b):
        return jnp.dot(a, b, preferred_element_type=F32)

    return dot(ah, bh) + (dot(ah, bl) + dot(al, bh))


def left_kernel(j_ref, own_ref, other_ref, *refs):
    yh_ref, yl_ref, jh, jl = refs[-4:]

    @pl.when(pl.program_id(0) == 0)
    def _():
        for k in range(4):
            cols = pl.ds(k * 256, 256)
            high, low = split(j_ref[cols, :].T)
            jh[:, cols] = high
            jl[:, cols] = low

    mh, ml = split(jnp.concatenate([own_ref[0], other_ref[0]], axis=1))
    for a in range(4):
        rows = pl.ds(a * 256, 256)
        high, low = split(product(jh[rows, :], jl[rows, :], mh, ml))
        yh_ref[rows, :] = high
        yl_ref[rows, :] = low


def left_product(pair, panel, own, other, previous):
    block = pl.BlockSpec((1, 1024, 256), lambda s: (s, pair, 0))
    out = pl.BlockSpec((1024, 512), lambda s: (pair, s))
    shape = jax.ShapeDtypeStruct((2048, 2048), BF16)
    extra = [] if previous is None else list(previous)
    return pl.pallas_call(
        left_kernel,
        grid=(4,),
        in_specs=[pl.BlockSpec((1024, 1024), lambda s: (0, 0)), block, block]
        + [pl.BlockSpec(memory_space=pl.ANY)] * len(extra),
        out_specs=[out, out],
        out_shape=[shape, shape],
        scratch_shapes=[pltpu.VMEM((1024, 1024), BF16), pltpu.VMEM((1024, 1024), BF16)],
        input_output_aliases={3: 0, 4: 1} if extra else {},
        compiler_params=pltpu.CompilerParams(vmem_limit_bytes=VMEM_LIMIT),
        cost_estimate=pl.CostEstimate(
            flops=3 * 2 * 1024 * 1024 * 2048, bytes_accessed=20 << 20, transcendentals=0
        ),
        name="left_product",
    )(panel, own, other, *extra)


def holders(r):
    up = (r & 4) | ((r + 3) & 3)
    down = (r & 4) | ((r + 1) & 3)
    far = (r & 4) | ((r + 2) & 3)
    return [r, r ^ 4, up, up ^ 4, down, down ^ 4, far, far ^ 4]


def right_kernel(where, yh_ref, yl_ref, *refs):
    pieces = refs[:8]
    up_ref, down_ref, first_ref, jh, jl = refs[8], refs[9], refs[10], refs[-2], refs[-1]
    stay_refs = refs[11:-2]
    q = pl.program_id(0)
    slot = pl.program_id(1)
    row_pos = where[0]
    layer = where[2]

    @pl.when((q == 0) & (slot == 0))
    def _():
        for start, piece in zip(holders(row_pos), pieces):
            base = (start ^ (2 * layer)) * 128
            for pair in range(2):
                for half in range(2):
                    high, low = split(piece[0, pair, half])
                    rows = pl.ds(pl.multiple_of(base + half * 64, 64), 64)
                    jh[pair, rows, :] = high
                    jl[pair, rows, :] = low

    block = product(yh_ref[...], yl_ref[...], jh[q], jl[q])

    def keep(index, value):
        if len(stay_refs) == 1:
            stay_refs[0][index, q] = value
        else:
            for pair in range(2):

                @pl.when(q == pair)
                def _(pair=pair):
                    stay_refs[pair][index] = value

    @pl.when(slot == 0)
    def _():
        first_ref[q] = block

        @pl.when(row_pos > 0)
        def _():
            keep(1, block)

    @pl.when(slot == 1)
    def _():
        down_ref[q] = block

        @pl.when(row_pos == 0)
        def _():
            keep(1, block)

    @pl.when(slot == 2)
    def _():
        up_ref[q] = block

    @pl.when(slot == 3)
    def _():
        keep(0, block)


def right_product(which, where, yh, yl, pieces, separate):
    y_block = pl.BlockSpec((512, 1024), lambda q, s, w: (s, q))
    piece = pl.BlockSpec((1, 2, 2, 64, 256), lambda q, s, w: (which, 0, 0, 0, 0))
    pair_block = pl.BlockSpec((2, 512, 256), lambda q, s, w: (0, 0, 0))
    pair_shape = jax.ShapeDtypeStruct((2, 512, 256), F32)
    if separate:
        stay_specs, stay_shapes = [pair_block] * 2, [pair_shape] * 2
    else:
        stay_specs = [pl.BlockSpec((2, 2, 512, 256), lambda q, s, w: (0, 0, 0, 0))]
        stay_shapes = [jax.ShapeDtypeStruct((2, 2, 512, 256), F32)]
    return pl.pallas_call(
        right_kernel,
        grid_spec=pltpu.PrefetchScalarGridSpec(
            num_scalar_prefetch=1,
            grid=(2, 4),
            in_specs=[y_block, y_block] + [piece] * 8,
            out_specs=[pair_block] * 3 + stay_specs,
            scratch_shapes=[pltpu.VMEM((2, 1024, 256), BF16)] * 2,
        ),
        out_shape=[pair_shape] * 3 + stay_shapes,
        compiler_params=pltpu.CompilerParams(vmem_limit_bytes=VMEM_LIMIT),
        cost_estimate=pl.CostEstimate(
            flops=3 * 2 * 2048 * 1024 * 512, bytes_accessed=24 << 20, transcendentals=0
        ),
        name="right_product",
    )(where, yh, yl, *pieces)


def fill_kernel(out_rows, choose, count, where, *refs):
    sources = refs[:count]
    out_ref, held, packed, in_sem, out_sem = refs[-5:]
    chosen = choose(where, sources)
    for k in range(2):
        for j in range(4):
            for condition, source in chosen[k][j]:

                @pl.when(condition)
                def _(source=source, k=k, j=j):
                    pltpu.make_async_copy(source, held.at[k, j], in_sem.at[k, j]).start()

    leaving = []
    for k in range(2):
        for j in range(4):
            pltpu.make_async_copy(chosen[k][j][0][1], held.at[k, j], in_sem.at[k, j]).wait()
            packed[k, :, j, :] = held[k, j]
        copy = pltpu.make_async_copy(packed.at[k], out_ref.at[out_rows[k]], out_sem.at[k])
        copy.start()
        leaving.append(copy)
    for copy in leaving:
        copy.wait()


def fill_rows(out_rows, choose, where, sources, previous):
    extra = [] if previous is None else [previous]
    count = len(sources)
    anywhere = pl.BlockSpec(memory_space=pl.ANY)

    def kernel(where, *refs):
        fill_kernel(out_rows, choose, count, where, *refs)

    return pl.pallas_call(
        kernel,
        grid_spec=pltpu.PrefetchScalarGridSpec(
            num_scalar_prefetch=1,
            grid=(1,),
            in_specs=[anywhere] * (count + len(extra)),
            out_specs=anywhere,
            scratch_shapes=[
                pltpu.VMEM((2, 4, 512, 256), F32),
                pltpu.VMEM((2, 512, 4, 256), F32),
                pltpu.SemaphoreType.DMA((2, 4)),
                pltpu.SemaphoreType.DMA((2,)),
            ],
        ),
        out_shape=jax.ShapeDtypeStruct((4, 512, 4, 256), F32),
        input_output_aliases={1 + count: 0} if extra else {},
        compiler_params=pltpu.CompilerParams(vmem_limit_bytes=VMEM_LIMIT),
        cost_estimate=pl.CostEstimate(flops=0, bytes_accessed=8 << 20, transcendentals=0),
        name="fill_rows",
    )(where, *sources, *extra)


def ring(piece):
    def across(r, c, l):
        return r ^ 4, c, l

    def above(r, c, l):
        return (r & 4) | ((r + 1) & 3), c, l

    def below(r, c, l):
        return (r & 4) | ((r + 3) & 3), c, l

    up = send(piece, above)
    down = send(piece, below)
    pair = send(piece, across)
    pair_up = send(pair, above)
    pair_down = send(pair, below)
    far = send(up, above)
    pair_far = send(pair_down, below)
    return [piece, pair, up, pair_up, down, pair_down, far, pair_far]


def step_up(axis):
    def place(r, c, l):
        to = [r, c, l]
        to[axis] += 1
        return to if to[axis] < 8 else None

    return place


def step_down(axis):
    def place(r, c, l):
        to = [r, c, l]
        to[axis] -= 1
        return to if to[axis] >= 0 else None

    return place


def shards(matrix, transforms):
    row_pos = lax.axis_index("row")
    col_pos = lax.axis_index("col")
    layer_pos = lax.axis_index("layer")
    where = jnp.stack([row_pos, col_pos, layer_pos]).astype(jnp.int32)
    mine = transforms[0]

    parts = mine.reshape(2, 64, 2, 2, 256)
    kept = lax.dynamic_index_in_dim(parts, layer_pos, 3, keepdims=False)
    crossing = lax.dynamic_index_in_dim(parts, 1 - layer_pos, 3, keepdims=False)

    def by_use(x):
        return jnp.stack([jnp.stack([x[0, :, 1], x[1, :, 0]]), jnp.stack([x[0, :, 0], x[1, :, 1]])])

    from_same = send(by_use(kept), lambda r, c, l: (c, r, l))
    from_cross = send(by_use(crossing), lambda r, c, l: (c, r, 1 - l))
    even = jnp.where(layer_pos == 0, from_same, from_cross)
    odd = jnp.where(layer_pos == 0, from_cross, from_same)
    piece = jnp.stack([even, odd], axis=2)
    pieces = ring(piece)

    panels = [lax.all_gather(mine[p], ("col", "layer"), axis=0, tiled=True) for p in range(2)]

    own = matrix.transpose(2, 0, 1, 3).reshape(4, 2048, 256)
    other = lax.ppermute(own, "layer", [(0, 1), (1, 0)])

    halves = left_product(0, panels[0], own, other, None)
    yh, yl = left_product(1, panels[1], own, other, halves)

    up, down, first, stay_down, stay_up = right_product(0, where, yh, yl, pieces, True)
    got_up = send(up, step_up(0))
    got_down = send(down, step_down(0))
    stay_got_up = send(stay_up, step_up(1))
    stay_got_down = send(stay_down, step_down(1))

    s_up, s_down, s_first, s_stay = right_product(1, where, yh, yl, pieces, False)
    s_got_up = send(s_up, step_up(0))
    s_got_down = send(s_down, step_down(0))

    top = jnp.where(row_pos == 0, first, got_up)
    bottom = jnp.where(row_pos == 7, up, got_down)
    moved_down = jnp.stack([top[0], bottom[0]])
    moved_up = jnp.stack([top[1], bottom[1]])
    moved_got_up = send(moved_up, step_up(1))
    moved_got_down = send(moved_down, step_down(1))

    def choose_stay(w, refs):
        stay, went_up, went_down, came_up, came_down = refs
        c = w[1]
        return [
            [
                [(c > 0, came_up.at[k]), (c == 0, stay.at[k, 0])],
                [(c >= 0, stay.at[k, 1])],
                [(c > 0, stay.at[k, 0]), (c == 0, went_down.at[k])],
                [(c < 7, came_down.at[k]), (c == 7, went_up.at[k])],
            ]
            for k in range(2)
        ]

    out = fill_rows(
        (1, 2), choose_stay, where, [s_stay, stay_up, stay_down, stay_got_up, stay_got_down], None
    )

    def choose_moved(w, refs):
        first_row, up_row, from_up, from_down, went_up, went_down, came_up, came_down = refs
        r, c = w[0], w[1]

        def stays(k, q, condition):
            if k == 0:
                return [
                    (condition & (r > 0), from_up.at[q]),
                    (condition & (r == 0), first_row.at[q]),
                ]
            return [
                (condition & (r < 7), from_down.at[q]),
                (condition & (r == 7), up_row.at[q]),
            ]

        return [
            [
                [(c > 0, came_up.at[k])] + stays(k, 0, c == 0),
                stays(k, 1, c >= 0),
                [(c == 0, went_down.at[k])] + stays(k, 0, c > 0),
                [(c < 7, came_down.at[k]), (c == 7, went_up.at[k])],
            ]
            for k in range(2)
        ]

    return fill_rows(
        (0, 3),
        choose_moved,
        where,
        [s_first, s_up, s_got_up, s_got_down, moved_up, moved_down, moved_got_up, moved_got_down],
        out,
    )


def solution(mesh):
    return jax.shard_map(
        shards,
        mesh=mesh,
        in_specs=(P("row", None, "col", "layer"), P(None, "row", ("col", "layer"), None)),
        out_specs=P("row", None, "col", "layer"),
        check_vma=False,
    )
```

time: 414 us -> 269 us (0.65)
  waiting for transfers between devices: 208 us -> 86 us
  Pallas kernels: 0 us -> 79 us
  matrix products: 62.6 us -> 0 us
  starting transfers between devices: 17.4 us -> 71.2 us
  local copies, waits for them, and re-layouts: 54.7 us -> 14.6 us
  other arithmetic: 34.9 us -> 3.68 us
  blocking collectives: 19 us -> 0 us
    pallas_call x0 -> x6, Pallas kernels: none -> 79 us  [the longest x2 38.7 us: left_product(): pl.pallas_call(left_kernel, grid=(4,), in_specs=[pl.BlockSpec((1024, 1024...]
    psum x1 -> x0, waiting for transfers between devices: 67.2 us -> none  [broadcast(): return lax.psum(jnp.where(mine, x, jnp.zeros_like(x)), axis)]
    dot_general x2 -> x0, matrix products: 62.6 us -> none  [the longest x1 31.5 us: shards(): jnp.einsum('pka,pkc->pac', left_panel, grouped, precision=exact_mode, pre...]
    ppermute x4 -> x18, starting transfers between devices: 17.4 us -> 71.2 us  [the longest x17 71.2 us: send(): return lax.ppermute(x, AXES, route(place))]
    all_gather x1 -> x2, waiting for transfers between devices: 56.1 us -> 4.91 us  [shards(): lax.all_gather(mine[p], ('col', 'layer'), axis=0, tiled=True)]
    all_to_all x1 -> x0, blocking collectives: 19 us -> none  [sum_at_owner(): blocks = lax.all_to_all(cut_along(x, dim, count), axis, 0, 0, tiled=True)]
    another operation x2 -> x3, local copies, waits for them, and re-layouts: 15.1 us -> 0.48 us  [the longest x1 0.44 us: shards(): parts = mine.reshape(2, 64, 2, 2, 256)]
    another operation x4 -> x11, other arithmetic: 13.2 us -> 0.94 us  [the longest x1 0.64 us: shards(): where = jnp.stack([row_pos, col_pos, layer_pos]).astype(jnp.int32)]
  transfers between devices with their start and end apart: 6 -> 20, of which waited for: 6 -> 7; matrix products, arithmetic and copies ran while one was open for 12% -> 5% of each run, Pallas kernels for 0% -> 22%
where the time goes in v1:
time: 269 us; the launch traced here: 268 us
  waiting for transfers between devices  86 us (32%)
  Pallas kernels  79 us (29%)
  starting transfers between devices  71.2 us (26%)
  local copies, waits for them, and re-layouts  14.6 us (5%)
  between operations  13.9 us (5%)
  other arithmetic  3.68 us (1%)
    ppermute x17, waiting for transfers between devices, send(): return lax.ppermute(x, AXES, route(place))  81.1 us
    ppermute x17, starting transfers between devices, send(): return lax.ppermute(x, AXES, route(place))  71.2 us
    pallas_call x2, Pallas kernels, left_product(): pl.pallas_call(left_kernel, grid=(4,), in_specs=[pl.BlockSpec((1024, 1024...  38.7 us
    pallas_call x2, Pallas kernels, right_product(): pl.pallas_call(right_kernel, grid_spec=pltpu.PrefetchScalarGridSpec(num_s...  31.4 us
    pallas_call x2, Pallas kernels, fill_rows(): pl.pallas_call(kernel, grid_spec=pltpu.PrefetchScalarGridSpec(num_scalar_...  8.88 us
    transpose x1, local copies, waits for them, and re-layouts, shards(): own = matrix.transpose(2, 0, 1, 3).reshape(4, 2048, 256)  8.45 us
  transfers between devices with their start and end apart: 20, of which 7 were waited for; matrix products, arithmetic and copies ran while one was open for 5% of the time, Pallas kernels for 22%

profile of v1, /device:TPU:6, one launch (start us, length us, event | category | flops | bytes accessed | tf_op | source)
XLA Modules:
  0.0 268.4 jit_solution(12005103836570528810)
XLA Ops:
  8.5 8.5 %copy.6 = f32[4,4,512,256]{3,2,1,0:T(8,128)} copy(f32[4,4,512,256]{3,0,2,1:T(4,128)} %bitcast.43) | data formatting | bytes 16777216 | tf_op jit(solution)/shard_map/transpose | solution.py:289
  19.4 11.4 %collective-permute-done.2 = f32[2,2,64,256]{3,2,1,0:T(8,128)S(1)} collective-permute-done((f32[2,2,64,256]{3,2,1,0:T(8,128)S(1)}, f32[2,2,64,256]{3,2,1,0:T(8,128)S(1)}, u32[]{:S(2)}, u32[]{:S(2)}) %collective-permute-start.2) | collective-permute-done | bytes 262176 | tf_op jit(solution)/shard_map/ppermute | solution.py:26
  31.0 4.5 %collective-permute-start.3 = (f32[2,2,2,64,256]{4,3,2,1,0:T(8,128)S(1)}, f32[2,2,2,64,256]{4,3,2,1,0:T(8,128)S(1)}, u32[]{:S(2)}, u32[]{:S(2)}) collective-permute-start(f32[2,2,2,64,256]{4,3,2,1,0:T(8,128)S(1)} %pad_maximum_fusion.2.refs_0_), channel_id=1, source_target_pairs={{0,64},{1,65},{2,66},{3,67},{4,68},{5,69},{6,70},{7,71},{8,72},{9,... | collective-permute-start | bytes 1572872 | tf_op jit(solution)/shard_map/ppermute | solution.py:26
  35.5 13.0 %collective-permute-start.4 = (f32[2,2,2,64,256]{4,3,2,1,0:T(8,128)S(1)}, f32[2,2,2,64,256]{4,3,2,1,0:T(8,128)S(1)}, u32[]{:S(2)}, u32[]{:S(2)}) collective-permute-start(f32[2,2,2,64,256]{4,3,2,1,0:T(8,128)S(1)} %pad_maximum_fusion.2.refs_0_), channel_id=1, source_target_pairs={{0,16},{1,17},{2,18},{3,19},{4,20},{5,21},{6,22},{7,23},{8,24},{9,... | collective-permute-start | bytes 1572872 | tf_op jit(solution)/shard_map/ppermute | solution.py:26
  48.5 11.5 %collective-permute-done.3.refs_1_ = f32[2,2,2,64,256]{4,3,2,1,0:T(8,128)S(1)} collective-permute-done((f32[2,2,2,64,256]{4,3,2,1,0:T(8,128)S(1)}, f32[2,2,2,64,256]{4,3,2,1,0:T(8,128)S(1)}, u32[]{:S(2)}, u32[]{:S(2)}) %collective-permute-start.3) | collective-permute-done | bytes 524320 | tf_op jit(solution)/shard_map/ppermute | solution.py:26
  60.1 9.3 %collective-permute-start.7 = (f32[2,2,2,64,256]{4,3,2,1,0:T(8,128)S(1)}, f32[2,2,2,64,256]{4,3,2,1,0:T(8,128)S(1)}, u32[]{:S(2)}, u32[]{:S(2)}) collective-permute-start(f32[2,2,2,64,256]{4,3,2,1,0:T(8,128)S(1)} %collective-permute-done.3.refs_1_), channel_id=1, source_target_pairs={{0,48},{1,49},{2,50},{3,51},{4,52},{5,53},{6,54},{7,55},{8,56},{9,... | collective-permute-start | bytes 1572872 | tf_op jit(solution)/shard_map/ppermute | solution.py:26
  70.0 8.3 %collective-permute-start.6 = (f32[2,2,2,64,256]{4,3,2,1,0:T(8,128)S(1)}, f32[2,2,2,64,256]{4,3,2,1,0:T(8,128)S(1)}, u32[]{:S(2)}, u32[]{:S(2)}) collective-permute-start(f32[2,2,2,64,256]{4,3,2,1,0:T(8,128)S(1)} %pad_maximum_fusion.2.refs_0_), channel_id=1, source_target_pairs={{0,48},{1,49},{2,50},{3,51},{4,52},{5,53},{6,54},{7,55},{8,56},{9,... | collective-permute-start | bytes 1572872 | tf_op jit(solution)/shard_map/ppermute | solution.py:26
  78.4 6.3 %collective-permute-done.7.refs_5_ = f32[2,2,2,64,256]{4,3,2,1,0:T(8,128)S(1)} collective-permute-done((f32[2,2,2,64,256]{4,3,2,1,0:T(8,128)S(1)}, f32[2,2,2,64,256]{4,3,2,1,0:T(8,128)S(1)}, u32[]{:S(2)}, u32[]{:S(2)}) %collective-permute-start.7) | collective-permute-done | bytes 524320 | tf_op jit(solution)/shard_map/ppermute | solution.py:26
  84.7 5.4 %collective-permute-start.9 = (f32[2,2,2,64,256]{4,3,2,1,0:T(8,128)S(1)}, f32[2,2,2,64,256]{4,3,2,1,0:T(8,128)}, u32[]{:S(2)}, u32[]{:S(2)}) collective-permute-start(f32[2,2,2,64,256]{4,3,2,1,0:T(8,128)S(1)} %collective-permute-done.7.refs_5_), channel_id=1, source_target_pairs={{0,48},{1,49},{2,50},{3,51},{4,52},{5,53},{6,54},{7,55},{8,56},{9,... | collective-permute-start | bytes 1572872 | tf_op jit(solution)/shard_map/ppermute | solution.py:26
  90.0 19.4 %left_product.2 = (bf16[2048,2048]{1,0:T(8,128)(2,1)}, bf16[2048,2048]{1,0:T(8,128)(2,1)}) custom-call(f32[1024,1024]{1,0:T(8,128)} %bitcast.44, f32[4,2048,256]{2,1,0:T(8,128)} %bitcast.5.own_ref, f32[4,2048,256]{2,1,0:T(8,128)} %collective-permute-done.other_ref), custom_call_target="tpu_custom_call" | custom-call | flops 12884901888 | bytes 20971520 | tf_op jit(solution)/shard_map/left_product/pallas_call | solution.py:65
  109.5 4.9 %all-gather.5.cloned.1.call-done = f32[1,1,1024,1024]{3,2,1,0:T(8,128)} async-done(((f32[1,1,64,1024]{3,2,1,0:T(8,128)}), f32[1,1,1024,1024]{3,2,1,0:T(8,128)}) %all-gather.5.cloned.1.call-update) | async-done | bytes 4194320 | tf_op jit(solution)/shard_map/all_gather | solution.py:287
  114.4 19.3 %left_product.3 = (bf16[2048,2048]{1,0:T(8,128)(2,1)}, bf16[2048,2048]{1,0:T(8,128)(2,1)}) custom-call(f32[1024,1024]{1,0:T(8,128)} %bitcast.45, f32[4,2048,256]{2,1,0:T(8,128)} %bitcast.5.own_ref, f32[4,2048,256]{2,1,0:T(8,128)} %collective-permute-done.other_ref, ...), custom_call_target="tpu_custom_call", output_to_operand_aliasing={{0}: (3, {}), {1}: (4, {})} | custom-call | flops 12884901888 | bytes 20971520 | tf_op jit(solution)/shard_map/left_product/pallas_call | solution.py:65
  134.7 15.7 %right_product.3 = (f32[2,512,256]{2,1,0:T(8,128)}, f32[2,512,256]{2,1,0:T(8,128)}, f32[2,512,256]{2,1,0:T(8,128)}, f32[2,512,256]{2,1,0:T(8,128)}, f32[2,512,256]{2,1,0:T(8,128)}) custom-call(s32[3]{0:T(128)} %pad_add_fusion.where, bf16[2048,2048]{1,0:T(8,128)(2,1)} %get-tuple-element.20.yh_ref, bf16[2048,2048]{1,0:T(8,128)(2,1)} %get-tuple-element.21.yl_ref, ...), custom_call_target="tpu_custom_call" | custom-call | flops 6442450944 | bytes 25165824 | tf_op jit(solution)/shard_map/right_product/pallas_call | solution.py:156
  150.5 5.7 %collective-permute-start.13 = (f32[2,512,256]{2,1,0:T(8,128)}, f32[2,512,256]{2,1,0:T(8,128)}, u32[]{:S(2)}, u32[]{:S(2)}) collective-permute-start(f32[2,512,256]{2,1,0:T(8,128)} %get-tuple-element.27), channel_id=1, source_target_pairs={{16,0},{17,1},{18,2},{19,3},{20,4},{21,5},{22,6},{23,7},{24,8},{25... | collective-permute-start | bytes 3145736 | tf_op jit(solution)/shard_map/ppermute | solution.py:26
  156.3 2.2 collective-permute-start.12
  158.4 15.7 %right_product.2 = (f32[2,512,256]{2,1,0:T(8,128)}, f32[2,512,256]{2,1,0:T(8,128)}, f32[2,512,256]{2,1,0:T(8,128)}, f32[2,2,512,256]{3,2,1,0:T(8,128)}) custom-call(s32[3]{0:T(128)} %pad_add_fusion.where, bf16[2048,2048]{1,0:T(8,128)(2,1)} %get-tuple-element.20.yh_ref, bf16[2048,2048]{1,0:T(8,128)(2,1)} %get-tuple-element.21.yl_ref, ...), custom_call_target="tpu_custom_call" | custom-call | flops 6442450944 | bytes 25165824 | tf_op jit(solution)/shard_map/right_product/pallas_call | solution.py:156
  176.1 7.5 %collective-permute-start.11 = (f32[2,512,256]{2,1,0:T(8,128)}, f32[2,512,256]{2,1,0:T(8,128)S(1)}, u32[]{:S(2)}, u32[]{:S(2)}) collective-permute-start(f32[2,512,256]{2,1,0:T(8,128)} %get-tuple-element.24), channel_id=1, source_target_pairs={{16,0},{17,1},{18,2},{19,3},{20,4},{21,5},{22,6},{23,7},{24,8},{25... | collective-permute-start | bytes 3145736 | tf_op jit(solution)/shard_map/ppermute | solution.py:26
  183.6 2.8 %collective-permute-start.16 = (f32[2,512,256]{2,1,0:T(8,128)S(1)}, f32[2,512,256]{2,1,0:T(8,128)S(1)}, u32[]{:S(2)}, u32[]{:S(2)}) collective-permute-start(f32[2,512,256]{2,1,0:T(8,128)S(1)} %copy-done.4), channel_id=1, source_target_pairs={{0,2},{1,3},{2,4},{3,5},{4,6},{5,7},{6,8},{7,9},{8,10},{9,11},{10,... | collective-permute-start | bytes 3145736 | tf_op jit(solution)/shard_map/ppermute | solution.py:26
  186.4 5.2 %collective-permute-start.17 = (f32[2,512,256]{2,1,0:T(8,128)S(1)}, f32[2,512,256]{2,1,0:T(8,128)S(1)}, u32[]{:S(2)}, u32[]{:S(2)}) collective-permute-start(f32[2,512,256]{2,1,0:T(8,128)S(1)} %copy-done.3), channel_id=1, source_target_pairs={{2,0},{3,1},{4,2},{5,3},{6,4},{7,5},{8,6},{9,7},{10,8},{11,9},{12,... | collective-permute-start | bytes 3145736 | tf_op jit(solution)/shard_map/ppermute | solution.py:26
  196.7 35.1 %collective-permute-done.16.refs_3_ = f32[2,512,256]{2,1,0:T(8,128)S(1)} collective-permute-done((f32[2,512,256]{2,1,0:T(8,128)S(1)}, f32[2,512,256]{2,1,0:T(8,128)S(1)}, u32[]{:S(2)}, u32[]{:S(2)}) %collective-permute-start.16) | collective-permute-done | bytes 1048608 | tf_op jit(solution)/shard_map/ppermute | solution.py:26
  234.9 4.4 %fill_rows.2.refs_8_ = f32[4,512,4,256]{3,2,1,0:T(4,128)} custom-call(s32[3]{0:T(128)} %pad_add_fusion.where, f32[2,2,512,256]{3,2,1,0:T(8,128)} %get-tuple-element.28.refs_0_, f32[2,512,256]{2,1,0:T(8,128)} %get-tuple-element.29.refs_1_, f32[2,512,256]{2,1,0:T(8,128)} %get-tuple-element.30.refs_2_, f32[2,512,256]{2,1,0:T(8,128)} %copy-done.7, ...), custom_call_target="tpu_custom_call" | custom-call | bytes 8388608 | tf_op jit(solution)/shard_map/fill_rows/pallas_call | solution.py:206
  239.4 13.5 %collective-permute-done.14.refs_6_ = f32[2,512,256]{2,1,0:T(8,128)} collective-permute-done((f32[2,512,256]{2,1,0:T(8,128)S(1)}, f32[2,512,256]{2,1,0:T(8,128)}, u32[]{:S(2)}, u32[]{:S(2)}) %collective-permute-start.14) | collective-permute-done | bytes 1048608 | tf_op jit(solution)/shard_map/ppermute | solution.py:26
  253.0 3.1 %collective-permute-done.15.refs_7_ = f32[2,512,256]{2,1,0:T(8,128)S(1)} collective-permute-done((f32[2,512,256]{2,1,0:T(8,128)S(1)}, f32[2,512,256]{2,1,0:T(8,128)S(1)}, u32[]{:S(2)}, u32[]{:S(2)}) %collective-permute-start.15) | collective-permute-done | bytes 1048608 | tf_op jit(solution)/shard_map/ppermute | solution.py:26
  257.1 4.4 %fill_rows.3 = f32[4,512,4,256]{3,2,1,0:T(4,128)} custom-call(s32[3]{0:T(128)} %pad_add_fusion.where, f32[2,512,256]{2,1,0:T(8,128)} %get-tuple-element.22.refs_0_, f32[2,512,256]{2,1,0:T(8,128)} %get-tuple-element.23.refs_1_, f32[2,512,256]{2,1,0:T(8,128)} %copy-done.5, f32[2,512,256]{2,1,0:T(8,128)} %copy-done.6, ...), custom_call_target="tpu_custom_call", output_to_operand_aliasing={{}: (9, {})} | custom-call | bytes 8388608 | tf_op jit(solution)/shard_map/fill_rows/pallas_call | solution.py:206
  (82 shorter events, 17.2 us)
Async XLA Ops:
  6.5 83.5 %all-gather.7.cloned.1.call-start = ((), (), s32[]{:S(2)}) async-start(), calls=%async_computation.1 | async-start | bytes 4456448 | tf_op jit(solution)/shard_map/all_gather | solution.py:287
  8.5 105.9 %all-gather.5.cloned.1.call-start = ((), (), s32[]{:S(2)}) async-start(), calls=%async_computation | async-start | bytes 4456448 | tf_op jit(solution)/shard_map/all_gather | solution.py:287
  17.0 73.0 %collective-permute-start = (f32[4,2048,256]{2,1,0:T(8,128)}, f32[4,2048,256]{2,1,0:T(8,128)}, u32[]{:S(2)}, u32[]{:S(2)}) collective-permute-start(f32[4,2048,256]{2,1,0:T(8,128)} %bitcast.5.own_ref), channel_id=1, source_target_pairs={{0,1},{1,0},{2,3},{3,2},{4,5},{5,4},{6,7},{7,6},{8,9},{9,8},{10,11... | collective-permute-start | bytes 25165832 | tf_op jit(solution)/shard_map/ppermute | solution.py:290
  18.1 1.4 collective-permute-start.1
  18.9 12.0 %collective-permute-start.2 = (f32[2,2,64,256]{3,2,1,0:T(8,128)S(1)}, f32[2,2,64,256]{3,2,1,0:T(8,128)S(1)}, u32[]{:S(2)}, u32[]{:S(2)}) collective-permute-start(f32[2,2,64,256]{3,2,1,0:T(8,128)S(1)} %pad_maximum_fusion.4), channel_id=1, source_target_pairs={{0,1},{1,0},{2,17},{3,16},{4,33},{5,32},{6,49},{7,48},{8,65},{9,64... | collective-permute-start | bytes 786440 | tf_op jit(solution)/shard_map/ppermute | solution.py:26
  31.0 78.5 %copy-start.12 = (f32[2,2,2,64,256]{4,3,2,1,0:T(8,128)}, f32[2,2,2,64,256]{4,3,2,1,0:T(8,128)S(1)}, u32[]{:S(2)}) copy-start(f32[2,2,2,64,256]{4,3,2,1,0:T(8,128)S(1)} %pad_maximum_fusion.2.refs_0_) | copy-start | bytes 1572868
  31.0 29.1 %collective-permute-start.3 = (f32[2,2,2,64,256]{4,3,2,1,0:T(8,128)S(1)}, f32[2,2,2,64,256]{4,3,2,1,0:T(8,128)S(1)}, u32[]{:S(2)}, u32[]{:S(2)}) collective-permute-start(f32[2,2,2,64,256]{4,3,2,1,0:T(8,128)S(1)} %pad_maximum_fusion.2.refs_0_), channel_id=1, source_target_pairs={{0,64},{1,65},{2,66},{3,67},{4,68},{5,69},{6,70},{7,71},{8,72},{9,... | collective-permute-start | bytes 1572872 | tf_op jit(solution)/shard_map/ppermute | solution.py:26
  35.5 42.8 %collective-permute-start.4 = (f32[2,2,2,64,256]{4,3,2,1,0:T(8,128)S(1)}, f32[2,2,2,64,256]{4,3,2,1,0:T(8,128)S(1)}, u32[]{:S(2)}, u32[]{:S(2)}) collective-permute-start(f32[2,2,2,64,256]{4,3,2,1,0:T(8,128)S(1)} %pad_maximum_fusion.2.refs_0_), channel_id=1, source_target_pairs={{0,16},{1,17},{2,18},{3,19},{4,20},{5,21},{6,22},{7,23},{8,24},{9,... | collective-permute-start | bytes 1572872 | tf_op jit(solution)/shard_map/ppermute | solution.py:26
  60.1 49.4 %copy-start.13 = (f32[2,2,2,64,256]{4,3,2,1,0:T(8,128)}, f32[2,2,2,64,256]{4,3,2,1,0:T(8,128)S(1)}, u32[]{:S(2)}) copy-start(f32[2,2,2,64,256]{4,3,2,1,0:T(8,128)S(1)} %collective-permute-done.3.refs_1_) | copy-start | bytes 1572868
  60.1 24.6 %collective-permute-start.7 = (f32[2,2,2,64,256]{4,3,2,1,0:T(8,128)S(1)}, f32[2,2,2,64,256]{4,3,2,1,0:T(8,128)S(1)}, u32[]{:S(2)}, u32[]{:S(2)}) collective-permute-start(f32[2,2,2,64,256]{4,3,2,1,0:T(8,128)S(1)} %collective-permute-done.3.refs_1_), channel_id=1, source_target_pairs={{0,48},{1,49},{2,50},{3,51},{4,52},{5,53},{6,54},{7,55},{8,56},{9,... | collective-permute-start | bytes 1572872 | tf_op jit(solution)/shard_map/ppermute | solution.py:26
  70.0 63.7 %collective-permute-start.6 = (f32[2,2,2,64,256]{4,3,2,1,0:T(8,128)S(1)}, f32[2,2,2,64,256]{4,3,2,1,0:T(8,128)S(1)}, u32[]{:S(2)}, u32[]{:S(2)}) collective-permute-start(f32[2,2,2,64,256]{4,3,2,1,0:T(8,128)S(1)} %pad_maximum_fusion.2.refs_0_), channel_id=1, source_target_pairs={{0,48},{1,49},{2,50},{3,51},{4,52},{5,53},{6,54},{7,55},{8,56},{9,... | collective-permute-start | bytes 1572872 | tf_op jit(solution)/shard_map/ppermute | solution.py:26
  78.3 55.4 %collective-permute-start.5 = (f32[2,2,2,64,256]{4,3,2,1,0:T(8,128)S(1)}, f32[2,2,2,64,256]{4,3,2,1,0:T(8,128)S(1)}, u32[]{:S(2)}, u32[]{:S(2)}) collective-permute-start(f32[2,2,2,64,256]{4,3,2,1,0:T(8,128)S(1)} %collective-permute-done.3.refs_1_), channel_id=1, source_target_pairs={{0,16},{1,17},{2,18},{3,19},{4,20},{5,21},{6,22},{7,23},{8,24},{9,... | collective-permute-start | bytes 1572872 | tf_op jit(solution)/shard_map/ppermute | solution.py:26
  78.3 55.4 %collective-permute-start.8 = (f32[2,2,2,64,256]{4,3,2,1,0:T(8,128)S(1)}, f32[2,2,2,64,256]{4,3,2,1,0:T(8,128)}, u32[]{:S(2)}, u32[]{:S(2)}) collective-permute-start(f32[2,2,2,64,256]{4,3,2,1,0:T(8,128)S(1)} %collective-permute-done.4.refs_2_), channel_id=1, source_target_pairs={{0,16},{1,17},{2,18},{3,19},{4,20},{5,21},{6,22},{7,23},{8,24},{9,... | collective-permute-start | bytes 1572872 | tf_op jit(solution)/shard_map/ppermute | solution.py:26
  84.7 49.1 %collective-permute-start.9 = (f32[2,2,2,64,256]{4,3,2,1,0:T(8,128)S(1)}, f32[2,2,2,64,256]{4,3,2,1,0:T(8,128)}, u32[]{:S(2)}, u32[]{:S(2)}) collective-permute-start(f32[2,2,2,64,256]{4,3,2,1,0:T(8,128)S(1)} %collective-permute-done.7.refs_5_), channel_id=1, source_target_pairs={{0,48},{1,49},{2,50},{3,51},{4,52},{5,53},{6,54},{7,55},{8,56},{9,... | collective-permute-start | bytes 1572872 | tf_op jit(solution)/shard_map/ppermute | solution.py:26
  150.5 35.9 %collective-permute-start.13 = (f32[2,512,256]{2,1,0:T(8,128)}, f32[2,512,256]{2,1,0:T(8,128)}, u32[]{:S(2)}, u32[]{:S(2)}) collective-permute-start(f32[2,512,256]{2,1,0:T(8,128)} %get-tuple-element.27), channel_id=1, source_target_pairs={{16,0},{17,1},{18,2},{19,3},{20,4},{21,5},{22,6},{23,7},{24,8},{25... | collective-permute-start | bytes 3145736 | tf_op jit(solution)/shard_map/ppermute | solution.py:26
  156.3 36.8 %collective-permute-start.12 = (f32[2,512,256]{2,1,0:T(8,128)}, f32[2,512,256]{2,1,0:T(8,128)}, u32[]{:S(2)}, u32[]{:S(2)}) collective-permute-start(f32[2,512,256]{2,1,0:T(8,128)} %get-tuple-element.26), channel_id=1, source_target_pairs={{0,16},{1,17},{2,18},{3,19},{4,20},{5,21},{6,22},{7,23},{8,24},{9,... | collective-permute-start | bytes 3145736 | tf_op jit(solution)/shard_map/ppermute | solution.py:26
  174.2 65.3 %collective-permute-start.10 = (f32[2,512,256]{2,1,0:T(8,128)}, f32[2,512,256]{2,1,0:T(8,128)S(1)}, u32[]{:S(2)}, u32[]{:S(2)}) collective-permute-start(f32[2,512,256]{2,1,0:T(8,128)} %get-tuple-element.23.refs_1_), channel_id=1, source_target_pairs={{0,16},{1,17},{2,18},{3,19},{4,20},{5,21},{6,22},{7,23},{8,24},{9,... | collective-permute-start | bytes 3145736 | tf_op jit(solution)/shard_map/ppermute | solution.py:26
  176.1 63.4 %collective-permute-start.11 = (f32[2,512,256]{2,1,0:T(8,128)}, f32[2,512,256]{2,1,0:T(8,128)S(1)}, u32[]{:S(2)}, u32[]{:S(2)}) collective-permute-start(f32[2,512,256]{2,1,0:T(8,128)} %get-tuple-element.24), channel_id=1, source_target_pairs={{16,0},{17,1},{18,2},{19,3},{20,4},{21,5},{22,6},{23,7},{24,8},{25... | collective-permute-start | bytes 3145736 | tf_op jit(solution)/shard_map/ppermute | solution.py:26
  183.6 48.1 %collective-permute-start.16 = (f32[2,512,256]{2,1,0:T(8,128)S(1)}, f32[2,512,256]{2,1,0:T(8,128)S(1)}, u32[]{:S(2)}, u32[]{:S(2)}) collective-permute-start(f32[2,512,256]{2,1,0:T(8,128)S(1)} %copy-done.4), channel_id=1, source_target_pairs={{0,2},{1,3},{2,4},{3,5},{4,6},{5,7},{6,8},{7,9},{8,10},{9,11},{10,... | collective-permute-start | bytes 3145736 | tf_op jit(solution)/shard_map/ppermute | solution.py:26
  186.4 47.5 %collective-permute-start.17 = (f32[2,512,256]{2,1,0:T(8,128)S(1)}, f32[2,512,256]{2,1,0:T(8,128)S(1)}, u32[]{:S(2)}, u32[]{:S(2)}) collective-permute-start(f32[2,512,256]{2,1,0:T(8,128)S(1)} %copy-done.3), channel_id=1, source_target_pairs={{2,0},{3,1},{4,2},{5,3},{6,4},{7,5},{8,6},{9,7},{10,8},{11,9},{12,... | collective-permute-start | bytes 3145736 | tf_op jit(solution)/shard_map/ppermute | solution.py:26
  194.6 44.8 %copy-start = (f32[2,512,256]{2,1,0:T(8,128)}, f32[2,512,256]{2,1,0:T(8,128)S(1)}, u32[]{:S(2)}) copy-start(f32[2,512,256]{2,1,0:T(8,128)S(1)} %pad_maximum_fusion.refs_4_) | copy-start | bytes 3145732
  194.6 58.4 %collective-permute-start.14 = (f32[2,512,256]{2,1,0:T(8,128)S(1)}, f32[2,512,256]{2,1,0:T(8,128)}, u32[]{:S(2)}, u32[]{:S(2)}) collective-permute-start(f32[2,512,256]{2,1,0:T(8,128)S(1)} %pad_maximum_fusion.refs_4_), channel_id=1, source_target_pairs={{0,2},{1,3},{2,4},{3,5},{4,6},{5,7},{6,8},{7,9},{8,10},{9,11},{10,... | collective-permute-start | bytes 3145736 | tf_op jit(solution)/shard_map/ppermute | solution.py:26
  196.6 59.5 %copy-start.1 = (f32[2,512,256]{2,1,0:T(8,128)}, f32[2,512,256]{2,1,0:T(8,128)S(1)}, u32[]{:S(2)}) copy-start(f32[2,512,256]{2,1,0:T(8,128)S(1)} %pad_maximum_fusion.1.refs_5_) | copy-start | bytes 3145732
  231.8 24.4 %collective-permute-start.15 = (f32[2,512,256]{2,1,0:T(8,128)S(1)}, f32[2,512,256]{2,1,0:T(8,128)S(1)}, u32[]{:S(2)}, u32[]{:S(2)}) collective-permute-start(f32[2,512,256]{2,1,0:T(8,128)S(1)} %pad_maximum_fusion.1.refs_5_), channel_id=1, source_target_pairs={{2,0},{3,1},{4,2},{5,3},{6,4},{7,5},{8,6},{9,7},{10,8},{11,9},{12,... | collective-permute-start | bytes 3145736 | tf_op jit(solution)/shard_map/ppermute | solution.py:26
  (14 other events, 234.9 us)
Sparse Core Ops, SparseCore 0:
  9.1 52.7 all-gather.6
  63.5 50.8 all-gather.4

commit v2 on v0

v2 whole, which is shorter than its diff:
```python
import jax
import jax.numpy as jnp
from jax import lax
from jax.experimental import pallas as pl
from jax.experimental.pallas import tpu as pltpu
from jax.sharding import PartitionSpec as P

F32 = jnp.float32
BF16 = jnp.bfloat16
AXES = ("row", "col", "layer")
VMEM_LIMIT = 58 * 1024 * 1024
EARLY = (0, 1, 2, 4)
LATE = (3, 5, 6, 7)
ANYWHERE = pl.BlockSpec(memory_space=pl.ANY)


def route(place):
    pairs = []
    for r in range(8):
        for c in range(8):
            for l in range(2):
                to = place(r, c, l)
                if to is not None:
                    pairs.append(((r * 8 + c) * 2 + l, (to[0] * 8 + to[1]) * 2 + to[2]))
    return pairs


def send(x, place):
    return lax.ppermute(x, AXES, route(place))


def in_chip(x):
    return lax.ppermute(x, "layer", [(0, 1), (1, 0)])


def split(x):
    high = x.astype(BF16)
    return high, (x - high.astype(F32)).astype(BF16)


def product(ah, al, bh, bl):
    def dot(a, b):
        return jnp.dot(a, b, preferred_element_type=F32)

    return dot(ah, bh) + (dot(ah, bl) + dot(al, bh))


def holders(i):
    up = (i & 4) | ((i + 3) & 3)
    down = (i & 4) | ((i + 1) & 3)
    far = (i & 4) | ((i + 2) & 3)
    return [i, i ^ 4, up, up ^ 4, down, down ^ 4, far, far ^ 4]


def turned(ref, index, pair, cols):
    rows = jnp.concatenate([ref[index, 0, pair, :, cols], ref[index, 1, pair, :, cols]], axis=0)
    return split(rows.T)


def halves_of_matrix(own_refs, other_refs, mh, ml):
    for n in range(4):
        for m in range(2):
            for k, block in enumerate((own_refs[n][m], other_refs[2 * n + m][...])):
                high, low = split(block)
                lanes = slice(m * 512 + k * 256, m * 512 + k * 256 + 256)
                mh[n * 128 : n * 128 + 128, lanes] = high
                ml[n * 128 : n * 128 + 128, lanes] = low


def early_kernel(where, *refs):
    ours, theirs = refs[:4], refs[4:8]
    own_refs, other_refs = refs[8:12], refs[12:20]
    y_ref, held, jh, jl, mh, ml, sem = refs[20:]
    pair = pl.program_id(0)
    layer = where[2]

    @pl.when(pair == 0)
    def _():
        for i in range(4):

            @pl.when(layer == 0)
            def _(i=i):
                pltpu.make_async_copy(ours[i], held.at[i], sem.at[i]).start()

            @pl.when(layer == 1)
            def _(i=i):
                pltpu.make_async_copy(theirs[i], held.at[i], sem.at[i]).start()

    halves_of_matrix(own_refs, other_refs, mh, ml)

    @pl.when(pair == 0)
    def _():
        for i in range(4):
            pltpu.make_async_copy(ours[i], held.at[i], sem.at[i]).wait()

    for i in range(4):
        for half in range(4):
            high, low = turned(held, i, pair, pl.ds(half * 256, 256))
            jh[half * 256 : half * 256 + 256, i * 128 : i * 128 + 128] = high
            jl[half * 256 : half * 256 + 256, i * 128 : i * 128 + 128] = low
    for a in range(4):
        rows = pl.ds(a * 256, 256)
        y_ref[rows, :] = product(jh[rows, :], jl[rows, :], mh[...], ml[...])


def matrix_pieces(which, pair_of):
    def rows(i):
        return lambda step, w: pair_of(step, w) * 8 + holders(w[1])[i]

    own = [pl.BlockSpec((2, 128, 256), lambda s, w, f=rows(i): (w[2], f(s, w), 0)) for i in which]
    other = [pl.BlockSpec((128, 256), lambda s, w, f=rows(i): (f(s, w), 0)) for i in which]
    return own + [spec for spec in other for m in range(2)]


def early_product(where, pieces, crossed, own, other):
    return pl.pallas_call(
        early_kernel,
        grid_spec=pltpu.PrefetchScalarGridSpec(
            num_scalar_prefetch=1,
            grid=(2,),
            in_specs=[ANYWHERE] * 8 + matrix_pieces(EARLY, lambda p, w: p),
            out_specs=pl.BlockSpec((1024, 1024), lambda p, w: (p, 0)),
            scratch_shapes=[
                pltpu.VMEM((4, 2, 2, 64, 1024), F32),
                pltpu.VMEM((1024, 512), BF16),
                pltpu.VMEM((1024, 512), BF16),
                pltpu.VMEM((512, 1024), BF16),
                pltpu.VMEM((512, 1024), BF16),
                pltpu.SemaphoreType.DMA((4,)),
            ],
        ),
        out_shape=jax.ShapeDtypeStruct((2048, 1024), F32),
        compiler_params=pltpu.CompilerParams(vmem_limit_bytes=VMEM_LIMIT),
        cost_estimate=pl.CostEstimate(
            flops=3 * 2 * 2048 * 512 * 1024, bytes_accessed=24 << 20, transcendentals=0
        ),
        name="early_product",
    )(
        where,
        *[pieces[i] for i in EARLY],
        *[crossed[i] for i in EARLY],
        *[own] * 4,
        *[other[m] for n in range(4) for m in range(2)],
    )


def slot_of(moving, step, row_pos):
    edge = (row_pos == 0).astype(jnp.int32)
    if moving:
        return jnp.where(step == 0, 1 - edge, 2)
    return jnp.where(step == 0, 3, edge)


def late_kernel(moving, where, *refs):
    ours, theirs = refs[:8], refs[8:16]
    y_ref = refs[16]
    own_refs, other_refs = refs[17:21], refs[21:29]
    outs = refs[29:-14]
    held_a, held_b, jh, jl, mh, ml, yh, yl, qh, ql, done, sem_a, sem_b, sem_out = refs[-14:]
    step = pl.program_id(0)
    row_pos, layer = where[0], where[2]
    slot = slot_of(moving, step, row_pos)
    pair = slot // 2

    @pl.when(step == 0)
    def _():
        for n, i in enumerate(LATE):

            @pl.when(layer == 0)
            def _(n=n, i=i):
                pltpu.make_async_copy(ours[i], held_a.at[n], sem_a.at[n]).start()

            @pl.when(layer == 1)
            def _(n=n, i=i):
                pltpu.make_async_copy(theirs[i], held_a.at[n], sem_a.at[n]).start()

        for i in range(8):

            @pl.when(layer == 0)
            def _(i=i):
                pltpu.make_async_copy(theirs[i].at[:, 0], held_b.at[i], sem_b.at[i]).start()

            @pl.when(layer == 1)
            def _(i=i):
                pltpu.make_async_copy(ours[i].at[:, 1], held_b.at[i], sem_b.at[i]).start()

    halves_of_matrix(own_refs, other_refs, mh, ml)

    @pl.when(step == 0)
    def _():
        for n, i in enumerate(LATE):
            pltpu.make_async_copy(ours[i], held_a.at[n], sem_a.at[n]).wait()

    for n in range(4):
        for a in range(2):
            cols = pl.ds(pl.multiple_of((slot % 2) * 512 + a * 256, 256), 256)
            high, low = turned(held_a, n, pair, cols)
            jh[a * 256 : a * 256 + 256, n * 128 : n * 128 + 128] = high
            jl[a * 256 : a * 256 + 256, n * 128 : n * 128 + 128] = low

    for h in range(2):
        cols = slice(h * 512, h * 512 + 512)
        high, low = split(y_ref[:, cols] + product(jh[...], jl[...], mh[:, cols], ml[:, cols]))
        yh[:, cols] = high
        yl[:, cols] = low

    @pl.when(step == 0)
    def _():
        for i, start in enumerate(holders(row_pos)):
            pltpu.make_async_copy(ours[i].at[:, 0], held_b.at[i], sem_b.at[i]).wait()
            base = (start ^ (2 * layer)) * 128
            for half in range(2):
                high, low = split(held_b[i, half])
                rows = pl.ds(pl.multiple_of(base + half * 64, 64), 64)
                qh[rows, :] = high
                ql[rows, :] = low

    for h in range(4):
        cols = slice(h * 256, h * 256 + 256)
        done[step, h] = product(yh[...], yl[...], qh[:, cols], ql[:, cols])

    order = (3 * layer, layer + 1, 2 - layer, 3 - 3 * layer, 3 - 3 * layer)

    def leave(s, *targets):
        for n, target in enumerate(targets):
            pltpu.make_async_copy(done.at[s, order[n]], target, sem_out.at[s, n]).start()

    for s in range(2):

        @pl.when(step == s)
        def _(s=s):
            if moving:
                d_down, d_up, w_down, w_up, beside = outs
                d, w = ((d_down, w_down), (d_up, w_up))[s]
                leave(s, w, beside.at[s], d.at[0], d.at[1])
            else:
                straight, across, still, beside = outs
                leave(s, still.at[s], beside.at[s], straight.at[s], across.at[s], beside.at[2 + s])

    @pl.when(step == 1)
    def _():
        for s in range(2):
            for n in range(4 if moving else 5):
                pltpu.make_async_copy(done.at[s, 0], outs[0].at[0], sem_out.at[s, n]).wait()


def late_product(moving, where, pieces, crossed, y, own, other):
    one = jax.ShapeDtypeStruct((512, 256), F32)
    two = jax.ShapeDtypeStruct((2, 512, 256), F32)
    four = jax.ShapeDtypeStruct((4, 512, 256), F32)
    shapes = [two, two, one, one, two] if moving else [two, two, two, four]

    def kernel(where, *refs):
        late_kernel(moving, where, *refs)

    def pair_of(step, w):
        return slot_of(moving, step, w[0]) // 2

    return pl.pallas_call(
        kernel,
        grid_spec=pltpu.PrefetchScalarGridSpec(
            num_scalar_prefetch=1,
            grid=(2,),
            in_specs=[ANYWHERE] * 16
            + [pl.BlockSpec((512, 1024), lambda s, w: (slot_of(moving, s, w[0]), 0))]
            + matrix_pieces(LATE, pair_of),
            out_specs=[ANYWHERE] * len(shapes),
            scratch_shapes=[
                pltpu.VMEM((4, 2, 2, 64, 1024), F32),
                pltpu.VMEM((8, 2, 64, 1024), F32),
                pltpu.VMEM((512, 512), BF16),
                pltpu.VMEM((512, 512), BF16),
                pltpu.VMEM((512, 1024), BF16),
                pltpu.VMEM((512, 1024), BF16),
                pltpu.VMEM((512, 1024), BF16),
                pltpu.VMEM((512, 1024), BF16),
                pltpu.VMEM((1024, 1024), BF16),
                pltpu.VMEM((1024, 1024), BF16),
                pltpu.VMEM((2, 4, 512, 256), F32),
                pltpu.SemaphoreType.DMA((4,)),
                pltpu.SemaphoreType.DMA((8,)),
                pltpu.SemaphoreType.DMA((2, 5)),
            ],
        ),
        out_shape=shapes,
        compiler_params=pltpu.CompilerParams(vmem_limit_bytes=VMEM_LIMIT),
        cost_estimate=pl.CostEstimate(
            flops=3 * 2 * 1024 * 1024 * (512 + 1024), bytes_accessed=24 << 20, transcendentals=0
        ),
        name="late_moving" if moving else "late_other",
    )(where, *pieces, *crossed, y, *[own] * 4, *[other[m] for n in range(4) for m in range(2)])


def fill_kernel(out_rows, choose, count, where, *refs):
    sources = refs[:count]
    out_ref, held, packed, in_sem, out_sem = refs[-5:]
    chosen = choose(where, sources)
    for k in range(2):
        for j in range(4):
            for condition, source in chosen[k][j]:

                @pl.when(condition)
                def _(source=source, k=k, j=j):
                    pltpu.make_async_copy(source, held.at[k, j], in_sem.at[k, j]).start()

    leaving = []
    for k in range(2):
        for j in range(4):
            pltpu.make_async_copy(chosen[k][j][0][1], held.at[k, j], in_sem.at[k, j]).wait()
            packed[k, :, j, :] = held[k, j]
        copy = pltpu.make_async_copy(packed.at[k], out_ref.at[out_rows[k]], out_sem.at[k])
        copy.start()
        leaving.append(copy)
    for copy in leaving:
        copy.wait()


def fill_rows(out_rows, choose, where, sources, previous):
    extra = [] if previous is None else [previous]
    count = len(sources)
    anywhere = pl.BlockSpec(memory_space=pl.ANY)

    def kernel(where, *refs):
        fill_kernel(out_rows, choose, count, where, *refs)

    return pl.pallas_call(
        kernel,
        grid_spec=pltpu.PrefetchScalarGridSpec(
            num_scalar_prefetch=1,
            grid=(1,),
            in_specs=[anywhere] * (count + len(extra)),
            out_specs=anywhere,
            scratch_shapes=[
                pltpu.VMEM((2, 4, 512, 256), F32),
                pltpu.VMEM((2, 512, 4, 256), F32),
                pltpu.SemaphoreType.DMA((2, 4)),
                pltpu.SemaphoreType.DMA((2,)),
            ],
        ),
        out_shape=jax.ShapeDtypeStruct((4, 512, 4, 256), F32),
        input_output_aliases={1 + count: 0} if extra else {},
        compiler_params=pltpu.CompilerParams(vmem_limit_bytes=VMEM_LIMIT),
        cost_estimate=pl.CostEstimate(flops=0, bytes_accessed=8 << 20, transcendentals=0),
        name="fill_rows",
    )(where, *sources, *extra)


def upward(r, c, l):
    if l == 0:
        return r, (c & 4) | ((c + 1) & 3), l
    return (r & 4) | ((r + 1) & 3), c, l


def downward(r, c, l):
    if l == 0:
        return r, (c & 4) | ((c + 3) & 3), l
    return (r & 4) | ((r + 3) & 3), c, l


def first_hop(r, c, l):
    return (r, c ^ 4, l) if l == 0 else (c, r, l)


def first_hop_across(r, c, l):
    return (c, r, 1) if l == 0 else (r, c ^ 4, 0)


def second_hop(r, c, l):
    return (r ^ 4, c, l) if l == 1 else (r, c, l)


def row_up(r, c, l):
    return (r + 1) & 7, c, l


def row_down(r, c, l):
    return (r + 7) & 7, c, l


def column_straight(r, c, l):
    if (c, l) in ((0, 0), (7, 1)):
        return r, c, 1 - l
    return r, c + (1 if l else -1), l


def column_across(r, c, l):
    if (c, l) in ((0, 0), (7, 1)):
        return r, c, l
    return r, c + (1 if l else -1), 1 - l


def ring_straight(r, c, l):
    return r, (c & 4) | ((c + (1 if l else 3)) & 3), l


def ring_across(r, c, l):
    return r, (c & 4) | ((c + (1 if l else 3)) & 3), 1 - l


def ring_change(r, c, l):
    return (r, c ^ 4, l) if c in (0, 7) else None


def shards(matrix, transforms):
    barrier = lax.optimization_barrier
    row_pos = lax.axis_index("row")
    col_pos = lax.axis_index("col")
    layer_pos = lax.axis_index("layer")
    where = jnp.stack([row_pos, col_pos, layer_pos]).astype(jnp.int32)
    mine = transforms[0]

    lower = layer_pos == 0
    hop = send(mine, first_hop)
    hop_across = send(mine, first_hop_across)
    beside = in_chip(mine)
    hop, hop_across, beside, mine = barrier((hop, hop_across, beside, mine))
    block = jnp.stack([jnp.where(lower, mine, beside), jnp.where(lower, beside, mine)])
    hop = jnp.stack([jnp.where(lower, hop, hop_across), jnp.where(lower, hop_across, hop)])
    own = matrix.transpose(2, 0, 1, 3).reshape(4, 2048, 256)
    away = lax.dynamic_slice_in_dim(own, 2 * (1 - layer_pos), 2, 0)
    other = [in_chip(away[m]) for m in range(2)]
    start = jnp.where(lower, block, hop)
    up = send(start, upward)
    down = send(start, downward)
    far_side = send(hop, second_hop)
    start, up, down, far_side = barrier((start, up, down, far_side))
    partner = jnp.where(lower, hop, far_side)
    partner_up = send(partner, upward)
    partner_down = send(partner, downward)
    crossed = {i: in_chip(x) for i, x in zip(EARLY, (start, partner, up, down))}
    up, partner_up, partner_down, *early = barrier(
        (up, partner_up, partner_down, *[crossed[i] for i in EARLY])
    )
    crossed = dict(zip(EARLY, early))
    far = send(up, upward)
    partner_far = send(partner_down, downward)
    y = early_product(
        where,
        [start, partner, up, None, down],
        [crossed.get(i) for i in range(5)],
        own,
        other,
    )
    crossed[3], crossed[5] = in_chip(partner_up), in_chip(partner_down)
    far, partner_far, y, crossed[3], crossed[5] = barrier(
        (far, partner_far, y, crossed[3], crossed[5])
    )
    crossed[6], crossed[7] = in_chip(far), in_chip(partner_far)
    pieces = [start, partner, up, partner_up, down, partner_down, far, partner_far]
    crossed = [crossed[i] for i in range(8)]
    d_down, d_up, w_down, w_up, beside = late_product(
        True, where, pieces, crossed, y, own, other
    )
    got_up = send(d_up, row_up)
    got_down = send(d_down, row_down)
    from_beside = in_chip(beside)
    straight, across, still, still_beside = late_product(
        False, where, pieces, crossed, y, own, other
    )
    got_up, got_down, straight, across = barrier((got_up, got_down, straight, across))
    edge_up = jnp.stack([w_up, from_beside[1]])
    edge_down = jnp.stack([w_down, from_beside[0]])
    got_straight = send(straight, ring_straight)
    got_across = send(across, ring_across)
    edge_up, edge_down, got_up, got_down = barrier((edge_up, edge_down, got_up, got_down))
    still_got_up = send(edge_up, row_up)
    still_got_down = send(edge_down, row_down)

    top = jnp.where(row_pos == 0, d_down, got_up)
    bottom = jnp.where(row_pos == 7, d_up, got_down)
    inside = jnp.where(lower, col_pos > 0, col_pos < 7)
    then_straight = jnp.stack([jnp.where(inside, x[0], x[1]) for x in (top, bottom)])
    then_across = jnp.stack([jnp.where(inside, x[1], x[0]) for x in (top, bottom)])
    then_got_straight = send(then_straight, column_straight)
    then_got_across = send(then_across, column_across)
    from_still = in_chip(still_beside)
    got_straight, got_across, then_straight = barrier((got_straight, got_across, then_straight))
    changing = jnp.where((col_pos == 0) == lower, got_across, got_straight)
    changed = send(changing, ring_change)

    def blocks(w, own, partner, moving, moving_beside, came_straight, came_across, came_changed):
        c, l = w[1], w[2]

        def both(condition, if_lower, if_upper):
            return [
                (condition & (l == which) & also, ref)
                for which, refs in ((0, if_lower), (1, if_upper))
                for also, ref in refs
            ]

        yes = c >= 0
        far_up = c == (4 if came_changed is not None else -1)
        far_down = c == (3 if came_changed is not None else -1)
        first = both((c > 0) & ~far_up, [(yes, came_across)], [(yes, came_straight)])
        last = both((c < 7) & ~far_down, [(yes, came_straight)], [(yes, came_across)])
        if came_changed is not None:
            first.append((far_up, came_changed))
            last.append((far_down, came_changed))
        return [
            first + both(c == 0, own, partner),
            both(yes, partner, own),
            both(c > 0, own, partner) + both(c == 0, [(yes, moving)], [(yes, moving_beside)]),
            last + both(c == 7, [(yes, moving_beside)], [(yes, moving)]),
        ]

    def choose_stay(w, refs):
        still, beside, straight, came_straight, came_across, came_changed = refs
        yes = w[1] >= 0
        return [
            blocks(
                w,
                [(yes, still.at[k])],
                [(yes, beside.at[k])],
                straight.at[k],
                beside.at[2 + k],
                came_straight.at[k],
                came_across.at[k],
                came_changed.at[k],
            )
            for k in range(2)
        ]

    out = fill_rows(
        (1, 2),
        choose_stay,
        where,
        [still, from_still, straight, got_straight, got_across, changed],
        None,
    )

    def choose_moved(w, refs):
        edge_up, edge_down, from_up, from_down, kept, came_straight, came_across = refs
        r = w[0]
        rows = [
            lambda n: [(r > 0, from_up.at[n]), (r == 0, edge_down.at[n])],
            lambda n: [(r < 7, from_down.at[n]), (r == 7, edge_up.at[n])],
        ]
        return [
            blocks(
                w,
                rows[k](0),
                rows[k](1),
                kept.at[k],
                came_straight.at[k],
                came_straight.at[k],
                came_across.at[k],
                None,
            )
            for k in range(2)
        ]

    return fill_rows(
        (0, 3),
        choose_moved,
        where,
        [
            edge_up,
            edge_down,
            still_got_up,
            still_got_down,
            then_across,
            then_got_straight,
            then_got_across,
        ],
        out,
    )


def solution(mesh):
    return jax.shard_map(
        shards,
        mesh=mesh,
        in_specs=(P("row", None, "col", "layer"), P(None, "row", ("col", "layer"), None)),
        out_specs=P("row", None, "col", "layer"),
        check_vma=False,
    )
```

time: 414 us -> 240 us (0.58)
  the two profiles are of different devices: /device:TPU:6 before, /device:TPU:0 now
where the time goes in v2:
time: 240 us; the launch traced here: 239 us
  waiting for transfers between devices  91.7 us (38%)
  Pallas kernels  63.3 us (26%)
  starting transfers between devices  59.6 us (25%)
  local copies, waits for them, and re-layouts  16.4 us (7%)
  other arithmetic  7.02 us (3%)
    ppermute x18, waiting for transfers between devices, send(): return lax.ppermute(x, AXES, route(place))  83 us
    ppermute x18, starting transfers between devices, send(): return lax.ppermute(x, AXES, route(place))  53.1 us
    pallas_call x2, Pallas kernels, late_product(): pl.pallas_call(kernel, grid_spec=pltpu.PrefetchScalarGridSpec(num_scalar_...  40.2 us
    pallas_call x1, Pallas kernels, early_product(): pl.pallas_call(early_kernel, grid_spec=pltpu.PrefetchScalarGridSpec(num_s...  14.2 us
    pallas_call x2, Pallas kernels, fill_rows(): pl.pallas_call(kernel, grid_spec=pltpu.PrefetchScalarGridSpec(num_scalar_...  8.91 us
    ppermute x13, waiting for transfers between devices, in_chip(): return lax.ppermute(x, 'layer', [(0, 1), (1, 0)])  8.64 us
    transpose x1, local copies, waits for them, and re-layouts, shards(): own = matrix.transpose(2, 0, 1, 3).reshape(4, 2048, 256)  8.4 us
    ppermute x13, starting transfers between devices, in_chip(): return lax.ppermute(x, 'layer', [(0, 1), (1, 0)])  6.54 us
  transfers between devices with their start and end apart: 31, of which 12 were waited for; matrix products, arithmetic and copies ran while one was open for 6% of the time, Pallas kernels for 16%

profile of v2, /device:TPU:0, one launch (start us, length us, event | category | flops | bytes accessed | tf_op | source)
XLA Modules:
  0.0 238.7 jit_solution(5806908995177682088)
XLA Ops:
  0.0 3.5 %collective-permute-start = (f32[2,64,1024]{2,1,0:T(8,128)}, f32[2,64,1024]{2,1,0:T(8,128)S(1)}, u32[]{:S(2)}, u32[]{:S(2)}) collective-permute-start(f32[2,64,1024]{2,1,0:T(8,128)} %bitcast.34), channel_id=1, source_target_pairs={{0,8},{1,1},{2,10},{3,17},{4,12},{5,33},{6,14},{7,49},{8,0},{9,65}... | collective-permute-start | bytes 1572872 | tf_op jit(solution)/shard_map/ppermute | solution.py:29
  4.1 11.9 %collective-permute-done = f32[2,64,1024]{2,1,0:T(8,128)S(1)} collective-permute-done((f32[2,64,1024]{2,1,0:T(8,128)}, f32[2,64,1024]{2,1,0:T(8,128)S(1)}, u32[]{:S(2)}, u32[]{:S(2)}) %collective-permute-start) | collective-permute-done | bytes 524320 | tf_op jit(solution)/shard_map/ppermute | solution.py:29
  19.5 10.7 %collective-permute-start.3 = (f32[2,2,64,1024]{3,2,1,0:T(8,128)S(1)}, f32[2,2,64,1024]{3,2,1,0:T(8,128)S(1)}, u32[]{:S(2)}, u32[]{:S(2)}) collective-permute-start(f32[2,2,64,1024]{3,2,1,0:T(8,128)S(1)} %get-tuple-element.48.refs_0_), channel_id=1, source_target_pairs={{0,2},{1,17},{2,4},{3,19},{4,6},{5,21},{6,0},{7,23},{8,10},{9,25},... | collective-permute-start | bytes 3145736 | tf_op jit(solution)/shard_map/ppermute | solution.py:29
  30.2 3.9 %collective-permute-start.4 = (f32[2,2,64,1024]{3,2,1,0:T(8,128)S(1)}, f32[2,2,64,1024]{3,2,1,0:T(8,128)S(1)}, u32[]{:S(2)}, u32[]{:S(2)}) collective-permute-start(f32[2,2,64,1024]{3,2,1,0:T(8,128)S(1)} %get-tuple-element.48.refs_0_), channel_id=1, source_target_pairs={{0,6},{1,49},{2,0},{3,51},{4,2},{5,53},{6,4},{7,55},{8,14},{9,57},... | collective-permute-start | bytes 3145736 | tf_op jit(solution)/shard_map/ppermute | solution.py:29
  34.1 9.5 %collective-permute-start.5 = (f32[2,2,64,1024]{3,2,1,0:T(8,128)}, f32[2,2,64,1024]{3,2,1,0:T(8,128)}, u32[]{:S(2)}, u32[]{:S(2)}) collective-permute-start(f32[2,2,64,1024]{3,2,1,0:T(8,128)} %get-tuple-element.91), channel_id=1, source_target_pairs={{0,0},{1,65},{2,2},{3,67},{4,4},{5,69},{6,6},{7,71},{8,8},{9,73},{... | collective-permute-start | bytes 3145736 | tf_op jit(solution)/shard_map/ppermute | solution.py:29
  43.5 8.4 %copy.4 = f32[4,4,512,256]{3,2,1,0:T(8,128)} copy(f32[4,4,512,256]{3,0,2,1:T(4,128)} %bitcast.33) | data formatting | bytes 16777216 | tf_op jit(solution)/shard_map/transpose | solution.py:419
  54.1 3.2 %collective-permute-start.7 = (f32[2,2,64,1024]{3,2,1,0:T(8,128)S(1)}, f32[2,2,64,1024]{3,2,1,0:T(8,128)}, u32[]{:S(2)}, u32[]{:S(2)}) collective-permute-start(f32[2,2,64,1024]{3,2,1,0:T(8,128)S(1)} %broadcast_select_fusion.3.refs_1_), channel_id=1, source_target_pairs={{0,6},{1,49},{2,0},{3,51},{4,2},{5,53},{6,4},{7,55},{8,14},{9,57},... | collective-permute-start | bytes 3145736 | tf_op jit(solution)/shard_map/ppermute | solution.py:29
  59.1 3.8 %dynamic-slice_bitcast_fusion = (f32[2048,256]{1,0:T(8,128)}, f32[2048,256]{1,0:T(8,128)S(1)}) fusion(f32[4,2048,256]{2,1,0:T(8,128)} %bitcast.20, s32[]{:T(128)S(6)} %add.6, s32[]{:T(128)S(6)} %select_n.91), kind=kLoop, calls=%fused_computation | loop fusion | bytes 8388616 | tf_op jit(solution)/shard_map/squeeze | solution.py:421
  63.5 6.7 %collective-permute-done.6.refs_3_ = f32[2,2,64,1024]{3,2,1,0:T(8,128)} collective-permute-done((f32[2,2,64,1024]{3,2,1,0:T(8,128)S(1)}, f32[2,2,64,1024]{3,2,1,0:T(8,128)}, u32[]{:S(2)}, u32[]{:S(2)}) %collective-permute-start.6) | collective-permute-done | bytes 1048608 | tf_op jit(solution)/shard_map/ppermute | solution.py:29
  73.9 3.0 %collective-permute-done.11.refs_7_.refs_12_ = f32[2,2,64,1024]{3,2,1,0:T(8,128)S(1)} collective-permute-done((f32[2,2,64,1024]{3,2,1,0:T(8,128)}, f32[2,2,64,1024]{3,2,1,0:T(8,128)S(1)}, u32[]{:S(2)}, u32[]{:S(2)}) %collective-permute-start.11) | collective-permute-done | bytes 1048608 | tf_op jit(solution)/shard_map/ppermute | solution.py:33
  76.9 3.2 %collective-permute-start.13 = (f32[2,2,64,1024]{3,2,1,0:T(8,128)}, f32[2,2,64,1024]{3,2,1,0:T(8,128)}, u32[]{:S(2)}, u32[]{:S(2)}) collective-permute-start(f32[2,2,64,1024]{3,2,1,0:T(8,128)} %collective-permute-done.7.refs_5_), channel_id=1, source_target_pairs={{0,6},{1,49},{2,0},{3,51},{4,2},{5,53},{6,4},{7,55},{8,14},{9,57},... | collective-permute-start | bytes 3145736 | tf_op jit(solution)/shard_map/ppermute | solution.py:29
  81.6 14.2 %early_product.1.refs_16_ = f32[2048,1024]{1,0:T(8,128)} custom-call(s32[3]{0:T(128)} %pad_add_fusion.where, f32[2,2,64,1024]{3,2,1,0:T(8,128)} %copy-done.1, f32[2,2,64,1024]{3,2,1,0:T(8,128)} %copy-done.2, f32[2,2,64,1024]{3,2,1,0:T(8,128)} %copy-done.3, f32[2,2,64,1024]{3,2,1,0:T(8,128)} %copy-done.4, f32[2,2,64,1024]{3,2,1,0:T(8,128)} %copy-done.8, ...), custom_call_target="tpu_custom_call" | custom-call | flops 6442450944 | bytes 25165824 | tf_op jit(solution)/shard_map/early_product/pallas_call | solution.py:116
  101.4 20.1 %late_moving.1 = (f32[2,512,256]{2,1,0:T(8,128)}, f32[2,512,256]{2,1,0:T(8,128)}, f32[512,256]{1,0:T(8,128)}, f32[512,256]{1,0:T(8,128)}, f32[2,512,256]{2,1,0:T(8,128)}) custom-call(s32[3]{0:T(128)} %pad_add_fusion.where, f32[2,2,64,1024]{3,2,1,0:T(8,128)} %copy-done.1, f32[2,2,64,1024]{3,2,1,0:T(8,128)} %copy-done.2, f32[2,2,64,1024]{3,2,1,0:T(8,128)} %copy-done.3, ...), custom_call_target="tpu_custom_call" | custom-call | flops 9663676416 | bytes 25165824 | tf_op jit(solution)/shard_map/late_moving/pallas_call | solution.py:259
  121.9 5.6 %collective-permute-start.22 = (f32[2,512,256]{2,1,0:T(8,128)}, f32[2,512,256]{2,1,0:T(8,128)S(1)}, u32[]{:S(2)}, u32[]{:S(2)}) collective-permute-start(f32[2,512,256]{2,1,0:T(8,128)} %get-tuple-element.68), channel_id=1, source_target_pairs={{0,112},{1,113},{2,114},{3,115},{4,116},{5,117},{6,118},{7,119},{8... | collective-permute-start | bytes 3145736 | tf_op jit(solution)/shard_map/ppermute | solution.py:29
  127.6 20.2 %late_other.1 = (f32[2,512,256]{2,1,0:T(8,128)}, f32[2,512,256]{2,1,0:T(8,128)}, f32[2,512,256]{2,1,0:T(8,128)}, f32[4,512,256]{2,1,0:T(8,128)}) custom-call(s32[3]{0:T(128)} %pad_add_fusion.where, f32[2,2,64,1024]{3,2,1,0:T(8,128)} %copy-done.1, f32[2,2,64,1024]{3,2,1,0:T(8,128)} %copy-done.2, f32[2,2,64,1024]{3,2,1,0:T(8,128)} %copy-done.3, ...), custom_call_target="tpu_custom_call" | custom-call | flops 9663676416 | bytes 25165824 | tf_op jit(solution)/shard_map/late_other/pallas_call | solution.py:259
  148.0 3.0 %collective-permute-done.21 = f32[2,512,256]{2,1,0:T(8,128)S(1)} collective-permute-done((f32[2,512,256]{2,1,0:T(8,128)}, f32[2,512,256]{2,1,0:T(8,128)S(1)}, u32[]{:S(2)}, u32[]{:S(2)}) %collective-permute-start.21) | collective-permute-done | bytes 1048608 | tf_op jit(solution)/shard_map/ppermute | solution.py:29
  156.7 21.7 %collective-permute-done.28.refs_3_ = f32[2,512,256]{2,1,0:T(8,128)S(1)} collective-permute-done((f32[2,512,256]{2,1,0:T(8,128)S(1)}, f32[2,512,256]{2,1,0:T(8,128)S(1)}, u32[]{:S(2)}, u32[]{:S(2)}) %collective-permute-start.28) | collective-permute-done | bytes 1048608 | tf_op jit(solution)/shard_map/ppermute | solution.py:29
  178.4 11.2 %collective-permute-done.29.refs_4_ = f32[2,512,256]{2,1,0:T(8,128)S(1)} collective-permute-done((f32[2,512,256]{2,1,0:T(8,128)S(1)}, f32[2,512,256]{2,1,0:T(8,128)S(1)}, u32[]{:S(2)}, u32[]{:S(2)}) %collective-permute-start.29) | collective-permute-done | bytes 1048608 | tf_op jit(solution)/shard_map/ppermute | solution.py:29
  189.8 3.8 %collective-permute-start.30 = (f32[2,512,256]{2,1,0:T(8,128)S(1)}, f32[2,512,256]{2,1,0:T(8,128)S(1)}, u32[]{:S(2)}, u32[]{:S(2)}) collective-permute-start(f32[2,512,256]{2,1,0:T(8,128)S(1)} %broadcast_select_fusion), channel_id=1, source_target_pairs={{0,8},{1,9},{14,6},{15,7},{16,24},{17,25},{30,22},{31,23},{32,40},... | collective-permute-start | bytes 3145736 | tf_op jit(solution)/shard_map/ppermute | solution.py:29
  195.3 5.7 %collective-permute-start.24 = (f32[2,512,256]{2,1,0:T(8,128)S(1)}, f32[2,512,256]{2,1,0:T(8,128)}, u32[]{:S(2)}, u32[]{:S(2)}) collective-permute-start(f32[2,512,256]{2,1,0:T(8,128)S(1)} %pad_maximum_fusion.2.refs_1_), channel_id=1, source_target_pairs={{0,112},{1,113},{2,114},{3,115},{4,116},{5,117},{6,118},{7,119},{8... | collective-permute-start | bytes 3145736 | tf_op jit(solution)/shard_map/ppermute | solution.py:29
  201.0 15.7 %collective-permute-done.30.refs_5_ = f32[2,512,256]{2,1,0:T(8,128)S(1)} collective-permute-done((f32[2,512,256]{2,1,0:T(8,128)S(1)}, f32[2,512,256]{2,1,0:T(8,128)S(1)}, u32[]{:S(2)}, u32[]{:S(2)}) %collective-permute-start.30) | collective-permute-done | bytes 1048608 | tf_op jit(solution)/shard_map/ppermute | solution.py:29
  217.6 4.5 %fill_rows.2.refs_7_ = f32[4,512,4,256]{3,2,1,0:T(4,128)} custom-call(s32[3]{0:T(128)} %pad_add_fusion.where, f32[2,512,256]{2,1,0:T(8,128)} %get-tuple-element.77.refs_0_, f32[4,512,256]{2,1,0:T(8,128)} %copy-done.19, f32[2,512,256]{2,1,0:T(8,128)} %get-tuple-element.79.refs_2_, f32[2,512,256]{2,1,0:T(8,128)} %copy-done.14, f32[2,512,256]{2,1,0:T(8,128)} %copy-done.15, ...), custom_call_target="tpu_custom_call" | custom-call | bytes 8388608 | tf_op jit(solution)/shard_map/fill_rows/pallas_call | solution.py:326
  222.1 11.9 %collective-permute-done.23.refs_2_ = f32[2,512,256]{2,1,0:T(8,128)} collective-permute-done((f32[2,512,256]{2,1,0:T(8,128)S(1)}, f32[2,512,256]{2,1,0:T(8,128)}, u32[]{:S(2)}, u32[]{:S(2)}) %collective-permute-start.23) | collective-permute-done | bytes 1048608 | tf_op jit(solution)/shard_map/ppermute | solution.py:29
  234.1 4.5 %fill_rows.3 = f32[4,512,4,256]{3,2,1,0:T(4,128)} custom-call(s32[3]{0:T(128)} %pad_add_fusion.where, f32[2,512,256]{2,1,0:T(8,128)} %copy-done.17, f32[2,512,256]{2,1,0:T(8,128)} %copy-done.16, f32[2,512,256]{2,1,0:T(8,128)} %collective-permute-done.23.refs_2_, f32[2,512,256]{2,1,0:T(8,128)} %collective-permute-done.24.refs_3_, ...), custom_call_target="tpu_custom_call", output_to_operand_aliasing={{}: (8, {})} | custom-call | bytes 8388608 | tf_op jit(solution)/shard_map/fill_rows/pallas_call | solution.py:326
  (115 shorter events, 28.2 us)
Async XLA Ops:
  0.0 16.1 %collective-permute-start = (f32[2,64,1024]{2,1,0:T(8,128)}, f32[2,64,1024]{2,1,0:T(8,128)S(1)}, u32[]{:S(2)}, u32[]{:S(2)}) collective-permute-start(f32[2,64,1024]{2,1,0:T(8,128)} %bitcast.34), channel_id=1, source_target_pairs={{0,8},{1,1},{2,10},{3,17},{4,12},{5,33},{6,14},{7,49},{8,0},{9,65}... | collective-permute-start | bytes 1572872 | tf_op jit(solution)/shard_map/ppermute | solution.py:29
  19.5 32.5 %collective-permute-start.3 = (f32[2,2,64,1024]{3,2,1,0:T(8,128)S(1)}, f32[2,2,64,1024]{3,2,1,0:T(8,128)S(1)}, u32[]{:S(2)}, u32[]{:S(2)}) collective-permute-start(f32[2,2,64,1024]{3,2,1,0:T(8,128)S(1)} %get-tuple-element.48.refs_0_), channel_id=1, source_target_pairs={{0,2},{1,17},{2,4},{3,19},{4,6},{5,21},{6,0},{7,23},{8,10},{9,25},... | collective-permute-start | bytes 3145736 | tf_op jit(solution)/shard_map/ppermute | solution.py:29
  30.2 21.8 %collective-permute-start.4 = (f32[2,2,64,1024]{3,2,1,0:T(8,128)S(1)}, f32[2,2,64,1024]{3,2,1,0:T(8,128)S(1)}, u32[]{:S(2)}, u32[]{:S(2)}) collective-permute-start(f32[2,2,64,1024]{3,2,1,0:T(8,128)S(1)} %get-tuple-element.48.refs_0_), channel_id=1, source_target_pairs={{0,6},{1,49},{2,0},{3,51},{4,2},{5,53},{6,4},{7,55},{8,14},{9,57},... | collective-permute-start | bytes 3145736 | tf_op jit(solution)/shard_map/ppermute | solution.py:29
  34.1 17.9 %collective-permute-start.5 = (f32[2,2,64,1024]{3,2,1,0:T(8,128)}, f32[2,2,64,1024]{3,2,1,0:T(8,128)}, u32[]{:S(2)}, u32[]{:S(2)}) collective-permute-start(f32[2,2,64,1024]{3,2,1,0:T(8,128)} %get-tuple-element.91), channel_id=1, source_target_pairs={{0,0},{1,65},{2,2},{3,67},{4,4},{5,69},{6,6},{7,71},{8,8},{9,73},{... | collective-permute-start | bytes 3145736 | tf_op jit(solution)/shard_map/ppermute | solution.py:29
  54.1 16.2 %collective-permute-start.6 = (f32[2,2,64,1024]{3,2,1,0:T(8,128)S(1)}, f32[2,2,64,1024]{3,2,1,0:T(8,128)}, u32[]{:S(2)}, u32[]{:S(2)}) collective-permute-start(f32[2,2,64,1024]{3,2,1,0:T(8,128)S(1)} %broadcast_select_fusion.3.refs_1_), channel_id=1, source_target_pairs={{0,2},{1,17},{2,4},{3,19},{4,6},{5,21},{6,0},{7,23},{8,10},{9,25},... | collective-permute-start | bytes 3145736 | tf_op jit(solution)/shard_map/ppermute | solution.py:29
  54.1 17.2 %collective-permute-start.7 = (f32[2,2,64,1024]{3,2,1,0:T(8,128)S(1)}, f32[2,2,64,1024]{3,2,1,0:T(8,128)}, u32[]{:S(2)}, u32[]{:S(2)}) collective-permute-start(f32[2,2,64,1024]{3,2,1,0:T(8,128)S(1)} %broadcast_select_fusion.3.refs_1_), channel_id=1, source_target_pairs={{0,6},{1,49},{2,0},{3,51},{4,2},{5,53},{6,4},{7,55},{8,14},{9,57},... | collective-permute-start | bytes 3145736 | tf_op jit(solution)/shard_map/ppermute | solution.py:29
  57.4 14.0 %collective-permute-start.9 = (f32[2,2,64,1024]{3,2,1,0:T(8,128)S(1)}, f32[2,2,64,1024]{3,2,1,0:T(8,128)S(1)}, u32[]{:S(2)}, u32[]{:S(2)}) collective-permute-start(f32[2,2,64,1024]{3,2,1,0:T(8,128)S(1)} %broadcast_select_fusion.3.refs_1_), channel_id=1, source_target_pairs={{0,1},{1,0},{2,3},{3,2},{4,5},{5,4},{6,7},{7,6},{8,9},{9,8},{10,11... | collective-permute-start | bytes 3145736 | tf_op jit(solution)/shard_map/ppermute | solution.py:33
  62.9 17.2 %collective-permute-start.14 = (f32[2048,256]{1,0:T(8,128)S(1)}, f32[2048,256]{1,0:T(8,128)S(1)}, u32[]{:S(2)}, u32[]{:S(2)}) collective-permute-start(f32[2048,256]{1,0:T(8,128)S(1)} %get-tuple-element.84), channel_id=1, source_target_pairs={{0,1},{1,0},{2,3},{3,2},{4,5},{5,4},{6,7},{7,6},{8,9},{9,8},{10,11... | collective-permute-start | bytes 6291464 | tf_op jit(solution)/shard_map/ppermute | solution.py:33
  63.0 18.3 %collective-permute-start.15 = (f32[2048,256]{1,0:T(8,128)}, f32[2048,256]{1,0:T(8,128)}, u32[]{:S(2)}, u32[]{:S(2)}) collective-permute-start(f32[2048,256]{1,0:T(8,128)} %get-tuple-element.83), channel_id=1, source_target_pairs={{0,1},{1,0},{2,3},{3,2},{4,5},{5,4},{6,7},{7,6},{8,9},{9,8},{10,11... | collective-permute-start | bytes 6291464 | tf_op jit(solution)/shard_map/ppermute | solution.py:33
  76.9 18.9 %collective-permute-start.12 = (f32[2,2,64,1024]{3,2,1,0:T(8,128)}, f32[2,2,64,1024]{3,2,1,0:T(8,128)S(1)}, u32[]{:S(2)}, u32[]{:S(2)}) collective-permute-start(f32[2,2,64,1024]{3,2,1,0:T(8,128)} %copy-done.3), channel_id=1, source_target_pairs={{0,2},{1,17},{2,4},{3,19},{4,6},{5,21},{6,0},{7,23},{8,10},{9,25},... | collective-permute-start | bytes 3145736 | tf_op jit(solution)/shard_map/ppermute | solution.py:29
  76.9 18.9 %collective-permute-start.13 = (f32[2,2,64,1024]{3,2,1,0:T(8,128)}, f32[2,2,64,1024]{3,2,1,0:T(8,128)}, u32[]{:S(2)}, u32[]{:S(2)}) collective-permute-start(f32[2,2,64,1024]{3,2,1,0:T(8,128)} %collective-permute-done.7.refs_5_), channel_id=1, source_target_pairs={{0,6},{1,49},{2,0},{3,51},{4,2},{5,53},{6,4},{7,55},{8,14},{9,57},... | collective-permute-start | bytes 3145736 | tf_op jit(solution)/shard_map/ppermute | solution.py:29
  80.1 15.7 %collective-permute-start.16 = (f32[2,2,64,1024]{3,2,1,0:T(8,128)}, f32[2,2,64,1024]{3,2,1,0:T(8,128)}, u32[]{:S(2)}, u32[]{:S(2)}) collective-permute-start(f32[2,2,64,1024]{3,2,1,0:T(8,128)} %collective-permute-done.6.refs_3_), channel_id=1, source_target_pairs={{0,1},{1,0},{2,3},{3,2},{4,5},{5,4},{6,7},{7,6},{8,9},{9,8},{10,11... | collective-permute-start | bytes 3145736 | tf_op jit(solution)/shard_map/ppermute | solution.py:33
  80.2 15.7 %collective-permute-start.17 = (f32[2,2,64,1024]{3,2,1,0:T(8,128)}, f32[2,2,64,1024]{3,2,1,0:T(8,128)}, u32[]{:S(2)}, u32[]{:S(2)}) collective-permute-start(f32[2,2,64,1024]{3,2,1,0:T(8,128)} %collective-permute-done.7.refs_5_), channel_id=1, source_target_pairs={{0,1},{1,0},{2,3},{3,2},{4,5},{5,4},{6,7},{7,6},{8,9},{9,8},{10,11... | collective-permute-start | bytes 3145736 | tf_op jit(solution)/shard_map/ppermute | solution.py:33
  121.5 26.4 %collective-permute-start.20 = (f32[2,512,256]{2,1,0:T(8,128)}, f32[2,512,256]{2,1,0:T(8,128)S(1)}, u32[]{:S(2)}, u32[]{:S(2)}) collective-permute-start(f32[2,512,256]{2,1,0:T(8,128)} %get-tuple-element.65), channel_id=1, source_target_pairs={{0,1},{1,0},{2,3},{3,2},{4,5},{5,4},{6,7},{7,6},{8,9},{9,8},{10,11... | collective-permute-start | bytes 3145736 | tf_op jit(solution)/shard_map/ppermute | solution.py:33
  121.9 29.0 %collective-permute-start.21 = (f32[2,512,256]{2,1,0:T(8,128)}, f32[2,512,256]{2,1,0:T(8,128)S(1)}, u32[]{:S(2)}, u32[]{:S(2)}) collective-permute-start(f32[2,512,256]{2,1,0:T(8,128)} %get-tuple-element.67), channel_id=1, source_target_pairs={{0,16},{1,17},{2,18},{3,19},{4,20},{5,21},{6,22},{7,23},{8,24},{9,... | collective-permute-start | bytes 3145736 | tf_op jit(solution)/shard_map/ppermute | solution.py:29
  121.9 29.0 %collective-permute-start.22 = (f32[2,512,256]{2,1,0:T(8,128)}, f32[2,512,256]{2,1,0:T(8,128)S(1)}, u32[]{:S(2)}, u32[]{:S(2)}) collective-permute-start(f32[2,512,256]{2,1,0:T(8,128)} %get-tuple-element.68), channel_id=1, source_target_pairs={{0,112},{1,113},{2,114},{3,115},{4,116},{5,117},{6,118},{7,119},{8... | collective-permute-start | bytes 3145736 | tf_op jit(solution)/shard_map/ppermute | solution.py:29
  147.8 47.5 %collective-permute-start.27 = (f32[4,512,256]{2,1,0:T(8,128)}, f32[4,512,256]{2,1,0:T(8,128)S(1)}, u32[]{:S(2)}, u32[]{:S(2)}) collective-permute-start(f32[4,512,256]{2,1,0:T(8,128)} %get-tuple-element.78), channel_id=1, source_target_pairs={{0,1},{1,0},{2,3},{3,2},{4,5},{5,4},{6,7},{7,6},{8,9},{9,8},{10,11... | collective-permute-start | bytes 6291464 | tf_op jit(solution)/shard_map/ppermute | solution.py:33
  152.9 25.5 %collective-permute-start.28 = (f32[2,512,256]{2,1,0:T(8,128)S(1)}, f32[2,512,256]{2,1,0:T(8,128)S(1)}, u32[]{:S(2)}, u32[]{:S(2)}) collective-permute-start(f32[2,512,256]{2,1,0:T(8,128)S(1)} %copy-done.20), channel_id=1, source_target_pairs={{0,6},{1,3},{2,0},{3,5},{4,2},{5,7},{6,4},{7,1},{8,14},{9,11},{10,... | collective-permute-start | bytes 3145736 | tf_op jit(solution)/shard_map/ppermute | solution.py:29
  154.9 34.8 %collective-permute-start.29 = (f32[2,512,256]{2,1,0:T(8,128)S(1)}, f32[2,512,256]{2,1,0:T(8,128)S(1)}, u32[]{:S(2)}, u32[]{:S(2)}) collective-permute-start(f32[2,512,256]{2,1,0:T(8,128)S(1)} %copy-done.27), channel_id=1, source_target_pairs={{0,7},{1,2},{2,1},{3,4},{4,3},{5,6},{6,5},{7,0},{8,15},{9,10},{10,... | collective-permute-start | bytes 3145736 | tf_op jit(solution)/shard_map/ppermute | solution.py:29
  156.4 65.7 %collective-permute-start.25 = (f32[2,512,256]{2,1,0:T(8,128)}, f32[2,512,256]{2,1,0:T(8,128)}, u32[]{:S(2)}, u32[]{:S(2)}) collective-permute-start(f32[2,512,256]{2,1,0:T(8,128)} %pad_maximum_fusion.4), channel_id=1, source_target_pairs={{0,1},{1,3},{2,0},{3,5},{4,2},{5,7},{6,4},{7,9},{8,6},{9,11},{10,8... | collective-permute-start | bytes 3145736 | tf_op jit(solution)/shard_map/ppermute | solution.py:29
  189.8 26.9 %collective-permute-start.30 = (f32[2,512,256]{2,1,0:T(8,128)S(1)}, f32[2,512,256]{2,1,0:T(8,128)S(1)}, u32[]{:S(2)}, u32[]{:S(2)}) collective-permute-start(f32[2,512,256]{2,1,0:T(8,128)S(1)} %broadcast_select_fusion), channel_id=1, source_target_pairs={{0,8},{1,9},{14,6},{15,7},{16,24},{17,25},{30,22},{31,23},{32,40},... | collective-permute-start | bytes 3145736 | tf_op jit(solution)/shard_map/ppermute | solution.py:29
  193.6 28.5 %collective-permute-start.26 = (f32[2,512,256]{2,1,0:T(8,128)S(1)}, f32[2,512,256]{2,1,0:T(8,128)}, u32[]{:S(2)}, u32[]{:S(2)}) collective-permute-start(f32[2,512,256]{2,1,0:T(8,128)S(1)} %pad_maximum_fusion.3.refs_4_), channel_id=1, source_target_pairs={{0,0},{1,2},{2,1},{3,4},{4,3},{5,6},{6,5},{7,8},{8,7},{9,10},{10,9... | collective-permute-start | bytes 3145736 | tf_op jit(solution)/shard_map/ppermute | solution.py:29
  195.3 38.8 %collective-permute-start.23 = (f32[2,512,256]{2,1,0:T(8,128)S(1)}, f32[2,512,256]{2,1,0:T(8,128)}, u32[]{:S(2)}, u32[]{:S(2)}) collective-permute-start(f32[2,512,256]{2,1,0:T(8,128)S(1)} %pad_maximum_fusion.1.refs_0_), channel_id=1, source_target_pairs={{0,16},{1,17},{2,18},{3,19},{4,20},{5,21},{6,22},{7,23},{8,24},{9,... | collective-permute-start | bytes 3145736 | tf_op jit(solution)/shard_map/ppermute | solution.py:29
  195.3 38.8 %collective-permute-start.24 = (f32[2,512,256]{2,1,0:T(8,128)S(1)}, f32[2,512,256]{2,1,0:T(8,128)}, u32[]{:S(2)}, u32[]{:S(2)}) collective-permute-start(f32[2,512,256]{2,1,0:T(8,128)S(1)} %pad_maximum_fusion.2.refs_1_), channel_id=1, source_target_pairs={{0,112},{1,113},{2,114},{3,115},{4,116},{5,117},{6,118},{7,119},{8... | collective-permute-start | bytes 3145736 | tf_op jit(solution)/shard_map/ppermute | solution.py:29
  (35 other events, 410.0 us)

commit v3 on v2

--- a/solution.py
+++ b/solution.py
@@ -144,49 +144,68 @@
     )
 
 
-def slot_of(moving, step, row_pos):
-    edge = (row_pos == 0).astype(jnp.int32)
-    if moving:
-        return jnp.where(step == 0, 1 - edge, 2)
-    return jnp.where(step == 0, 3, edge)
-
-
-def late_kernel(moving, where, *refs):
+def by_role(slot, row_pos, down, up, stays):
+    for s, condition, action in (
+        (0, row_pos == 0, down),
+        (0, row_pos > 0, lambda s: stays(s, 1)),
+        (1, row_pos == 0, lambda s: stays(s, 1)),
+        (1, row_pos > 0, down),
+        (2, row_pos >= 0, up),
+        (3, row_pos >= 0, lambda s: stays(s, 0)),
+    ):
+
+        @pl.when((slot == s) & condition)
+        def _(s=s, action=action):
+            action(s)
+
+
+def fetch_columns(layer, ours, theirs, lane, held, sem):
+    for core, sources in ((0, theirs), (1, ours)):
+
+        @pl.when(layer == core)
+        def _(core=core, sources=sources):
+            for i in range(8):
+                source = sources[i].at[:, core, :, pl.ds(lane(core) * 512, 512)]
+                pltpu.make_async_copy(source, held.at[i], sem.at[i]).start()
+
+
+def take_columns(row_pos, layer, held, sem, qh, ql):
+    for i, start in enumerate(holders(row_pos)):
+        pltpu.make_async_copy(held.at[i], held.at[i], sem.at[i]).wait()
+        base = (start ^ (2 * layer)) * 128
+        for half in range(2):
+            high, low = split(held[i, half])
+            rows = pl.ds(pl.multiple_of(base + half * 64, 64), 64)
+            qh[rows, :] = high
+            ql[rows, :] = low
+
+
+def moving_kernel(where, *refs):
     ours, theirs = refs[:8], refs[8:16]
     y_ref = refs[16]
     own_refs, other_refs = refs[17:21], refs[21:29]
-    outs = refs[29:-14]
-    held_a, held_b, jh, jl, mh, ml, yh, yl, qh, ql, done, sem_a, sem_b, sem_out = refs[-14:]
-    step = pl.program_id(0)
+    yh, yl, d_down, d_up, straight, across = refs[29:35]
+    held_a, held_b, jh, jl, mh, ml, qh, ql, done, sem_a, sem_b, sem_out = refs[35:]
+    slot = pl.program_id(0)
     row_pos, layer = where[0], where[2]
-    slot = slot_of(moving, step, row_pos)
     pair = slot // 2
 
-    @pl.when(step == 0)
-    def _():
-        for n, i in enumerate(LATE):
-
-            @pl.when(layer == 0)
-            def _(n=n, i=i):
-                pltpu.make_async_copy(ours[i], held_a.at[n], sem_a.at[n]).start()
-
-            @pl.when(layer == 1)
-            def _(n=n, i=i):
-                pltpu.make_async_copy(theirs[i], held_a.at[n], sem_a.at[n]).start()
-
-        for i in range(8):
-
-            @pl.when(layer == 0)
-            def _(i=i):
-                pltpu.make_async_copy(theirs[i].at[:, 0], held_b.at[i], sem_b.at[i]).start()
-
-            @pl.when(layer == 1)
-            def _(i=i):
-                pltpu.make_async_copy(ours[i].at[:, 1], held_b.at[i], sem_b.at[i]).start()
-
-    halves_of_matrix(own_refs, other_refs, mh, ml)
-
-    @pl.when(step == 0)
+    @pl.when(slot == 0)
+    def _():
+        for core, sources in ((0, ours), (1, theirs)):
+
+            @pl.when(layer == core)
+            def _(sources=sources):
+                for n, i in enumerate(LATE):
+                    pltpu.make_async_copy(sources[i], held_a.at[n], sem_a.at[n]).start()
+
+        fetch_columns(layer, ours, theirs, lambda core: 1 - core, held_b, sem_b)
+
+    @pl.when(slot % 2 == 0)
+    def _():
+        halves_of_matrix(own_refs, other_refs, mh, ml)
+
+    @pl.when(slot == 0)
     def _():
         for n, i in enumerate(LATE):
             pltpu.make_async_copy(ours[i], held_a.at[n], sem_a.at[n]).wait()
@@ -204,91 +223,133 @@
         yh[:, cols] = high
         yl[:, cols] = low
 
-    @pl.when(step == 0)
-    def _():
-        for i, start in enumerate(holders(row_pos)):
-            pltpu.make_async_copy(ours[i].at[:, 0], held_b.at[i], sem_b.at[i]).wait()
-            base = (start ^ (2 * layer)) * 128
-            for half in range(2):
-                high, low = split(held_b[i, half])
-                rows = pl.ds(pl.multiple_of(base + half * 64, 64), 64)
-                qh[rows, :] = high
-                ql[rows, :] = low
-
-    for h in range(4):
+    @pl.when(slot == 0)
+    def _():
+        take_columns(row_pos, layer, held_b, sem_b, qh, ql)
+
+    for h in range(2):
         cols = slice(h * 256, h * 256 + 256)
-        done[step, h] = product(yh[...], yl[...], qh[:, cols], ql[:, cols])
-
-    order = (3 * layer, layer + 1, 2 - layer, 3 - 3 * layer, 3 - 3 * layer)
-
-    def leave(s, *targets):
-        for n, target in enumerate(targets):
-            pltpu.make_async_copy(done.at[s, order[n]], target, sem_out.at[s, n]).start()
-
-    for s in range(2):
-
-        @pl.when(step == s)
-        def _(s=s):
-            if moving:
-                d_down, d_up, w_down, w_up, beside = outs
-                d, w = ((d_down, w_down), (d_up, w_up))[s]
-                leave(s, w, beside.at[s], d.at[0], d.at[1])
-            else:
-                straight, across, still, beside = outs
-                leave(s, still.at[s], beside.at[s], straight.at[s], across.at[s], beside.at[2 + s])
-
-    @pl.when(step == 1)
-    def _():
-        for s in range(2):
-            for n in range(4 if moving else 5):
-                pltpu.make_async_copy(done.at[s, 0], outs[0].at[0], sem_out.at[s, n]).wait()
-
-
-def late_product(moving, where, pieces, crossed, y, own, other):
-    one = jax.ShapeDtypeStruct((512, 256), F32)
-    two = jax.ShapeDtypeStruct((2, 512, 256), F32)
-    four = jax.ShapeDtypeStruct((4, 512, 256), F32)
-    shapes = [two, two, one, one, two] if moving else [two, two, two, four]
-
-    def kernel(where, *refs):
-        late_kernel(moving, where, *refs)
-
-    def pair_of(step, w):
-        return slot_of(moving, step, w[0]) // 2
-
+        done[slot, h] = product(yh[...], yl[...], qh[:, cols], ql[:, cols])
+
+    def leave(s, near, far):
+        pltpu.make_async_copy(done.at[s, layer], near, sem_out.at[s, 0]).start()
+        pltpu.make_async_copy(done.at[s, 1 - layer], far, sem_out.at[s, 1]).start()
+
+    by_role(
+        slot,
+        row_pos,
+        lambda s: leave(s, d_down.at[0], d_down.at[1]),
+        lambda s: leave(s, d_up.at[0], d_up.at[1]),
+        lambda s, k: leave(s, straight.at[k], across.at[k]),
+    )
+
+    @pl.when(slot == 3)
+    def _():
+        for s in range(4):
+            for n in range(2):
+                pltpu.make_async_copy(done.at[s, n], d_up.at[n], sem_out.at[s, n]).wait()
+
+
+def still_kernel(where, *refs):
+    ours, theirs = refs[:8], refs[8:16]
+    yh, yl = refs[16:18]
+    w_down, w_up, still, beside = refs[18:22]
+    held_b, qh, ql, done, sem_b, sem_out = refs[22:]
+    slot = pl.program_id(0)
+    row_pos, layer = where[0], where[2]
+
+    @pl.when(slot == 0)
+    def _():
+        fetch_columns(layer, ours, theirs, lambda core: core, held_b, sem_b)
+        take_columns(row_pos, layer, held_b, sem_b, qh, ql)
+
+    for h in range(2):
+        cols = slice(h * 256, h * 256 + 256)
+        done[slot, h] = product(yh[...], yl[...], qh[:, cols], ql[:, cols])
+
+    def leave(s, near, far):
+        pltpu.make_async_copy(done.at[s, layer], near, sem_out.at[s, 0]).start()
+        pltpu.make_async_copy(done.at[s, 1 - layer], far, sem_out.at[s, 1]).start()
+
+    by_role(
+        slot,
+        row_pos,
+        lambda s: leave(s, w_down, beside.at[2]),
+        lambda s: leave(s, w_up, beside.at[3]),
+        lambda s, k: leave(s, still.at[k], beside.at[k]),
+    )
+
+    @pl.when(slot == 3)
+    def _():
+        for s in range(4):
+            for n in range(2):
+                pltpu.make_async_copy(done.at[s, n], w_up, sem_out.at[s, n]).wait()
+
+
+ONE = jax.ShapeDtypeStruct((512, 256), F32)
+TWO = jax.ShapeDtypeStruct((2, 512, 256), F32)
+FOUR = jax.ShapeDtypeStruct((4, 512, 256), F32)
+HALF = jax.ShapeDtypeStruct((2048, 1024), BF16)
+
+
+def moving_product(where, pieces, crossed, y, own, other):
+    block = pl.BlockSpec((512, 1024), lambda s, w: (s, 0))
     return pl.pallas_call(
-        kernel,
+        moving_kernel,
         grid_spec=pltpu.PrefetchScalarGridSpec(
             num_scalar_prefetch=1,
-            grid=(2,),
-            in_specs=[ANYWHERE] * 16
-            + [pl.BlockSpec((512, 1024), lambda s, w: (slot_of(moving, s, w[0]), 0))]
-            + matrix_pieces(LATE, pair_of),
-            out_specs=[ANYWHERE] * len(shapes),
+            grid=(4,),
+            in_specs=[ANYWHERE] * 16 + [block] + matrix_pieces(LATE, lambda s, w: s // 2),
+            out_specs=[block] * 2 + [ANYWHERE] * 4,
             scratch_shapes=[
                 pltpu.VMEM((4, 2, 2, 64, 1024), F32),
-                pltpu.VMEM((8, 2, 64, 1024), F32),
+                pltpu.VMEM((8, 2, 64, 512), F32),
                 pltpu.VMEM((512, 512), BF16),
                 pltpu.VMEM((512, 512), BF16),
                 pltpu.VMEM((512, 1024), BF16),
                 pltpu.VMEM((512, 1024), BF16),
-                pltpu.VMEM((512, 1024), BF16),
-                pltpu.VMEM((512, 1024), BF16),
-                pltpu.VMEM((1024, 1024), BF16),
-                pltpu.VMEM((1024, 1024), BF16),
-                pltpu.VMEM((2, 4, 512, 256), F32),
+                pltpu.VMEM((1024, 512), BF16),
+                pltpu.VMEM((1024, 512), BF16),
+                pltpu.VMEM((4, 2, 512, 256), F32),
                 pltpu.SemaphoreType.DMA((4,)),
                 pltpu.SemaphoreType.DMA((8,)),
-                pltpu.SemaphoreType.DMA((2, 5)),
+                pltpu.SemaphoreType.DMA((4, 2)),
             ],
         ),
-        out_shape=shapes,
+        out_shape=[HALF] * 2 + [TWO] * 4,
         compiler_params=pltpu.CompilerParams(vmem_limit_bytes=VMEM_LIMIT),
         cost_estimate=pl.CostEstimate(
-            flops=3 * 2 * 1024 * 1024 * (512 + 1024), bytes_accessed=24 << 20, transcendentals=0
+            flops=3 * 2 * 2048 * 1024 * (512 + 512), bytes_accessed=36 << 20, transcendentals=0
         ),
-        name="late_moving" if moving else "late_other",
+        name="moving_product",
     )(where, *pieces, *crossed, y, *[own] * 4, *[other[m] for n in range(4) for m in range(2)])
+
+
+def still_product(where, pieces, crossed, yh, yl):
+    block = pl.BlockSpec((512, 1024), lambda s, w: (s, 0))
+    return pl.pallas_call(
+        still_kernel,
+        grid_spec=pltpu.PrefetchScalarGridSpec(
+            num_scalar_prefetch=1,
+            grid=(4,),
+            in_specs=[ANYWHERE] * 16 + [block] * 2,
+            out_specs=[ANYWHERE] * 4,
+            scratch_shapes=[
+                pltpu.VMEM((8, 2, 64, 512), F32),
+                pltpu.VMEM((1024, 512), BF16),
+                pltpu.VMEM((1024, 512), BF16),
+                pltpu.VMEM((4, 2, 512, 256), F32),
+                pltpu.SemaphoreType.DMA((8,)),
+                pltpu.SemaphoreType.DMA((4, 2)),
+            ],
+        ),
+        out_shape=[ONE, ONE, TWO, FOUR],
+        compiler_params=pltpu.CompilerParams(vmem_limit_bytes=VMEM_LIMIT),
+        cost_estimate=pl.CostEstimate(
+            flops=3 * 2 * 2048 * 1024 * 512, bytes_accessed=20 << 20, transcendentals=0
+        ),
+        name="still_product",
+    )(where, *pieces, *crossed, yh, yl)
 
 
 def fill_kernel(out_rows, choose, count, where, *refs):
@@ -366,7 +427,7 @@
 
 
 def second_hop(r, c, l):
-    return (r ^ 4, c, l) if l == 1 else (r, c, l)
+    return (r ^ 4, c, l) if l == 1 else None
 
 
 def row_up(r, c, l):
@@ -448,21 +509,22 @@
     crossed[6], crossed[7] = in_chip(far), in_chip(partner_far)
     pieces = [start, partner, up, partner_up, down, partner_down, far, partner_far]
     crossed = [crossed[i] for i in range(8)]
-    d_down, d_up, w_down, w_up, beside = late_product(
-        True, where, pieces, crossed, y, own, other
+    yh, yl, d_down, d_up, straight, across = moving_product(
+        where, pieces, crossed, y, own, other
     )
     got_up = send(d_up, row_up)
     got_down = send(d_down, row_down)
-    from_beside = in_chip(beside)
-    straight, across, still, still_beside = late_product(
-        False, where, pieces, crossed, y, own, other
-    )
-    got_up, got_down, straight, across = barrier((got_up, got_down, straight, across))
-    edge_up = jnp.stack([w_up, from_beside[1]])
-    edge_down = jnp.stack([w_down, from_beside[0]])
     got_straight = send(straight, ring_straight)
     got_across = send(across, ring_across)
-    edge_up, edge_down, got_up, got_down = barrier((edge_up, edge_down, got_up, got_down))
+    across_beside = in_chip(across)
+    w_down, w_up, still, beside = still_product(where, pieces, crossed, yh, yl)
+    got_up, got_down, got_straight, got_across, across_beside, w_down, w_up, still, beside = barrier(
+        (got_up, got_down, got_straight, got_across, across_beside, w_down, w_up, still, beside)
+    )
+    changed = send(jnp.where((col_pos == 0) == lower, got_across, got_straight), ring_change)
+    from_still = in_chip(beside)
+    edge_up = jnp.stack([w_up, from_still[3]])
+    edge_down = jnp.stack([w_down, from_still[2]])
     still_got_up = send(edge_up, row_up)
     still_got_down = send(edge_down, row_down)
 
@@ -473,12 +535,7 @@
     then_across = jnp.stack([jnp.where(inside, x[1], x[0]) for x in (top, bottom)])
     then_got_straight = send(then_straight, column_straight)
     then_got_across = send(then_across, column_across)
-    from_still = in_chip(still_beside)
-    got_straight, got_across, then_straight = barrier((got_straight, got_across, then_straight))
-    changing = jnp.where((col_pos == 0) == lower, got_across, got_straight)
-    changed = send(changing, ring_change)
-
-    def blocks(w, own, partner, moving, moving_beside, came_straight, came_across, came_changed):
+    def blocks(w, own, partner, kept, kept_beside, came_straight, came_across, came_changed):
         c, l = w[1], w[2]
 
         def both(condition, if_lower, if_upper):
@@ -489,30 +546,30 @@
             ]
 
         yes = c >= 0
-        far_up = c == (4 if came_changed is not None else -1)
-        far_down = c == (3 if came_changed is not None else -1)
-        first = both((c > 0) & ~far_up, [(yes, came_across)], [(yes, came_straight)])
-        last = both((c < 7) & ~far_down, [(yes, came_straight)], [(yes, came_across)])
-        if came_changed is not None:
-            first.append((far_up, came_changed))
-            last.append((far_down, came_changed))
+        kept, kept_beside = [(yes, kept)], [(yes, kept_beside)]
+        straight, across = [(yes, came_straight)], [(yes, came_across)]
+        if came_changed is None:
+            first, last = both(c > 0, across, straight), both(c < 7, straight, across)
+        else:
+            first = both((c > 0) & (c != 4), across, straight) + [(c == 4, came_changed)]
+            last = both((c < 7) & (c != 3), straight, across) + [(c == 3, came_changed)]
         return [
             first + both(c == 0, own, partner),
             both(yes, partner, own),
-            both(c > 0, own, partner) + both(c == 0, [(yes, moving)], [(yes, moving_beside)]),
-            last + both(c == 7, [(yes, moving_beside)], [(yes, moving)]),
+            both(c > 0, own, partner) + both(c == 0, kept, kept_beside),
+            last + both(c == 7, kept_beside, kept),
         ]
 
     def choose_stay(w, refs):
-        still, beside, straight, came_straight, came_across, came_changed = refs
+        still, beside, kept, kept_beside, came_straight, came_across, came_changed = refs
         yes = w[1] >= 0
         return [
             blocks(
                 w,
                 [(yes, still.at[k])],
                 [(yes, beside.at[k])],
-                straight.at[k],
-                beside.at[2 + k],
+                kept.at[k],
+                kept_beside.at[k],
                 came_straight.at[k],
                 came_across.at[k],
                 came_changed.at[k],
@@ -524,7 +581,7 @@
         (1, 2),
         choose_stay,
         where,
-        [still, from_still, straight, got_straight, got_across, changed],
+        [still, from_still, straight, across_beside, got_straight, got_across, changed],
         None,
     )
 

time: 240 us -> 220 us (0.917)
  the two profiles are of different devices: /device:TPU:0 before, /device:TPU:6 now
where the time goes in v3:
time: 220 us; the launch traced here: 219 us
  waiting for transfers between devices  74.3 us (34%)
  starting transfers between devices  61.1 us (28%)
  Pallas kernels  59.7 us (27%)
  local copies, waits for them, and re-layouts  17.2 us (8%)
  other arithmetic  6.14 us (3%)
    ppermute x18, waiting for transfers between devices, send(): return lax.ppermute(x, AXES, route(place))  65.7 us
    ppermute x18, starting transfers between devices, send(): return lax.ppermute(x, AXES, route(place))  45.3 us
    pallas_call x1, Pallas kernels, moving_product(): pl.pallas_call(moving_kernel, grid_spec=pltpu.PrefetchScalarGridSpec(num_...  24.3 us
    ppermute x13, starting transfers between devices, in_chip(): return lax.ppermute(x, 'layer', [(0, 1), (1, 0)])  15.8 us
    pallas_call x1, Pallas kernels, early_product(): pl.pallas_call(early_kernel, grid_spec=pltpu.PrefetchScalarGridSpec(num_s...  14.2 us
    pallas_call x1, Pallas kernels, still_product(): pl.pallas_call(still_kernel, grid_spec=pltpu.PrefetchScalarGridSpec(num_s...  12.4 us
    pallas_call x2, Pallas kernels, fill_rows(): pl.pallas_call(kernel, grid_spec=pltpu.PrefetchScalarGridSpec(num_scalar_...  8.9 us
    ppermute x13, waiting for transfers between devices, in_chip(): return lax.ppermute(x, 'layer', [(0, 1), (1, 0)])  8.64 us
  transfers between devices with their start and end apart: 31, of which 14 were waited for; matrix products, arithmetic and copies ran while one was open for 6% of the time, Pallas kernels for 14%

profile of v3, /device:TPU:6, one launch (start us, length us, event | category | flops | bytes accessed | tf_op | source)
XLA Modules:
  0.0 219.0 jit_solution(1321179637315508737)
XLA Ops:
  0.0 2.7 %collective-permute-start = (f32[2,64,1024]{2,1,0:T(8,128)}, f32[2,64,1024]{2,1,0:T(8,128)S(1)}, u32[]{:S(2)}, u32[]{:S(2)}) collective-permute-start(f32[2,64,1024]{2,1,0:T(8,128)} %bitcast.30), channel_id=1, source_target_pairs={{0,8},{1,1},{2,10},{3,17},{4,12},{5,33},{6,14},{7,49},{8,0},{9,65}... | collective-permute-start | bytes 1572872 | tf_op jit(solution)/shard_map/ppermute | solution.py:29
  4.1 12.4 %collective-permute-done = f32[2,64,1024]{2,1,0:T(8,128)S(1)} collective-permute-done((f32[2,64,1024]{2,1,0:T(8,128)}, f32[2,64,1024]{2,1,0:T(8,128)S(1)}, u32[]{:S(2)}, u32[]{:S(2)}) %collective-permute-start) | collective-permute-done | bytes 524320 | tf_op jit(solution)/shard_map/ppermute | solution.py:29
  19.5 10.6 %collective-permute-start.3 = (f32[2,2,64,1024]{3,2,1,0:T(8,128)S(1)}, f32[2,2,64,1024]{3,2,1,0:T(8,128)S(1)}, u32[]{:S(2)}, u32[]{:S(2)}) collective-permute-start(f32[2,2,64,1024]{3,2,1,0:T(8,128)S(1)} %get-tuple-element.48.refs_0_), channel_id=1, source_target_pairs={{0,2},{1,17},{2,4},{3,19},{4,6},{5,21},{6,0},{7,23},{8,10},{9,25},... | collective-permute-start | bytes 3145736 | tf_op jit(solution)/shard_map/ppermute | solution.py:29
  30.1 3.9 %collective-permute-start.4 = (f32[2,2,64,1024]{3,2,1,0:T(8,128)S(1)}, f32[2,2,64,1024]{3,2,1,0:T(8,128)S(1)}, u32[]{:S(2)}, u32[]{:S(2)}) collective-permute-start(f32[2,2,64,1024]{3,2,1,0:T(8,128)S(1)} %get-tuple-element.48.refs_0_), channel_id=1, source_target_pairs={{0,6},{1,49},{2,0},{3,51},{4,2},{5,53},{6,4},{7,55},{8,14},{9,57},... | collective-permute-start | bytes 3145736 | tf_op jit(solution)/shard_map/ppermute | solution.py:29
  35.7 8.4 %copy.4 = f32[4,4,512,256]{3,2,1,0:T(8,128)} copy(f32[4,4,512,256]{3,0,2,1:T(4,128)} %bitcast.29) | data formatting | bytes 16777216 | tf_op jit(solution)/shard_map/transpose | solution.py:480
  52.1 6.2 %collective-permute-start.9 = (f32[2,2,64,1024]{3,2,1,0:T(8,128)S(1)}, f32[2,2,64,1024]{3,2,1,0:T(8,128)S(1)}, u32[]{:S(2)}, u32[]{:S(2)}) collective-permute-start(f32[2,2,64,1024]{3,2,1,0:T(8,128)S(1)} %broadcast_select_fusion.3.refs_1_), channel_id=1, source_target_pairs={{0,1},{1,0},{2,3},{3,2},{4,5},{5,4},{6,7},{7,6},{8,9},{9,8},{10,11... | collective-permute-start | bytes 3145736 | tf_op jit(solution)/shard_map/ppermute | solution.py:33
  58.3 3.8 %dynamic-slice_bitcast_fusion = (f32[2048,256]{1,0:T(8,128)}, f32[2048,256]{1,0:T(8,128)S(1)}) fusion(f32[4,2048,256]{2,1,0:T(8,128)} %bitcast.20, s32[]{:T(128)S(6)} %add.6, s32[]{:T(128)S(6)} %select_n.91), kind=kLoop, calls=%fused_computation | loop fusion | bytes 8388616 | tf_op jit(solution)/shard_map/squeeze | solution.py:482
  65.0 5.6 %collective-permute-start.10 = (f32[2,2,64,1024]{3,2,1,0:T(8,128)}, f32[2,2,64,1024]{3,2,1,0:T(8,128)S(1)}, u32[]{:S(2)}, u32[]{:S(2)}) collective-permute-start(f32[2,2,64,1024]{3,2,1,0:T(8,128)} %copy-done.3), channel_id=1, source_target_pairs={{0,1},{1,0},{2,3},{3,2},{4,5},{5,4},{6,7},{7,6},{8,9},{9,8},{10,11... | collective-permute-start | bytes 3145736 | tf_op jit(solution)/shard_map/ppermute | solution.py:33
  73.1 3.0 %collective-permute-done.11.refs_7_.refs_12_ = f32[2,2,64,1024]{3,2,1,0:T(8,128)S(1)} collective-permute-done((f32[2,2,64,1024]{3,2,1,0:T(8,128)}, f32[2,2,64,1024]{3,2,1,0:T(8,128)S(1)}, u32[]{:S(2)}, u32[]{:S(2)}) %collective-permute-start.11) | collective-permute-done | bytes 1048608 | tf_op jit(solution)/shard_map/ppermute | solution.py:33
  76.1 3.2 %collective-permute-start.13 = (f32[2,2,64,1024]{3,2,1,0:T(8,128)}, f32[2,2,64,1024]{3,2,1,0:T(8,128)}, u32[]{:S(2)}, u32[]{:S(2)}) collective-permute-start(f32[2,2,64,1024]{3,2,1,0:T(8,128)} %collective-permute-done.7.refs_5_), channel_id=1, source_target_pairs={{0,6},{1,49},{2,0},{3,51},{4,2},{5,53},{6,4},{7,55},{8,14},{9,57},... | collective-permute-start | bytes 3145736 | tf_op jit(solution)/shard_map/ppermute | solution.py:29
  80.7 14.2 %early_product.1.refs_16_ = f32[2048,1024]{1,0:T(8,128)} custom-call(s32[3]{0:T(128)} %pad_add_fusion.where, f32[2,2,64,1024]{3,2,1,0:T(8,128)} %copy-done.1, f32[2,2,64,1024]{3,2,1,0:T(8,128)} %copy-done.2, f32[2,2,64,1024]{3,2,1,0:T(8,128)} %copy-done.3, f32[2,2,64,1024]{3,2,1,0:T(8,128)} %copy-done.4, f32[2,2,64,1024]{3,2,1,0:T(8,128)} %copy-done.8, ...), custom_call_target="tpu_custom_call" | custom-call | flops 6442450944 | bytes 25165824 | tf_op jit(solution)/shard_map/early_product/pallas_call | solution.py:116
  100.6 24.3 %moving_product.1 = (bf16[2048,1024]{1,0:T(8,128)(2,1)}, bf16[2048,1024]{1,0:T(8,128)(2,1)}, f32[2,512,256]{2,1,0:T(8,128)}, f32[2,512,256]{2,1,0:T(8,128)}, f32...) custom-call(s32[3]{0:T(128)} %pad_add_fusion.where, f32[2,2,64,1024]{3,2,1,0:T(8,128)} %copy-done.1, ...), custom_call_target="tpu_custom_call" | custom-call | flops 12884901888 | bytes 37748736 | tf_op jit(solution)/shard_map/moving_product/pallas_call | solution.py:297
  124.9 5.6 %collective-permute-start.21 = (f32[2,512,256]{2,1,0:T(8,128)}, f32[2,512,256]{2,1,0:T(8,128)S(1)}, u32[]{:S(2)}, u32[]{:S(2)}) collective-permute-start(f32[2,512,256]{2,1,0:T(8,128)} %get-tuple-element.65), channel_id=1, source_target_pairs={{0,112},{1,113},{2,114},{3,115},{4,116},{5,117},{6,118},{7,119},{8... | collective-permute-start | bytes 3145736 | tf_op jit(solution)/shard_map/ppermute | solution.py:29
  132.9 12.4 %still_product.1 = (f32[512,256]{1,0:T(8,128)}, f32[512,256]{1,0:T(8,128)}, f32[2,512,256]{2,1,0:T(8,128)}, f32[4,512,256]{2,1,0:T(8,128)}) custom-call(s32[3]{0:T(128)} %pad_add_fusion.where, f32[2,2,64,1024]{3,2,1,0:T(8,128)} %copy-done.1, f32[2,2,64,1024]{3,2,1,0:T(8,128)} %copy-done.2, f32[2,2,64,1024]{3,2,1,0:T(8,128)} %copy-done.3, ...), custom_call_target="tpu_custom_call" | custom-call | flops 6442450944 | bytes 20971520 | tf_op jit(solution)/shard_map/still_product/pallas_call | solution.py:330
  145.3 8.9 %collective-permute-done.20 = f32[2,512,256]{2,1,0:T(8,128)S(1)} collective-permute-done((f32[2,512,256]{2,1,0:T(8,128)}, f32[2,512,256]{2,1,0:T(8,128)S(1)}, u32[]{:S(2)}, u32[]{:S(2)}) %collective-permute-start.20) | collective-permute-done | bytes 1048608 | tf_op jit(solution)/shard_map/ppermute | solution.py:29
  160.8 3.7 %collective-permute-start.28 = (f32[2,512,256]{2,1,0:T(8,128)S(1)}, f32[2,512,256]{2,1,0:T(8,128)}, u32[]{:S(2)}, u32[]{:S(2)}) collective-permute-start(f32[2,512,256]{2,1,0:T(8,128)S(1)} %pad_maximum_fusion.4), channel_id=1, source_target_pairs={{0,1},{1,3},{2,0},{3,5},{4,2},{5,7},{6,4},{7,9},{8,6},{9,11},{10,8... | collective-permute-start | bytes 3145736 | tf_op jit(solution)/shard_map/ppermute | solution.py:29
  164.6 3.3 %collective-permute-start.29 = (f32[2,512,256]{2,1,0:T(8,128)S(1)}, f32[2,512,256]{2,1,0:T(8,128)}, u32[]{:S(2)}, u32[]{:S(2)}) collective-permute-start(f32[2,512,256]{2,1,0:T(8,128)S(1)} %pad_maximum_fusion.3.refs_4_), channel_id=1, source_target_pairs={{0,0},{1,2},{2,1},{3,4},{4,3},{5,6},{6,5},{7,8},{8,7},{9,10},{10,9... | collective-permute-start | bytes 3145736 | tf_op jit(solution)/shard_map/ppermute | solution.py:29
  169.3 3.0 %collective-permute-start.27 = (f32[2,512,256]{2,1,0:T(8,128)S(1)}, f32[2,512,256]{2,1,0:T(8,128)}, u32[]{:S(2)}, u32[]{:S(2)}) collective-permute-start(f32[2,512,256]{2,1,0:T(8,128)S(1)} %pad_maximum_fusion.2.refs_1_), channel_id=1, source_target_pairs={{0,112},{1,113},{2,114},{3,115},{4,116},{5,117},{6,118},{7,119},{8... | collective-permute-start | bytes 3145736 | tf_op jit(solution)/shard_map/ppermute | solution.py:29
  172.4 14.8 %collective-permute-done.30.refs_6_ = f32[2,512,256]{2,1,0:T(8,128)} collective-permute-done((f32[2,512,256]{2,1,0:T(8,128)S(1)}, f32[2,512,256]{2,1,0:T(8,128)}, u32[]{:S(2)}, u32[]{:S(2)}) %collective-permute-start.30) | collective-permute-done | bytes 1048608 | tf_op jit(solution)/shard_map/ppermute | solution.py:29
  187.3 4.5 %fill_rows.2.refs_7_ = f32[4,512,4,256]{3,2,1,0:T(4,128)} custom-call(s32[3]{0:T(128)} %pad_add_fusion.where, f32[2,512,256]{2,1,0:T(8,128)} %get-tuple-element.79.refs_0_, f32[4,512,256]{2,1,0:T(8,128)} %copy-done.9, f32[2,512,256]{2,1,0:T(8,128)} %get-tuple-element.66.refs_2_, f32[2,512,256]{2,1,0:T(8,128)} %copy-done.20, f32[2,512,256]{2,1,0:T(8,128)} %copy-done.15, ...), custom_call_target="tpu_custom_call" | custom-call | bytes 8388608 | tf_op jit(solution)/shard_map/fill_rows/pallas_call | solution.py:387
  191.8 9.1 %collective-permute-done.29.refs_6_ = f32[2,512,256]{2,1,0:T(8,128)} collective-permute-done((f32[2,512,256]{2,1,0:T(8,128)S(1)}, f32[2,512,256]{2,1,0:T(8,128)}, u32[]{:S(2)}, u32[]{:S(2)}) %collective-permute-start.29) | collective-permute-done | bytes 1048608 | tf_op jit(solution)/shard_map/ppermute | solution.py:29
  200.8 9.7 %collective-permute-done.27.refs_3_ = f32[2,512,256]{2,1,0:T(8,128)} collective-permute-done((f32[2,512,256]{2,1,0:T(8,128)S(1)}, f32[2,512,256]{2,1,0:T(8,128)}, u32[]{:S(2)}, u32[]{:S(2)}) %collective-permute-start.27) | collective-permute-done | bytes 1048608 | tf_op jit(solution)/shard_map/ppermute | solution.py:29
  210.5 2.9 %collective-permute-done.26.refs_2_ = f32[2,512,256]{2,1,0:T(8,128)S(1)} collective-permute-done((f32[2,512,256]{2,1,0:T(8,128)S(1)}, f32[2,512,256]{2,1,0:T(8,128)S(1)}, u32[]{:S(2)}, u32[]{:S(2)}) %collective-permute-start.26) | collective-permute-done | bytes 1048608 | tf_op jit(solution)/shard_map/ppermute | solution.py:29
  214.4 4.4 %fill_rows.3 = f32[4,512,4,256]{3,2,1,0:T(4,128)} custom-call(s32[3]{0:T(128)} %pad_add_fusion.where, f32[2,512,256]{2,1,0:T(8,128)} %copy-done.19, f32[2,512,256]{2,1,0:T(8,128)} %copy-done.18, f32[2,512,256]{2,1,0:T(8,128)} %copy-done.27, f32[2,512,256]{2,1,0:T(8,128)} %collective-permute-done.27.refs_3_, ...), custom_call_target="tpu_custom_call", output_to_operand_aliasing={{}: (8, {})} | custom-call | bytes 8388608 | tf_op jit(solution)/shard_map/fill_rows/pallas_call | solution.py:387
  (119 shorter events, 37.7 us)
Async XLA Ops:
  0.0 16.5 %collective-permute-start = (f32[2,64,1024]{2,1,0:T(8,128)}, f32[2,64,1024]{2,1,0:T(8,128)S(1)}, u32[]{:S(2)}, u32[]{:S(2)}) collective-permute-start(f32[2,64,1024]{2,1,0:T(8,128)} %bitcast.30), channel_id=1, source_target_pairs={{0,8},{1,1},{2,10},{3,17},{4,12},{5,33},{6,14},{7,49},{8,0},{9,65}... | collective-permute-start | bytes 1572872 | tf_op jit(solution)/shard_map/ppermute | solution.py:29
  2.7 14.2 %collective-permute-start.1 = (f32[2,64,1024]{2,1,0:T(8,128)}, f32[2,64,1024]{2,1,0:T(8,128)S(1)}, u32[]{:S(2)}, u32[]{:S(2)}) collective-permute-start(f32[2,64,1024]{2,1,0:T(8,128)} %bitcast.31), channel_id=1, source_target_pairs={{0,1},{1,8},{2,17},{3,10},{4,33},{5,12},{6,49},{7,14},{8,65},{9,0}... | collective-permute-start | bytes 1572872 | tf_op jit(solution)/shard_map/ppermute | solution.py:29
  2.8 14.1 %collective-permute-start.2 = (f32[2,64,1024]{2,1,0:T(8,128)}, f32[2,64,1024]{2,1,0:T(8,128)S(1)}, u32[]{:S(2)}, u32[]{:S(2)}) collective-permute-start(f32[2,64,1024]{2,1,0:T(8,128)} %bitcast.32), channel_id=1, source_target_pairs={{0,1},{1,0},{2,3},{3,2},{4,5},{5,4},{6,7},{7,6},{8,9},{9,8},{10,11... | collective-permute-start | bytes 1572872 | tf_op jit(solution)/shard_map/ppermute | solution.py:33
  19.5 27.2 %collective-permute-start.3 = (f32[2,2,64,1024]{3,2,1,0:T(8,128)S(1)}, f32[2,2,64,1024]{3,2,1,0:T(8,128)S(1)}, u32[]{:S(2)}, u32[]{:S(2)}) collective-permute-start(f32[2,2,64,1024]{3,2,1,0:T(8,128)S(1)} %get-tuple-element.48.refs_0_), channel_id=1, source_target_pairs={{0,2},{1,17},{2,4},{3,19},{4,6},{5,21},{6,0},{7,23},{8,10},{9,25},... | collective-permute-start | bytes 3145736 | tf_op jit(solution)/shard_map/ppermute | solution.py:29
  30.1 16.6 %collective-permute-start.4 = (f32[2,2,64,1024]{3,2,1,0:T(8,128)S(1)}, f32[2,2,64,1024]{3,2,1,0:T(8,128)S(1)}, u32[]{:S(2)}, u32[]{:S(2)}) collective-permute-start(f32[2,2,64,1024]{3,2,1,0:T(8,128)S(1)} %get-tuple-element.48.refs_0_), channel_id=1, source_target_pairs={{0,6},{1,49},{2,0},{3,51},{4,2},{5,53},{6,4},{7,55},{8,14},{9,57},... | collective-permute-start | bytes 3145736 | tf_op jit(solution)/shard_map/ppermute | solution.py:29
  48.8 16.2 %collective-permute-start.6 = (f32[2,2,64,1024]{3,2,1,0:T(8,128)S(1)}, f32[2,2,64,1024]{3,2,1,0:T(8,128)}, u32[]{:S(2)}, u32[]{:S(2)}) collective-permute-start(f32[2,2,64,1024]{3,2,1,0:T(8,128)S(1)} %broadcast_select_fusion.3.refs_1_), channel_id=1, source_target_pairs={{0,2},{1,17},{2,4},{3,19},{4,6},{5,21},{6,0},{7,23},{8,10},{9,25},... | collective-permute-start | bytes 3145736 | tf_op jit(solution)/shard_map/ppermute | solution.py:29
  49.9 20.7 %collective-permute-start.7 = (f32[2,2,64,1024]{3,2,1,0:T(8,128)S(1)}, f32[2,2,64,1024]{3,2,1,0:T(8,128)}, u32[]{:S(2)}, u32[]{:S(2)}) collective-permute-start(f32[2,2,64,1024]{3,2,1,0:T(8,128)S(1)} %broadcast_select_fusion.3.refs_1_), channel_id=1, source_target_pairs={{0,6},{1,49},{2,0},{3,51},{4,2},{5,53},{6,4},{7,55},{8,14},{9,57},... | collective-permute-start | bytes 3145736 | tf_op jit(solution)/shard_map/ppermute | solution.py:29
  52.1 18.5 %collective-permute-start.9 = (f32[2,2,64,1024]{3,2,1,0:T(8,128)S(1)}, f32[2,2,64,1024]{3,2,1,0:T(8,128)S(1)}, u32[]{:S(2)}, u32[]{:S(2)}) collective-permute-start(f32[2,2,64,1024]{3,2,1,0:T(8,128)S(1)} %broadcast_select_fusion.3.refs_1_), channel_id=1, source_target_pairs={{0,1},{1,0},{2,3},{3,2},{4,5},{5,4},{6,7},{7,6},{8,9},{9,8},{10,11... | collective-permute-start | bytes 3145736 | tf_op jit(solution)/shard_map/ppermute | solution.py:33
  62.2 17.2 %collective-permute-start.14 = (f32[2048,256]{1,0:T(8,128)S(1)}, f32[2048,256]{1,0:T(8,128)S(1)}, u32[]{:S(2)}, u32[]{:S(2)}) collective-permute-start(f32[2048,256]{1,0:T(8,128)S(1)} %get-tuple-element.84), channel_id=1, source_target_pairs={{0,1},{1,0},{2,3},{3,2},{4,5},{5,4},{6,7},{7,6},{8,9},{9,8},{10,11... | collective-permute-start | bytes 6291464 | tf_op jit(solution)/shard_map/ppermute | solution.py:33
  62.3 18.4 %collective-permute-start.15 = (f32[2048,256]{1,0:T(8,128)}, f32[2048,256]{1,0:T(8,128)}, u32[]{:S(2)}, u32[]{:S(2)}) collective-permute-start(f32[2048,256]{1,0:T(8,128)} %get-tuple-element.83), channel_id=1, source_target_pairs={{0,1},{1,0},{2,3},{3,2},{4,5},{5,4},{6,7},{7,6},{8,9},{9,8},{10,11... | collective-permute-start | bytes 6291464 | tf_op jit(solution)/shard_map/ppermute | solution.py:33
  76.1 18.8 %collective-permute-start.12 = (f32[2,2,64,1024]{3,2,1,0:T(8,128)}, f32[2,2,64,1024]{3,2,1,0:T(8,128)S(1)}, u32[]{:S(2)}, u32[]{:S(2)}) collective-permute-start(f32[2,2,64,1024]{3,2,1,0:T(8,128)} %copy-done.3), channel_id=1, source_target_pairs={{0,2},{1,17},{2,4},{3,19},{4,6},{5,21},{6,0},{7,23},{8,10},{9,25},... | collective-permute-start | bytes 3145736 | tf_op jit(solution)/shard_map/ppermute | solution.py:29
  76.1 18.8 %collective-permute-start.13 = (f32[2,2,64,1024]{3,2,1,0:T(8,128)}, f32[2,2,64,1024]{3,2,1,0:T(8,128)}, u32[]{:S(2)}, u32[]{:S(2)}) collective-permute-start(f32[2,2,64,1024]{3,2,1,0:T(8,128)} %collective-permute-done.7.refs_5_), channel_id=1, source_target_pairs={{0,6},{1,49},{2,0},{3,51},{4,2},{5,53},{6,4},{7,55},{8,14},{9,57},... | collective-permute-start | bytes 3145736 | tf_op jit(solution)/shard_map/ppermute | solution.py:29
  79.4 15.6 %collective-permute-start.16 = (f32[2,2,64,1024]{3,2,1,0:T(8,128)}, f32[2,2,64,1024]{3,2,1,0:T(8,128)}, u32[]{:S(2)}, u32[]{:S(2)}) collective-permute-start(f32[2,2,64,1024]{3,2,1,0:T(8,128)} %collective-permute-done.6.refs_3_), channel_id=1, source_target_pairs={{0,1},{1,0},{2,3},{3,2},{4,5},{5,4},{6,7},{7,6},{8,9},{9,8},{10,11... | collective-permute-start | bytes 3145736 | tf_op jit(solution)/shard_map/ppermute | solution.py:33
  79.4 15.6 %collective-permute-start.17 = (f32[2,2,64,1024]{3,2,1,0:T(8,128)}, f32[2,2,64,1024]{3,2,1,0:T(8,128)}, u32[]{:S(2)}, u32[]{:S(2)}) collective-permute-start(f32[2,2,64,1024]{3,2,1,0:T(8,128)} %collective-permute-done.7.refs_5_), channel_id=1, source_target_pairs={{0,1},{1,0},{2,3},{3,2},{4,5},{5,4},{6,7},{7,6},{8,9},{9,8},{10,11... | collective-permute-start | bytes 3145736 | tf_op jit(solution)/shard_map/ppermute | solution.py:33
  124.8 29.3 %collective-permute-start.20 = (f32[2,512,256]{2,1,0:T(8,128)}, f32[2,512,256]{2,1,0:T(8,128)S(1)}, u32[]{:S(2)}, u32[]{:S(2)}) collective-permute-start(f32[2,512,256]{2,1,0:T(8,128)} %get-tuple-element.64), channel_id=1, source_target_pairs={{0,16},{1,17},{2,18},{3,19},{4,20},{5,21},{6,22},{7,23},{8,24},{9,... | collective-permute-start | bytes 3145736 | tf_op jit(solution)/shard_map/ppermute | solution.py:29
  124.9 29.3 %collective-permute-start.21 = (f32[2,512,256]{2,1,0:T(8,128)}, f32[2,512,256]{2,1,0:T(8,128)S(1)}, u32[]{:S(2)}, u32[]{:S(2)}) collective-permute-start(f32[2,512,256]{2,1,0:T(8,128)} %get-tuple-element.65), channel_id=1, source_target_pairs={{0,112},{1,113},{2,114},{3,115},{4,116},{5,117},{6,118},{7,119},{8... | collective-permute-start | bytes 3145736 | tf_op jit(solution)/shard_map/ppermute | solution.py:29
  130.5 23.6 %collective-permute-start.22 = (f32[2,512,256]{2,1,0:T(8,128)}, f32[2,512,256]{2,1,0:T(8,128)S(1)}, u32[]{:S(2)}, u32[]{:S(2)}) collective-permute-start(f32[2,512,256]{2,1,0:T(8,128)} %get-tuple-element.66.refs_2_), channel_id=1, source_target_pairs={{0,6},{1,3},{2,0},{3,5},{4,2},{5,7},{6,4},{7,1},{8,14},{9,11},{10,... | collective-permute-start | bytes 3145736 | tf_op jit(solution)/shard_map/ppermute | solution.py:29
  132.1 24.7 %collective-permute-start.23 = (f32[2,512,256]{2,1,0:T(8,128)}, f32[2,512,256]{2,1,0:T(8,128)S(1)}, u32[]{:S(2)}, u32[]{:S(2)}) collective-permute-start(f32[2,512,256]{2,1,0:T(8,128)} %get-tuple-element.67), channel_id=1, source_target_pairs={{0,7},{1,2},{2,1},{3,4},{4,3},{5,6},{6,5},{7,0},{8,15},{9,10},{10,... | collective-permute-start | bytes 3145736 | tf_op jit(solution)/shard_map/ppermute | solution.py:29
  132.9 23.9 %collective-permute-start.24 = (f32[2,512,256]{2,1,0:T(8,128)}, f32[2,512,256]{2,1,0:T(8,128)S(1)}, u32[]{:S(2)}, u32[]{:S(2)}) collective-permute-start(f32[2,512,256]{2,1,0:T(8,128)} %get-tuple-element.67), channel_id=1, source_target_pairs={{0,1},{1,0},{2,3},{3,2},{4,5},{5,4},{6,7},{7,6},{8,9},{9,8},{10,11... | collective-permute-start | bytes 3145736 | tf_op jit(solution)/shard_map/ppermute | solution.py:33
  158.4 28.8 %collective-permute-start.30 = (f32[2,512,256]{2,1,0:T(8,128)S(1)}, f32[2,512,256]{2,1,0:T(8,128)}, u32[]{:S(2)}, u32[]{:S(2)}) collective-permute-start(f32[2,512,256]{2,1,0:T(8,128)S(1)} %broadcast_select_fusion), channel_id=1, source_target_pairs={{0,8},{1,9},{14,6},{15,7},{16,24},{17,25},{30,22},{31,23},{32,40},... | collective-permute-start | bytes 3145736 | tf_op jit(solution)/shard_map/ppermute | solution.py:29
  160.8 31.0 %collective-permute-start.28 = (f32[2,512,256]{2,1,0:T(8,128)S(1)}, f32[2,512,256]{2,1,0:T(8,128)}, u32[]{:S(2)}, u32[]{:S(2)}) collective-permute-start(f32[2,512,256]{2,1,0:T(8,128)S(1)} %pad_maximum_fusion.4), channel_id=1, source_target_pairs={{0,1},{1,3},{2,0},{3,5},{4,2},{5,7},{6,4},{7,9},{8,6},{9,11},{10,8... | collective-permute-start | bytes 3145736 | tf_op jit(solution)/shard_map/ppermute | solution.py:29
  164.6 36.2 %collective-permute-start.29 = (f32[2,512,256]{2,1,0:T(8,128)S(1)}, f32[2,512,256]{2,1,0:T(8,128)}, u32[]{:S(2)}, u32[]{:S(2)}) collective-permute-start(f32[2,512,256]{2,1,0:T(8,128)S(1)} %pad_maximum_fusion.3.refs_4_), channel_id=1, source_target_pairs={{0,0},{1,2},{2,1},{3,4},{4,3},{5,6},{6,5},{7,8},{8,7},{9,10},{10,9... | collective-permute-start | bytes 3145736 | tf_op jit(solution)/shard_map/ppermute | solution.py:29
  169.3 41.3 %collective-permute-start.27 = (f32[2,512,256]{2,1,0:T(8,128)S(1)}, f32[2,512,256]{2,1,0:T(8,128)}, u32[]{:S(2)}, u32[]{:S(2)}) collective-permute-start(f32[2,512,256]{2,1,0:T(8,128)S(1)} %pad_maximum_fusion.2.refs_1_), channel_id=1, source_target_pairs={{0,112},{1,113},{2,114},{3,115},{4,116},{5,117},{6,118},{7,119},{8... | collective-permute-start | bytes 3145736 | tf_op jit(solution)/shard_map/ppermute | solution.py:29
  172.4 41.1 %collective-permute-start.26 = (f32[2,512,256]{2,1,0:T(8,128)S(1)}, f32[2,512,256]{2,1,0:T(8,128)S(1)}, u32[]{:S(2)}, u32[]{:S(2)}) collective-permute-start(f32[2,512,256]{2,1,0:T(8,128)S(1)} %pad_maximum_fusion.1.refs_0_), channel_id=1, source_target_pairs={{0,16},{1,17},{2,18},{3,19},{4,20},{5,21},{6,22},{7,23},{8,24},{9,... | collective-permute-start | bytes 3145736 | tf_op jit(solution)/shard_map/ppermute | solution.py:29
  (37 other events, 256.6 us)

commit v4 on v3

--- a/solution.py
+++ b/solution.py
@@ -518,11 +518,11 @@
     got_across = send(across, ring_across)
     across_beside = in_chip(across)
     w_down, w_up, still, beside = still_product(where, pieces, crossed, yh, yl)
-    got_up, got_down, got_straight, got_across, across_beside, w_down, w_up, still, beside = barrier(
-        (got_up, got_down, got_straight, got_across, across_beside, w_down, w_up, still, beside)
+    from_still = in_chip(beside)
+    got_up, got_down, got_straight, got_across, across_beside, w_down, w_up, still = barrier(
+        (got_up, got_down, got_straight, got_across, across_beside, w_down, w_up, still)
     )
     changed = send(jnp.where((col_pos == 0) == lower, got_across, got_straight), ring_change)
-    from_still = in_chip(beside)
     edge_up = jnp.stack([w_up, from_still[3]])
     edge_down = jnp.stack([w_down, from_still[2]])
     still_got_up = send(edge_up, row_up)
@@ -584,6 +584,8 @@
         [still, from_still, straight, across_beside, got_straight, got_across, changed],
         None,
     )
+
+    out, still_got_up, still_got_down = barrier((out, still_got_up, still_got_down))
 
     def choose_moved(w, refs):
         edge_up, edge_down, from_up, from_down, kept, came_straight, came_across = refs

time: 220 us -> 222 us (level)
  the two profiles are of different devices: /device:TPU:6 before, /device:TPU:0 now
where the time goes in v4:
time: 222 us; the launch traced here: 221 us
  waiting for transfers between devices  68.3 us (31%)
  starting transfers between devices  64.9 us (29%)
  Pallas kernels  59.8 us (27%)
  local copies, waits for them, and re-layouts  17.8 us (8%)
  other arithmetic  9.9 us (4%)
    ppermute x18, waiting for transfers between devices, send(): return lax.ppermute(x, AXES, route(place))  59.7 us
    ppermute x18, starting transfers between devices, send(): return lax.ppermute(x, AXES, route(place))  48.5 us
    pallas_call x1, Pallas kernels, moving_product(): pl.pallas_call(moving_kernel, grid_spec=pltpu.PrefetchScalarGridSpec(num_...  24.3 us
    ppermute x13, starting transfers between devices, in_chip(): return lax.ppermute(x, 'layer', [(0, 1), (1, 0)])  16.3 us
    pallas_call x1, Pallas kernels, early_product(): pl.pallas_call(early_kernel, grid_spec=pltpu.PrefetchScalarGridSpec(num_s...  14.2 us
    pallas_call x1, Pallas kernels, still_product(): pl.pallas_call(still_kernel, grid_spec=pltpu.PrefetchScalarGridSpec(num_s...  12.4 us
    pallas_call x2, Pallas kernels, fill_rows(): pl.pallas_call(kernel, grid_spec=pltpu.PrefetchScalarGridSpec(num_scalar_...  8.9 us
    ppermute x13, waiting for transfers between devices, in_chip(): return lax.ppermute(x, 'layer', [(0, 1), (1, 0)])  8.64 us
  transfers between devices with their start and end apart: 31, of which 12 were waited for; matrix products, arithmetic and copies ran while one was open for 8% of the time, Pallas kernels for 14%

profile of v4, /device:TPU:0, one launch (start us, length us, event | category | flops | bytes accessed | tf_op | source)
XLA Modules:
  0.0 221.2 jit_solution(4559718549462292237)
XLA Ops:
  0.0 3.5 %collective-permute-start = (f32[2,64,1024]{2,1,0:T(8,128)}, f32[2,64,1024]{2,1,0:T(8,128)S(1)}, u32[]{:S(2)}, u32[]{:S(2)}) collective-permute-start(f32[2,64,1024]{2,1,0:T(8,128)} %bitcast.30), channel_id=1, source_target_pairs={{0,8},{1,1},{2,10},{3,17},{4,12},{5,33},{6,14},{7,49},{8,0},{9,65}... | collective-permute-start | bytes 1572872 | tf_op jit(solution)/shard_map/ppermute | solution.py:29
  4.1 11.9 %collective-permute-done = f32[2,64,1024]{2,1,0:T(8,128)S(1)} collective-permute-done((f32[2,64,1024]{2,1,0:T(8,128)}, f32[2,64,1024]{2,1,0:T(8,128)S(1)}, u32[]{:S(2)}, u32[]{:S(2)}) %collective-permute-start) | collective-permute-done | bytes 524320 | tf_op jit(solution)/shard_map/ppermute | solution.py:29
  19.5 10.7 %collective-permute-start.3 = (f32[2,2,64,1024]{3,2,1,0:T(8,128)S(1)}, f32[2,2,64,1024]{3,2,1,0:T(8,128)S(1)}, u32[]{:S(2)}, u32[]{:S(2)}) collective-permute-start(f32[2,2,64,1024]{3,2,1,0:T(8,128)S(1)} %get-tuple-element.50.refs_0_), channel_id=1, source_target_pairs={{0,2},{1,17},{2,4},{3,19},{4,6},{5,21},{6,0},{7,23},{8,10},{9,25},... | collective-permute-start | bytes 3145736 | tf_op jit(solution)/shard_map/ppermute | solution.py:29
  30.2 3.9 %collective-permute-start.4 = (f32[2,2,64,1024]{3,2,1,0:T(8,128)S(1)}, f32[2,2,64,1024]{3,2,1,0:T(8,128)S(1)}, u32[]{:S(2)}, u32[]{:S(2)}) collective-permute-start(f32[2,2,64,1024]{3,2,1,0:T(8,128)S(1)} %get-tuple-element.50.refs_0_), channel_id=1, source_target_pairs={{0,6},{1,49},{2,0},{3,51},{4,2},{5,53},{6,4},{7,55},{8,14},{9,57},... | collective-permute-start | bytes 3145736 | tf_op jit(solution)/shard_map/ppermute | solution.py:29
  35.8 8.4 %copy.4 = f32[4,4,512,256]{3,2,1,0:T(8,128)} copy(f32[4,4,512,256]{3,0,2,1:T(4,128)} %bitcast.29) | data formatting | bytes 16777216 | tf_op jit(solution)/shard_map/transpose | solution.py:480
  44.2 2.6 %collective-permute-done.3.refs_2_ = f32[2,2,64,1024]{3,2,1,0:T(8,128)S(1)} collective-permute-done((f32[2,2,64,1024]{3,2,1,0:T(8,128)S(1)}, f32[2,2,64,1024]{3,2,1,0:T(8,128)S(1)}, u32[]{:S(2)}, u32[]{:S(2)}) %collective-permute-start.3) | collective-permute-done | bytes 1048608 | tf_op jit(solution)/shard_map/ppermute | solution.py:29
  52.2 6.9 %collective-permute-start.9 = (f32[2,2,64,1024]{3,2,1,0:T(8,128)S(1)}, f32[2,2,64,1024]{3,2,1,0:T(8,128)S(1)}, u32[]{:S(2)}, u32[]{:S(2)}) collective-permute-start(f32[2,2,64,1024]{3,2,1,0:T(8,128)S(1)} %broadcast_select_fusion.3.refs_1_), channel_id=1, source_target_pairs={{0,1},{1,0},{2,3},{3,2},{4,5},{5,4},{6,7},{7,6},{8,9},{9,8},{10,11... | collective-permute-start | bytes 3145736 | tf_op jit(solution)/shard_map/ppermute | solution.py:33
  59.1 3.8 %dynamic-slice_bitcast_fusion = (f32[2048,256]{1,0:T(8,128)}, f32[2048,256]{1,0:T(8,128)S(1)}) fusion(f32[4,2048,256]{2,1,0:T(8,128)} %bitcast.20, s32[]{:T(128)S(6)} %add.6, s32[]{:T(128)S(6)} %select_n.91), kind=kLoop, calls=%fused_computation | loop fusion | bytes 8388616 | tf_op jit(solution)/shard_map/squeeze | solution.py:482
  65.1 6.3 %collective-permute-start.10 = (f32[2,2,64,1024]{3,2,1,0:T(8,128)}, f32[2,2,64,1024]{3,2,1,0:T(8,128)S(1)}, u32[]{:S(2)}, u32[]{:S(2)}) collective-permute-start(f32[2,2,64,1024]{3,2,1,0:T(8,128)} %copy-done.3), channel_id=1, source_target_pairs={{0,1},{1,0},{2,3},{3,2},{4,5},{5,4},{6,7},{7,6},{8,9},{9,8},{10,11... | collective-permute-start | bytes 3145736 | tf_op jit(solution)/shard_map/ppermute | solution.py:33
  73.9 3.0 %collective-permute-done.11.refs_7_.refs_12_ = f32[2,2,64,1024]{3,2,1,0:T(8,128)S(1)} collective-permute-done((f32[2,2,64,1024]{3,2,1,0:T(8,128)}, f32[2,2,64,1024]{3,2,1,0:T(8,128)S(1)}, u32[]{:S(2)}, u32[]{:S(2)}) %collective-permute-start.11) | collective-permute-done | bytes 1048608 | tf_op jit(solution)/shard_map/ppermute | solution.py:33
  76.9 3.2 %collective-permute-start.13 = (f32[2,2,64,1024]{3,2,1,0:T(8,128)}, f32[2,2,64,1024]{3,2,1,0:T(8,128)}, u32[]{:S(2)}, u32[]{:S(2)}) collective-permute-start(f32[2,2,64,1024]{3,2,1,0:T(8,128)} %collective-permute-done.7.refs_5_), channel_id=1, source_target_pairs={{0,6},{1,49},{2,0},{3,51},{4,2},{5,53},{6,4},{7,55},{8,14},{9,57},... | collective-permute-start | bytes 3145736 | tf_op jit(solution)/shard_map/ppermute | solution.py:29
  81.5 14.2 %early_product.1.refs_16_ = f32[2048,1024]{1,0:T(8,128)} custom-call(s32[3]{0:T(128)} %pad_add_fusion.where, f32[2,2,64,1024]{3,2,1,0:T(8,128)} %copy-done.1, f32[2,2,64,1024]{3,2,1,0:T(8,128)} %copy-done.2, f32[2,2,64,1024]{3,2,1,0:T(8,128)} %copy-done.3, f32[2,2,64,1024]{3,2,1,0:T(8,128)} %copy-done.4, f32[2,2,64,1024]{3,2,1,0:T(8,128)} %copy-done.8, ...), custom_call_target="tpu_custom_call" | custom-call | flops 6442450944 | bytes 25165824 | tf_op jit(solution)/shard_map/early_product/pallas_call | solution.py:116
  101.4 24.3 %moving_product.1 = (bf16[2048,1024]{1,0:T(8,128)(2,1)}, bf16[2048,1024]{1,0:T(8,128)(2,1)}, f32[2,512,256]{2,1,0:T(8,128)}, f32[2,512,256]{2,1,0:T(8,128)}, f32...) custom-call(s32[3]{0:T(128)} %pad_add_fusion.where, f32[2,2,64,1024]{3,2,1,0:T(8,128)} %copy-done.1, ...), custom_call_target="tpu_custom_call" | custom-call | flops 12884901888 | bytes 37748736 | tf_op jit(solution)/shard_map/moving_product/pallas_call | solution.py:297
  127.2 5.3 %collective-permute-start.21 = (f32[2,512,256]{2,1,0:T(8,128)}, f32[2,512,256]{2,1,0:T(8,128)}, u32[]{:S(2)}, u32[]{:S(2)}) collective-permute-start(f32[2,512,256]{2,1,0:T(8,128)} %get-tuple-element.67), channel_id=1, source_target_pairs={{0,112},{1,113},{2,114},{3,115},{4,116},{5,117},{6,118},{7,119},{8... | collective-permute-start | bytes 3145736 | tf_op jit(solution)/shard_map/ppermute | solution.py:29
  132.4 2.3 %collective-permute-start.22 = (f32[2,512,256]{2,1,0:T(8,128)}, f32[2,512,256]{2,1,0:T(8,128)}, u32[]{:S(2)}, u32[]{:S(2)}) collective-permute-start(f32[2,512,256]{2,1,0:T(8,128)} %get-tuple-element.68.refs_2_), channel_id=1, source_target_pairs={{0,6},{1,3},{2,0},{3,5},{4,2},{5,7},{6,4},{7,1},{8,14},{9,11},{10,... | collective-permute-start | bytes 3145736 | tf_op jit(solution)/shard_map/ppermute | solution.py:29
  134.8 12.4 %still_product.1 = (f32[512,256]{1,0:T(8,128)}, f32[512,256]{1,0:T(8,128)}, f32[2,512,256]{2,1,0:T(8,128)}, f32[4,512,256]{2,1,0:T(8,128)}) custom-call(s32[3]{0:T(128)} %pad_add_fusion.where, f32[2,2,64,1024]{3,2,1,0:T(8,128)} %copy-done.1, f32[2,2,64,1024]{3,2,1,0:T(8,128)} %copy-done.2, f32[2,2,64,1024]{3,2,1,0:T(8,128)} %copy-done.3, ...), custom_call_target="tpu_custom_call" | custom-call | flops 6442450944 | bytes 20971520 | tf_op jit(solution)/shard_map/still_product/pallas_call | solution.py:330
  147.1 7.9 %collective-permute-done.20 = f32[2,512,256]{2,1,0:T(8,128)S(1)} collective-permute-done((f32[2,512,256]{2,1,0:T(8,128)}, f32[2,512,256]{2,1,0:T(8,128)S(1)}, u32[]{:S(2)}, u32[]{:S(2)}) %collective-permute-start.20) | collective-permute-done | bytes 1048608 | tf_op jit(solution)/shard_map/ppermute | solution.py:29
  161.1 5.9 %collective-permute-start.26 = (f32[2,512,256]{2,1,0:T(8,128)S(1)}, f32[2,512,256]{2,1,0:T(8,128)S(1)}, u32[]{:S(2)}, u32[]{:S(2)}) collective-permute-start(f32[2,512,256]{2,1,0:T(8,128)S(1)} %broadcast_select_fusion.2), channel_id=1, source_target_pairs={{0,8},{1,9},{14,6},{15,7},{16,24},{17,25},{30,22},{31,23},{32,40},... | collective-permute-start | bytes 3145736 | tf_op jit(solution)/shard_map/ppermute | solution.py:29
  168.4 4.9 %collective-permute-start.28 = (f32[2,512,256]{2,1,0:T(8,128)S(1)}, f32[2,512,256]{2,1,0:T(8,128)}, u32[]{:S(2)}, u32[]{:S(2)}) collective-permute-start(f32[2,512,256]{2,1,0:T(8,128)S(1)} %pad_maximum_fusion.2.refs_1_), channel_id=1, source_target_pairs={{0,112},{1,113},{2,114},{3,115},{4,116},{5,117},{6,118},{7,119},{8... | collective-permute-start | bytes 3145736 | tf_op jit(solution)/shard_map/ppermute | solution.py:29
  175.3 15.3 %collective-permute-done.26.refs_6_ = f32[2,512,256]{2,1,0:T(8,128)S(1)} collective-permute-done((f32[2,512,256]{2,1,0:T(8,128)S(1)}, f32[2,512,256]{2,1,0:T(8,128)S(1)}, u32[]{:S(2)}, u32[]{:S(2)}) %collective-permute-start.26) | collective-permute-done | bytes 1048608 | tf_op jit(solution)/shard_map/ppermute | solution.py:29
  191.5 4.5 %fill_rows.2.refs_7_ = f32[4,512,4,256]{3,2,1,0:T(4,128)} custom-call(s32[3]{0:T(128)} %pad_add_fusion.where, f32[2,512,256]{2,1,0:T(8,128)} %get-tuple-element.78.refs_0_, f32[4,512,256]{2,1,0:T(8,128)} %copy-done.9, f32[2,512,256]{2,1,0:T(8,128)} %get-tuple-element.68.refs_2_, f32[2,512,256]{2,1,0:T(8,128)} %collective-permute-done.24.refs_3_, ...), custom_call_target="tpu_custom_call" | custom-call | bytes 8388608 | tf_op jit(solution)/shard_map/fill_rows/pallas_call | solution.py:387
  196.0 14.2 %collective-permute-done.28.refs_3_ = f32[2,512,256]{2,1,0:T(8,128)} collective-permute-done((f32[2,512,256]{2,1,0:T(8,128)S(1)}, f32[2,512,256]{2,1,0:T(8,128)}, u32[]{:S(2)}, u32[]{:S(2)}) %collective-permute-start.28) | collective-permute-done | bytes 1048608 | tf_op jit(solution)/shard_map/ppermute | solution.py:29
  210.2 5.4 %collective-permute-done.27.refs_2_ = f32[2,512,256]{2,1,0:T(8,128)S(1)} collective-permute-done((f32[2,512,256]{2,1,0:T(8,128)S(1)}, f32[2,512,256]{2,1,0:T(8,128)S(1)}, u32[]{:S(2)}, u32[]{:S(2)}) %collective-permute-start.27) | collective-permute-done | bytes 1048608 | tf_op jit(solution)/shard_map/ppermute | solution.py:29
  216.6 4.4 %fill_rows.3 = f32[4,512,4,256]{3,2,1,0:T(4,128)} custom-call(s32[3]{0:T(128)} %pad_add_fusion.where, f32[2,512,256]{2,1,0:T(8,128)} %copy-done.17, f32[2,512,256]{2,1,0:T(8,128)} %copy-done.16, f32[2,512,256]{2,1,0:T(8,128)} %copy-done.22, f32[2,512,256]{2,1,0:T(8,128)} %collective-permute-done.28.refs_3_, ...), custom_call_target="tpu_custom_call", output_to_operand_aliasing={{}: (8, {})} | custom-call | bytes 8388608 | tf_op jit(solution)/shard_map/fill_rows/pallas_call | solution.py:387
  (109 shorter events, 35.5 us)
Async XLA Ops:
  0.0 16.1 %collective-permute-start = (f32[2,64,1024]{2,1,0:T(8,128)}, f32[2,64,1024]{2,1,0:T(8,128)S(1)}, u32[]{:S(2)}, u32[]{:S(2)}) collective-permute-start(f32[2,64,1024]{2,1,0:T(8,128)} %bitcast.30), channel_id=1, source_target_pairs={{0,8},{1,1},{2,10},{3,17},{4,12},{5,33},{6,14},{7,49},{8,0},{9,65}... | collective-permute-start | bytes 1572872 | tf_op jit(solution)/shard_map/ppermute | solution.py:29
  3.5 13.4 %collective-permute-start.1 = (f32[2,64,1024]{2,1,0:T(8,128)}, f32[2,64,1024]{2,1,0:T(8,128)S(1)}, u32[]{:S(2)}, u32[]{:S(2)}) collective-permute-start(f32[2,64,1024]{2,1,0:T(8,128)} %bitcast.31), channel_id=1, source_target_pairs={{0,1},{1,8},{2,17},{3,10},{4,33},{5,12},{6,49},{7,14},{8,65},{9,0}... | collective-permute-start | bytes 1572872 | tf_op jit(solution)/shard_map/ppermute | solution.py:29
  3.6 13.3 %collective-permute-start.2 = (f32[2,64,1024]{2,1,0:T(8,128)}, f32[2,64,1024]{2,1,0:T(8,128)S(1)}, u32[]{:S(2)}, u32[]{:S(2)}) collective-permute-start(f32[2,64,1024]{2,1,0:T(8,128)} %bitcast.32), channel_id=1, source_target_pairs={{0,1},{1,0},{2,3},{3,2},{4,5},{5,4},{6,7},{7,6},{8,9},{9,8},{10,11... | collective-permute-start | bytes 1572872 | tf_op jit(solution)/shard_map/ppermute | solution.py:33
  19.5 27.3 %collective-permute-start.3 = (f32[2,2,64,1024]{3,2,1,0:T(8,128)S(1)}, f32[2,2,64,1024]{3,2,1,0:T(8,128)S(1)}, u32[]{:S(2)}, u32[]{:S(2)}) collective-permute-start(f32[2,2,64,1024]{3,2,1,0:T(8,128)S(1)} %get-tuple-element.50.refs_0_), channel_id=1, source_target_pairs={{0,2},{1,17},{2,4},{3,19},{4,6},{5,21},{6,0},{7,23},{8,10},{9,25},... | collective-permute-start | bytes 3145736 | tf_op jit(solution)/shard_map/ppermute | solution.py:29
  30.2 16.6 %collective-permute-start.4 = (f32[2,2,64,1024]{3,2,1,0:T(8,128)S(1)}, f32[2,2,64,1024]{3,2,1,0:T(8,128)S(1)}, u32[]{:S(2)}, u32[]{:S(2)}) collective-permute-start(f32[2,2,64,1024]{3,2,1,0:T(8,128)S(1)} %get-tuple-element.50.refs_0_), channel_id=1, source_target_pairs={{0,6},{1,49},{2,0},{3,51},{4,2},{5,53},{6,4},{7,55},{8,14},{9,57},... | collective-permute-start | bytes 3145736 | tf_op jit(solution)/shard_map/ppermute | solution.py:29
  48.9 16.2 %collective-permute-start.6 = (f32[2,2,64,1024]{3,2,1,0:T(8,128)S(1)}, f32[2,2,64,1024]{3,2,1,0:T(8,128)}, u32[]{:S(2)}, u32[]{:S(2)}) collective-permute-start(f32[2,2,64,1024]{3,2,1,0:T(8,128)S(1)} %broadcast_select_fusion.3.refs_1_), channel_id=1, source_target_pairs={{0,2},{1,17},{2,4},{3,19},{4,6},{5,21},{6,0},{7,23},{8,10},{9,25},... | collective-permute-start | bytes 3145736 | tf_op jit(solution)/shard_map/ppermute | solution.py:29
  50.0 21.4 %collective-permute-start.7 = (f32[2,2,64,1024]{3,2,1,0:T(8,128)S(1)}, f32[2,2,64,1024]{3,2,1,0:T(8,128)}, u32[]{:S(2)}, u32[]{:S(2)}) collective-permute-start(f32[2,2,64,1024]{3,2,1,0:T(8,128)S(1)} %broadcast_select_fusion.3.refs_1_), channel_id=1, source_target_pairs={{0,6},{1,49},{2,0},{3,51},{4,2},{5,53},{6,4},{7,55},{8,14},{9,57},... | collective-permute-start | bytes 3145736 | tf_op jit(solution)/shard_map/ppermute | solution.py:29
  52.2 19.2 %collective-permute-start.9 = (f32[2,2,64,1024]{3,2,1,0:T(8,128)S(1)}, f32[2,2,64,1024]{3,2,1,0:T(8,128)S(1)}, u32[]{:S(2)}, u32[]{:S(2)}) collective-permute-start(f32[2,2,64,1024]{3,2,1,0:T(8,128)S(1)} %broadcast_select_fusion.3.refs_1_), channel_id=1, source_target_pairs={{0,1},{1,0},{2,3},{3,2},{4,5},{5,4},{6,7},{7,6},{8,9},{9,8},{10,11... | collective-permute-start | bytes 3145736 | tf_op jit(solution)/shard_map/ppermute | solution.py:33
  62.9 17.2 %collective-permute-start.14 = (f32[2048,256]{1,0:T(8,128)S(1)}, f32[2048,256]{1,0:T(8,128)S(1)}, u32[]{:S(2)}, u32[]{:S(2)}) collective-permute-start(f32[2048,256]{1,0:T(8,128)S(1)} %get-tuple-element.88), channel_id=1, source_target_pairs={{0,1},{1,0},{2,3},{3,2},{4,5},{5,4},{6,7},{7,6},{8,9},{9,8},{10,11... | collective-permute-start | bytes 6291464 | tf_op jit(solution)/shard_map/ppermute | solution.py:33
  63.0 18.3 %collective-permute-start.15 = (f32[2048,256]{1,0:T(8,128)}, f32[2048,256]{1,0:T(8,128)}, u32[]{:S(2)}, u32[]{:S(2)}) collective-permute-start(f32[2048,256]{1,0:T(8,128)} %get-tuple-element.87), channel_id=1, source_target_pairs={{0,1},{1,0},{2,3},{3,2},{4,5},{5,4},{6,7},{7,6},{8,9},{9,8},{10,11... | collective-permute-start | bytes 6291464 | tf_op jit(solution)/shard_map/ppermute | solution.py:33
  76.9 18.9 %collective-permute-start.12 = (f32[2,2,64,1024]{3,2,1,0:T(8,128)}, f32[2,2,64,1024]{3,2,1,0:T(8,128)S(1)}, u32[]{:S(2)}, u32[]{:S(2)}) collective-permute-start(f32[2,2,64,1024]{3,2,1,0:T(8,128)} %copy-done.3), channel_id=1, source_target_pairs={{0,2},{1,17},{2,4},{3,19},{4,6},{5,21},{6,0},{7,23},{8,10},{9,25},... | collective-permute-start | bytes 3145736 | tf_op jit(solution)/shard_map/ppermute | solution.py:29
  76.9 18.9 %collective-permute-start.13 = (f32[2,2,64,1024]{3,2,1,0:T(8,128)}, f32[2,2,64,1024]{3,2,1,0:T(8,128)}, u32[]{:S(2)}, u32[]{:S(2)}) collective-permute-start(f32[2,2,64,1024]{3,2,1,0:T(8,128)} %collective-permute-done.7.refs_5_), channel_id=1, source_target_pairs={{0,6},{1,49},{2,0},{3,51},{4,2},{5,53},{6,4},{7,55},{8,14},{9,57},... | collective-permute-start | bytes 3145736 | tf_op jit(solution)/shard_map/ppermute | solution.py:29
  80.1 15.7 %collective-permute-start.16 = (f32[2,2,64,1024]{3,2,1,0:T(8,128)}, f32[2,2,64,1024]{3,2,1,0:T(8,128)}, u32[]{:S(2)}, u32[]{:S(2)}) collective-permute-start(f32[2,2,64,1024]{3,2,1,0:T(8,128)} %collective-permute-done.6.refs_3_), channel_id=1, source_target_pairs={{0,1},{1,0},{2,3},{3,2},{4,5},{5,4},{6,7},{7,6},{8,9},{9,8},{10,11... | collective-permute-start | bytes 3145736 | tf_op jit(solution)/shard_map/ppermute | solution.py:33
  80.2 15.6 %collective-permute-start.17 = (f32[2,2,64,1024]{3,2,1,0:T(8,128)}, f32[2,2,64,1024]{3,2,1,0:T(8,128)}, u32[]{:S(2)}, u32[]{:S(2)}) collective-permute-start(f32[2,2,64,1024]{3,2,1,0:T(8,128)} %collective-permute-done.7.refs_5_), channel_id=1, source_target_pairs={{0,1},{1,0},{2,3},{3,2},{4,5},{5,4},{6,7},{7,6},{8,9},{9,8},{10,11... | collective-permute-start | bytes 3145736 | tf_op jit(solution)/shard_map/ppermute | solution.py:33
  125.7 29.3 %collective-permute-start.20 = (f32[2,512,256]{2,1,0:T(8,128)}, f32[2,512,256]{2,1,0:T(8,128)S(1)}, u32[]{:S(2)}, u32[]{:S(2)}) collective-permute-start(f32[2,512,256]{2,1,0:T(8,128)} %get-tuple-element.66), channel_id=1, source_target_pairs={{0,16},{1,17},{2,18},{3,19},{4,20},{5,21},{6,22},{7,23},{8,24},{9,... | collective-permute-start | bytes 3145736 | tf_op jit(solution)/shard_map/ppermute | solution.py:29
  125.8 30.2 %collective-permute-start.23 = (f32[2,512,256]{2,1,0:T(8,128)}, f32[2,512,256]{2,1,0:T(8,128)S(1)}, u32[]{:S(2)}, u32[]{:S(2)}) collective-permute-start(f32[2,512,256]{2,1,0:T(8,128)} %get-tuple-element.69), channel_id=1, source_target_pairs={{0,7},{1,2},{2,1},{3,4},{4,3},{5,6},{6,5},{7,0},{8,15},{9,10},{10,... | collective-permute-start | bytes 3145736 | tf_op jit(solution)/shard_map/ppermute | solution.py:29
  127.2 28.8 %collective-permute-start.24 = (f32[2,512,256]{2,1,0:T(8,128)}, f32[2,512,256]{2,1,0:T(8,128)}, u32[]{:S(2)}, u32[]{:S(2)}) collective-permute-start(f32[2,512,256]{2,1,0:T(8,128)} %get-tuple-element.69), channel_id=1, source_target_pairs={{0,1},{1,0},{2,3},{3,2},{4,5},{5,4},{6,7},{7,6},{8,9},{9,8},{10,11... | collective-permute-start | bytes 3145736 | tf_op jit(solution)/shard_map/ppermute | solution.py:33
  127.2 28.8 %collective-permute-start.21 = (f32[2,512,256]{2,1,0:T(8,128)}, f32[2,512,256]{2,1,0:T(8,128)}, u32[]{:S(2)}, u32[]{:S(2)}) collective-permute-start(f32[2,512,256]{2,1,0:T(8,128)} %get-tuple-element.67), channel_id=1, source_target_pairs={{0,112},{1,113},{2,114},{3,115},{4,116},{5,117},{6,118},{7,119},{8... | collective-permute-start | bytes 3145736 | tf_op jit(solution)/shard_map/ppermute | solution.py:29
  132.4 23.6 %collective-permute-start.22 = (f32[2,512,256]{2,1,0:T(8,128)}, f32[2,512,256]{2,1,0:T(8,128)}, u32[]{:S(2)}, u32[]{:S(2)}) collective-permute-start(f32[2,512,256]{2,1,0:T(8,128)} %get-tuple-element.68.refs_2_), channel_id=1, source_target_pairs={{0,6},{1,3},{2,0},{3,5},{4,2},{5,7},{6,4},{7,1},{8,14},{9,11},{10,... | collective-permute-start | bytes 3145736 | tf_op jit(solution)/shard_map/ppermute | solution.py:29
  160.5 55.1 %collective-permute-start.29 = (f32[2,512,256]{2,1,0:T(8,128)}, f32[2,512,256]{2,1,0:T(8,128)}, u32[]{:S(2)}, u32[]{:S(2)}) collective-permute-start(f32[2,512,256]{2,1,0:T(8,128)} %pad_maximum_fusion.4), channel_id=1, source_target_pairs={{0,1},{1,3},{2,0},{3,5},{4,2},{5,7},{6,4},{7,9},{8,6},{9,11},{10,8... | collective-permute-start | bytes 3145736 | tf_op jit(solution)/shard_map/ppermute | solution.py:29
  161.1 29.5 %collective-permute-start.26 = (f32[2,512,256]{2,1,0:T(8,128)S(1)}, f32[2,512,256]{2,1,0:T(8,128)S(1)}, u32[]{:S(2)}, u32[]{:S(2)}) collective-permute-start(f32[2,512,256]{2,1,0:T(8,128)S(1)} %broadcast_select_fusion.2), channel_id=1, source_target_pairs={{0,8},{1,9},{14,6},{15,7},{16,24},{17,25},{30,22},{31,23},{32,40},... | collective-permute-start | bytes 3145736 | tf_op jit(solution)/shard_map/ppermute | solution.py:29
  168.4 41.8 %collective-permute-start.28 = (f32[2,512,256]{2,1,0:T(8,128)S(1)}, f32[2,512,256]{2,1,0:T(8,128)}, u32[]{:S(2)}, u32[]{:S(2)}) collective-permute-start(f32[2,512,256]{2,1,0:T(8,128)S(1)} %pad_maximum_fusion.2.refs_1_), channel_id=1, source_target_pairs={{0,112},{1,113},{2,114},{3,115},{4,116},{5,117},{6,118},{7,119},{8... | collective-permute-start | bytes 3145736 | tf_op jit(solution)/shard_map/ppermute | solution.py:29
  173.4 42.2 %collective-permute-start.27 = (f32[2,512,256]{2,1,0:T(8,128)S(1)}, f32[2,512,256]{2,1,0:T(8,128)S(1)}, u32[]{:S(2)}, u32[]{:S(2)}) collective-permute-start(f32[2,512,256]{2,1,0:T(8,128)S(1)} %pad_maximum_fusion.1.refs_0_), channel_id=1, source_target_pairs={{0,16},{1,17},{2,18},{3,19},{4,20},{5,21},{6,22},{7,23},{8,24},{9,... | collective-permute-start | bytes 3145736 | tf_op jit(solution)/shard_map/ppermute | solution.py:29
  173.6 42.0 %collective-permute-start.30 = (f32[2,512,256]{2,1,0:T(8,128)S(1)}, f32[2,512,256]{2,1,0:T(8,128)}, u32[]{:S(2)}, u32[]{:S(2)}) collective-permute-start(f32[2,512,256]{2,1,0:T(8,128)S(1)} %pad_maximum_fusion.3.refs_4_), channel_id=1, source_target_pairs={{0,0},{1,2},{2,1},{3,4},{4,3},{5,6},{6,5},{7,8},{8,7},{9,10},{10,9... | collective-permute-start | bytes 3145736 | tf_op jit(solution)/shard_map/ppermute | solution.py:29
  (32 other events, 261.8 us)

commit v5 on v3

--- a/solution.py
+++ b/solution.py
@@ -438,6 +438,14 @@
     return (r + 7) & 7, c, l
 
 
+def still_up(r, c, l):
+    return (r + 1, c, l) if r < 7 else None
+
+
+def still_down(r, c, l):
+    return (r - 1, c, l) if r > 0 else None
+
+
 def column_straight(r, c, l):
     if (c, l) in ((0, 0), (7, 1)):
         return r, c, 1 - l
@@ -525,8 +533,8 @@
     from_still = in_chip(beside)
     edge_up = jnp.stack([w_up, from_still[3]])
     edge_down = jnp.stack([w_down, from_still[2]])
-    still_got_up = send(edge_up, row_up)
-    still_got_down = send(edge_down, row_down)
+    still_got_up = send(edge_up, still_up)
+    still_got_down = send(edge_down, still_down)
 
     top = jnp.where(row_pos == 0, d_down, got_up)
     bottom = jnp.where(row_pos == 7, d_up, got_down)

time: 220 us -> 220 us (level)
  waiting for transfers between devices: 74.3 us -> 70.6 us
  starting transfers between devices: 61.1 us -> 64.8 us
    ppermute x18, waiting for transfers between devices: 65.7 us -> 61.9 us  [send(): return lax.ppermute(x, AXES, route(place))]
    ppermute x18, starting transfers between devices: 45.3 us -> 49 us  [send(): return lax.ppermute(x, AXES, route(place))]
where the time goes in v5:
time: 220 us; the launch traced here: 219 us
  waiting for transfers between devices  70.6 us (32%)
  starting transfers between devices  64.8 us (29%)
  Pallas kernels  59.7 us (27%)
  local copies, waits for them, and re-layouts  17.2 us (8%)
  other arithmetic  6.14 us (3%)
    ppermute x18, waiting for transfers between devices, send(): return lax.ppermute(x, AXES, route(place))  61.9 us
    ppermute x18, starting transfers between devices, send(): return lax.ppermute(x, AXES, route(place))  49 us
    pallas_call x1, Pallas kernels, moving_product(): pl.pallas_call(moving_kernel, grid_spec=pltpu.PrefetchScalarGridSpec(num_...  24.3 us
    ppermute x13, starting transfers between devices, in_chip(): return lax.ppermute(x, 'layer', [(0, 1), (1, 0)])  15.8 us
    pallas_call x1, Pallas kernels, early_product(): pl.pallas_call(early_kernel, grid_spec=pltpu.PrefetchScalarGridSpec(num_s...  14.2 us
    pallas_call x1, Pallas kernels, still_product(): pl.pallas_call(still_kernel, grid_spec=pltpu.PrefetchScalarGridSpec(num_s...  12.4 us
    pallas_call x2, Pallas kernels, fill_rows(): pl.pallas_call(kernel, grid_spec=pltpu.PrefetchScalarGridSpec(num_scalar_...  8.9 us
    ppermute x13, waiting for transfers between devices, in_chip(): return lax.ppermute(x, 'layer', [(0, 1), (1, 0)])  8.64 us
  transfers between devices with their start and end apart: 31, of which 14 were waited for; matrix products, arithmetic and copies ran while one was open for 6% of the time, Pallas kernels for 14%

profile of v5, /device:TPU:6, one launch (start us, length us, event | category | flops | bytes accessed | tf_op | source)
XLA Modules:
  0.0 219.0 jit_solution(17557079474804834991)
XLA Ops:
  0.0 2.7 %collective-permute-start = (f32[2,64,1024]{2,1,0:T(8,128)}, f32[2,64,1024]{2,1,0:T(8,128)S(1)}, u32[]{:S(2)}, u32[]{:S(2)}) collective-permute-start(f32[2,64,1024]{2,1,0:T(8,128)} %bitcast.30), channel_id=1, source_target_pairs={{0,8},{1,1},{2,10},{3,17},{4,12},{5,33},{6,14},{7,49},{8,0},{9,65}... | collective-permute-start | bytes 1572872 | tf_op jit(solution)/shard_map/ppermute | solution.py:29
  4.1 12.4 %collective-permute-done = f32[2,64,1024]{2,1,0:T(8,128)S(1)} collective-permute-done((f32[2,64,1024]{2,1,0:T(8,128)}, f32[2,64,1024]{2,1,0:T(8,128)S(1)}, u32[]{:S(2)}, u32[]{:S(2)}) %collective-permute-start) | collective-permute-done | bytes 524320 | tf_op jit(solution)/shard_map/ppermute | solution.py:29
  19.5 10.6 %collective-permute-start.3 = (f32[2,2,64,1024]{3,2,1,0:T(8,128)S(1)}, f32[2,2,64,1024]{3,2,1,0:T(8,128)S(1)}, u32[]{:S(2)}, u32[]{:S(2)}) collective-permute-start(f32[2,2,64,1024]{3,2,1,0:T(8,128)S(1)} %get-tuple-element.48.refs_0_), channel_id=1, source_target_pairs={{0,2},{1,17},{2,4},{3,19},{4,6},{5,21},{6,0},{7,23},{8,10},{9,25},... | collective-permute-start | bytes 3145736 | tf_op jit(solution)/shard_map/ppermute | solution.py:29
  30.1 3.9 %collective-permute-start.4 = (f32[2,2,64,1024]{3,2,1,0:T(8,128)S(1)}, f32[2,2,64,1024]{3,2,1,0:T(8,128)S(1)}, u32[]{:S(2)}, u32[]{:S(2)}) collective-permute-start(f32[2,2,64,1024]{3,2,1,0:T(8,128)S(1)} %get-tuple-element.48.refs_0_), channel_id=1, source_target_pairs={{0,6},{1,49},{2,0},{3,51},{4,2},{5,53},{6,4},{7,55},{8,14},{9,57},... | collective-permute-start | bytes 3145736 | tf_op jit(solution)/shard_map/ppermute | solution.py:29
  35.7 8.4 %copy.4 = f32[4,4,512,256]{3,2,1,0:T(8,128)} copy(f32[4,4,512,256]{3,0,2,1:T(4,128)} %bitcast.29) | data formatting | bytes 16777216 | tf_op jit(solution)/shard_map/transpose | solution.py:488
  52.1 6.2 %collective-permute-start.9 = (f32[2,2,64,1024]{3,2,1,0:T(8,128)S(1)}, f32[2,2,64,1024]{3,2,1,0:T(8,128)S(1)}, u32[]{:S(2)}, u32[]{:S(2)}) collective-permute-start(f32[2,2,64,1024]{3,2,1,0:T(8,128)S(1)} %broadcast_select_fusion.3.refs_1_), channel_id=1, source_target_pairs={{0,1},{1,0},{2,3},{3,2},{4,5},{5,4},{6,7},{7,6},{8,9},{9,8},{10,11... | collective-permute-start | bytes 3145736 | tf_op jit(solution)/shard_map/ppermute | solution.py:33
  58.3 3.8 %dynamic-slice_bitcast_fusion = (f32[2048,256]{1,0:T(8,128)}, f32[2048,256]{1,0:T(8,128)S(1)}) fusion(f32[4,2048,256]{2,1,0:T(8,128)} %bitcast.20, s32[]{:T(128)S(6)} %add.6, s32[]{:T(128)S(6)} %select_n.91), kind=kLoop, calls=%fused_computation | loop fusion | bytes 8388616 | tf_op jit(solution)/shard_map/squeeze | solution.py:490
  65.0 5.6 %collective-permute-start.10 = (f32[2,2,64,1024]{3,2,1,0:T(8,128)}, f32[2,2,64,1024]{3,2,1,0:T(8,128)S(1)}, u32[]{:S(2)}, u32[]{:S(2)}) collective-permute-start(f32[2,2,64,1024]{3,2,1,0:T(8,128)} %copy-done.3), channel_id=1, source_target_pairs={{0,1},{1,0},{2,3},{3,2},{4,5},{5,4},{6,7},{7,6},{8,9},{9,8},{10,11... | collective-permute-start | bytes 3145736 | tf_op jit(solution)/shard_map/ppermute | solution.py:33
  73.1 3.0 %collective-permute-done.11.refs_7_.refs_12_ = f32[2,2,64,1024]{3,2,1,0:T(8,128)S(1)} collective-permute-done((f32[2,2,64,1024]{3,2,1,0:T(8,128)}, f32[2,2,64,1024]{3,2,1,0:T(8,128)S(1)}, u32[]{:S(2)}, u32[]{:S(2)}) %collective-permute-start.11) | collective-permute-done | bytes 1048608 | tf_op jit(solution)/shard_map/ppermute | solution.py:33
  76.1 3.2 %collective-permute-start.13 = (f32[2,2,64,1024]{3,2,1,0:T(8,128)}, f32[2,2,64,1024]{3,2,1,0:T(8,128)}, u32[]{:S(2)}, u32[]{:S(2)}) collective-permute-start(f32[2,2,64,1024]{3,2,1,0:T(8,128)} %collective-permute-done.7.refs_5_), channel_id=1, source_target_pairs={{0,6},{1,49},{2,0},{3,51},{4,2},{5,53},{6,4},{7,55},{8,14},{9,57},... | collective-permute-start | bytes 3145736 | tf_op jit(solution)/shard_map/ppermute | solution.py:29
  80.7 14.2 %early_product.1.refs_16_ = f32[2048,1024]{1,0:T(8,128)} custom-call(s32[3]{0:T(128)} %pad_add_fusion.where, f32[2,2,64,1024]{3,2,1,0:T(8,128)} %copy-done.1, f32[2,2,64,1024]{3,2,1,0:T(8,128)} %copy-done.2, f32[2,2,64,1024]{3,2,1,0:T(8,128)} %copy-done.3, f32[2,2,64,1024]{3,2,1,0:T(8,128)} %copy-done.4, f32[2,2,64,1024]{3,2,1,0:T(8,128)} %copy-done.8, ...), custom_call_target="tpu_custom_call" | custom-call | flops 6442450944 | bytes 25165824 | tf_op jit(solution)/shard_map/early_product/pallas_call | solution.py:116
  100.6 24.3 %moving_product.1 = (bf16[2048,1024]{1,0:T(8,128)(2,1)}, bf16[2048,1024]{1,0:T(8,128)(2,1)}, f32[2,512,256]{2,1,0:T(8,128)}, f32[2,512,256]{2,1,0:T(8,128)}, f32...) custom-call(s32[3]{0:T(128)} %pad_add_fusion.where, f32[2,2,64,1024]{3,2,1,0:T(8,128)} %copy-done.1, ...), custom_call_target="tpu_custom_call" | custom-call | flops 12884901888 | bytes 37748736 | tf_op jit(solution)/shard_map/moving_product/pallas_call | solution.py:297
  124.9 5.6 %collective-permute-start.21 = (f32[2,512,256]{2,1,0:T(8,128)}, f32[2,512,256]{2,1,0:T(8,128)S(1)}, u32[]{:S(2)}, u32[]{:S(2)}) collective-permute-start(f32[2,512,256]{2,1,0:T(8,128)} %get-tuple-element.65), channel_id=1, source_target_pairs={{0,112},{1,113},{2,114},{3,115},{4,116},{5,117},{6,118},{7,119},{8... | collective-permute-start | bytes 3145736 | tf_op jit(solution)/shard_map/ppermute | solution.py:29
  132.9 12.4 %still_product.1 = (f32[512,256]{1,0:T(8,128)}, f32[512,256]{1,0:T(8,128)}, f32[2,512,256]{2,1,0:T(8,128)}, f32[4,512,256]{2,1,0:T(8,128)}) custom-call(s32[3]{0:T(128)} %pad_add_fusion.where, f32[2,2,64,1024]{3,2,1,0:T(8,128)} %copy-done.1, f32[2,2,64,1024]{3,2,1,0:T(8,128)} %copy-done.2, f32[2,2,64,1024]{3,2,1,0:T(8,128)} %copy-done.3, ...), custom_call_target="tpu_custom_call" | custom-call | flops 6442450944 | bytes 20971520 | tf_op jit(solution)/shard_map/still_product/pallas_call | solution.py:330
  145.3 8.9 %collective-permute-done.20 = f32[2,512,256]{2,1,0:T(8,128)S(1)} collective-permute-done((f32[2,512,256]{2,1,0:T(8,128)}, f32[2,512,256]{2,1,0:T(8,128)S(1)}, u32[]{:S(2)}, u32[]{:S(2)}) %collective-permute-start.20) | collective-permute-done | bytes 1048608 | tf_op jit(solution)/shard_map/ppermute | solution.py:29
  160.8 3.7 %collective-permute-start.28 = (f32[2,512,256]{2,1,0:T(8,128)S(1)}, f32[2,512,256]{2,1,0:T(8,128)}, u32[]{:S(2)}, u32[]{:S(2)}) collective-permute-start(f32[2,512,256]{2,1,0:T(8,128)S(1)} %pad_maximum_fusion.4), channel_id=1, source_target_pairs={{0,1},{1,3},{2,0},{3,5},{4,2},{5,7},{6,4},{7,9},{8,6},{9,11},{10,8... | collective-permute-start | bytes 3145736 | tf_op jit(solution)/shard_map/ppermute | solution.py:29
  164.6 3.3 %collective-permute-start.29 = (f32[2,512,256]{2,1,0:T(8,128)S(1)}, f32[2,512,256]{2,1,0:T(8,128)}, u32[]{:S(2)}, u32[]{:S(2)}) collective-permute-start(f32[2,512,256]{2,1,0:T(8,128)S(1)} %pad_maximum_fusion.3.refs_4_), channel_id=1, source_target_pairs={{0,0},{1,2},{2,1},{3,4},{4,3},{5,6},{6,5},{7,8},{8,7},{9,10},{10,9... | collective-permute-start | bytes 3145736 | tf_op jit(solution)/shard_map/ppermute | solution.py:29
  169.3 4.9 %collective-permute-start.27 = (f32[2,512,256]{2,1,0:T(8,128)S(1)}, f32[2,512,256]{2,1,0:T(8,128)}, u32[]{:S(2)}, u32[]{:S(2)}) collective-permute-start(f32[2,512,256]{2,1,0:T(8,128)S(1)} %pad_maximum_fusion.2.refs_1_), channel_id=1, source_target_pairs={{16,0},{17,1},{18,2},{19,3},{20,4},{21,5},{22,6},{23,7},{24,8},{25... | collective-permute-start | bytes 3145736 | tf_op jit(solution)/shard_map/ppermute | solution.py:29
  176.2 11.1 %collective-permute-done.30.refs_6_ = f32[2,512,256]{2,1,0:T(8,128)} collective-permute-done((f32[2,512,256]{2,1,0:T(8,128)S(1)}, f32[2,512,256]{2,1,0:T(8,128)}, u32[]{:S(2)}, u32[]{:S(2)}) %collective-permute-start.30) | collective-permute-done | bytes 1048608 | tf_op jit(solution)/shard_map/ppermute | solution.py:29
  187.3 4.5 %fill_rows.2.refs_7_ = f32[4,512,4,256]{3,2,1,0:T(4,128)} custom-call(s32[3]{0:T(128)} %pad_add_fusion.where, f32[2,512,256]{2,1,0:T(8,128)} %get-tuple-element.79.refs_0_, f32[4,512,256]{2,1,0:T(8,128)} %copy-done.9, f32[2,512,256]{2,1,0:T(8,128)} %get-tuple-element.66.refs_2_, f32[2,512,256]{2,1,0:T(8,128)} %copy-done.20, f32[2,512,256]{2,1,0:T(8,128)} %copy-done.15, ...), custom_call_target="tpu_custom_call" | custom-call | bytes 8388608 | tf_op jit(solution)/shard_map/fill_rows/pallas_call | solution.py:387
  191.8 9.1 %collective-permute-done.29.refs_6_ = f32[2,512,256]{2,1,0:T(8,128)} collective-permute-done((f32[2,512,256]{2,1,0:T(8,128)S(1)}, f32[2,512,256]{2,1,0:T(8,128)}, u32[]{:S(2)}, u32[]{:S(2)}) %collective-permute-start.29) | collective-permute-done | bytes 1048608 | tf_op jit(solution)/shard_map/ppermute | solution.py:29
  200.8 9.7 %collective-permute-done.27.refs_3_ = f32[2,512,256]{2,1,0:T(8,128)} collective-permute-done((f32[2,512,256]{2,1,0:T(8,128)S(1)}, f32[2,512,256]{2,1,0:T(8,128)}, u32[]{:S(2)}, u32[]{:S(2)}) %collective-permute-start.27) | collective-permute-done | bytes 1048608 | tf_op jit(solution)/shard_map/ppermute | solution.py:29
  210.5 2.9 %collective-permute-done.26.refs_2_ = f32[2,512,256]{2,1,0:T(8,128)S(1)} collective-permute-done((f32[2,512,256]{2,1,0:T(8,128)S(1)}, f32[2,512,256]{2,1,0:T(8,128)S(1)}, u32[]{:S(2)}, u32[]{:S(2)}) %collective-permute-start.26) | collective-permute-done | bytes 1048608 | tf_op jit(solution)/shard_map/ppermute | solution.py:29
  214.4 4.4 %fill_rows.3 = f32[4,512,4,256]{3,2,1,0:T(4,128)} custom-call(s32[3]{0:T(128)} %pad_add_fusion.where, f32[2,512,256]{2,1,0:T(8,128)} %copy-done.19, f32[2,512,256]{2,1,0:T(8,128)} %copy-done.18, f32[2,512,256]{2,1,0:T(8,128)} %copy-done.27, f32[2,512,256]{2,1,0:T(8,128)} %collective-permute-done.27.refs_3_, ...), custom_call_target="tpu_custom_call", output_to_operand_aliasing={{}: (8, {})} | custom-call | bytes 8388608 | tf_op jit(solution)/shard_map/fill_rows/pallas_call | solution.py:387
  (119 shorter events, 39.5 us)
Async XLA Ops:
  0.0 16.5 %collective-permute-start = (f32[2,64,1024]{2,1,0:T(8,128)}, f32[2,64,1024]{2,1,0:T(8,128)S(1)}, u32[]{:S(2)}, u32[]{:S(2)}) collective-permute-start(f32[2,64,1024]{2,1,0:T(8,128)} %bitcast.30), channel_id=1, source_target_pairs={{0,8},{1,1},{2,10},{3,17},{4,12},{5,33},{6,14},{7,49},{8,0},{9,65}... | collective-permute-start | bytes 1572872 | tf_op jit(solution)/shard_map/ppermute | solution.py:29
  2.7 14.2 %collective-permute-start.1 = (f32[2,64,1024]{2,1,0:T(8,128)}, f32[2,64,1024]{2,1,0:T(8,128)S(1)}, u32[]{:S(2)}, u32[]{:S(2)}) collective-permute-start(f32[2,64,1024]{2,1,0:T(8,128)} %bitcast.31), channel_id=1, source_target_pairs={{0,1},{1,8},{2,17},{3,10},{4,33},{5,12},{6,49},{7,14},{8,65},{9,0}... | collective-permute-start | bytes 1572872 | tf_op jit(solution)/shard_map/ppermute | solution.py:29
  2.8 14.1 %collective-permute-start.2 = (f32[2,64,1024]{2,1,0:T(8,128)}, f32[2,64,1024]{2,1,0:T(8,128)S(1)}, u32[]{:S(2)}, u32[]{:S(2)}) collective-permute-start(f32[2,64,1024]{2,1,0:T(8,128)} %bitcast.32), channel_id=1, source_target_pairs={{0,1},{1,0},{2,3},{3,2},{4,5},{5,4},{6,7},{7,6},{8,9},{9,8},{10,11... | collective-permute-start | bytes 1572872 | tf_op jit(solution)/shard_map/ppermute | solution.py:33
  19.5 27.2 %collective-permute-start.3 = (f32[2,2,64,1024]{3,2,1,0:T(8,128)S(1)}, f32[2,2,64,1024]{3,2,1,0:T(8,128)S(1)}, u32[]{:S(2)}, u32[]{:S(2)}) collective-permute-start(f32[2,2,64,1024]{3,2,1,0:T(8,128)S(1)} %get-tuple-element.48.refs_0_), channel_id=1, source_target_pairs={{0,2},{1,17},{2,4},{3,19},{4,6},{5,21},{6,0},{7,23},{8,10},{9,25},... | collective-permute-start | bytes 3145736 | tf_op jit(solution)/shard_map/ppermute | solution.py:29
  30.1 16.6 %collective-permute-start.4 = (f32[2,2,64,1024]{3,2,1,0:T(8,128)S(1)}, f32[2,2,64,1024]{3,2,1,0:T(8,128)S(1)}, u32[]{:S(2)}, u32[]{:S(2)}) collective-permute-start(f32[2,2,64,1024]{3,2,1,0:T(8,128)S(1)} %get-tuple-element.48.refs_0_), channel_id=1, source_target_pairs={{0,6},{1,49},{2,0},{3,51},{4,2},{5,53},{6,4},{7,55},{8,14},{9,57},... | collective-permute-start | bytes 3145736 | tf_op jit(solution)/shard_map/ppermute | solution.py:29
  48.8 16.2 %collective-permute-start.6 = (f32[2,2,64,1024]{3,2,1,0:T(8,128)S(1)}, f32[2,2,64,1024]{3,2,1,0:T(8,128)}, u32[]{:S(2)}, u32[]{:S(2)}) collective-permute-start(f32[2,2,64,1024]{3,2,1,0:T(8,128)S(1)} %broadcast_select_fusion.3.refs_1_), channel_id=1, source_target_pairs={{0,2},{1,17},{2,4},{3,19},{4,6},{5,21},{6,0},{7,23},{8,10},{9,25},... | collective-permute-start | bytes 3145736 | tf_op jit(solution)/shard_map/ppermute | solution.py:29
  49.9 20.7 %collective-permute-start.7 = (f32[2,2,64,1024]{3,2,1,0:T(8,128)S(1)}, f32[2,2,64,1024]{3,2,1,0:T(8,128)}, u32[]{:S(2)}, u32[]{:S(2)}) collective-permute-start(f32[2,2,64,1024]{3,2,1,0:T(8,128)S(1)} %broadcast_select_fusion.3.refs_1_), channel_id=1, source_target_pairs={{0,6},{1,49},{2,0},{3,51},{4,2},{5,53},{6,4},{7,55},{8,14},{9,57},... | collective-permute-start | bytes 3145736 | tf_op jit(solution)/shard_map/ppermute | solution.py:29
  52.1 18.5 %collective-permute-start.9 = (f32[2,2,64,1024]{3,2,1,0:T(8,128)S(1)}, f32[2,2,64,1024]{3,2,1,0:T(8,128)S(1)}, u32[]{:S(2)}, u32[]{:S(2)}) collective-permute-start(f32[2,2,64,1024]{3,2,1,0:T(8,128)S(1)} %broadcast_select_fusion.3.refs_1_), channel_id=1, source_target_pairs={{0,1},{1,0},{2,3},{3,2},{4,5},{5,4},{6,7},{7,6},{8,9},{9,8},{10,11... | collective-permute-start | bytes 3145736 | tf_op jit(solution)/shard_map/ppermute | solution.py:33
  62.2 17.2 %collective-permute-start.14 = (f32[2048,256]{1,0:T(8,128)S(1)}, f32[2048,256]{1,0:T(8,128)S(1)}, u32[]{:S(2)}, u32[]{:S(2)}) collective-permute-start(f32[2048,256]{1,0:T(8,128)S(1)} %get-tuple-element.84), channel_id=1, source_target_pairs={{0,1},{1,0},{2,3},{3,2},{4,5},{5,4},{6,7},{7,6},{8,9},{9,8},{10,11... | collective-permute-start | bytes 6291464 | tf_op jit(solution)/shard_map/ppermute | solution.py:33
  62.3 18.4 %collective-permute-start.15 = (f32[2048,256]{1,0:T(8,128)}, f32[2048,256]{1,0:T(8,128)}, u32[]{:S(2)}, u32[]{:S(2)}) collective-permute-start(f32[2048,256]{1,0:T(8,128)} %get-tuple-element.83), channel_id=1, source_target_pairs={{0,1},{1,0},{2,3},{3,2},{4,5},{5,4},{6,7},{7,6},{8,9},{9,8},{10,11... | collective-permute-start | bytes 6291464 | tf_op jit(solution)/shard_map/ppermute | solution.py:33
  76.1 18.8 %collective-permute-start.12 = (f32[2,2,64,1024]{3,2,1,0:T(8,128)}, f32[2,2,64,1024]{3,2,1,0:T(8,128)S(1)}, u32[]{:S(2)}, u32[]{:S(2)}) collective-permute-start(f32[2,2,64,1024]{3,2,1,0:T(8,128)} %copy-done.3), channel_id=1, source_target_pairs={{0,2},{1,17},{2,4},{3,19},{4,6},{5,21},{6,0},{7,23},{8,10},{9,25},... | collective-permute-start | bytes 3145736 | tf_op jit(solution)/shard_map/ppermute | solution.py:29
  76.1 18.8 %collective-permute-start.13 = (f32[2,2,64,1024]{3,2,1,0:T(8,128)}, f32[2,2,64,1024]{3,2,1,0:T(8,128)}, u32[]{:S(2)}, u32[]{:S(2)}) collective-permute-start(f32[2,2,64,1024]{3,2,1,0:T(8,128)} %collective-permute-done.7.refs_5_), channel_id=1, source_target_pairs={{0,6},{1,49},{2,0},{3,51},{4,2},{5,53},{6,4},{7,55},{8,14},{9,57},... | collective-permute-start | bytes 3145736 | tf_op jit(solution)/shard_map/ppermute | solution.py:29
  79.4 15.6 %collective-permute-start.16 = (f32[2,2,64,1024]{3,2,1,0:T(8,128)}, f32[2,2,64,1024]{3,2,1,0:T(8,128)}, u32[]{:S(2)}, u32[]{:S(2)}) collective-permute-start(f32[2,2,64,1024]{3,2,1,0:T(8,128)} %collective-permute-done.6.refs_3_), channel_id=1, source_target_pairs={{0,1},{1,0},{2,3},{3,2},{4,5},{5,4},{6,7},{7,6},{8,9},{9,8},{10,11... | collective-permute-start | bytes 3145736 | tf_op jit(solution)/shard_map/ppermute | solution.py:33
  79.4 15.6 %collective-permute-start.17 = (f32[2,2,64,1024]{3,2,1,0:T(8,128)}, f32[2,2,64,1024]{3,2,1,0:T(8,128)}, u32[]{:S(2)}, u32[]{:S(2)}) collective-permute-start(f32[2,2,64,1024]{3,2,1,0:T(8,128)} %collective-permute-done.7.refs_5_), channel_id=1, source_target_pairs={{0,1},{1,0},{2,3},{3,2},{4,5},{5,4},{6,7},{7,6},{8,9},{9,8},{10,11... | collective-permute-start | bytes 3145736 | tf_op jit(solution)/shard_map/ppermute | solution.py:33
  124.8 29.3 %collective-permute-start.20 = (f32[2,512,256]{2,1,0:T(8,128)}, f32[2,512,256]{2,1,0:T(8,128)S(1)}, u32[]{:S(2)}, u32[]{:S(2)}) collective-permute-start(f32[2,512,256]{2,1,0:T(8,128)} %get-tuple-element.64), channel_id=1, source_target_pairs={{0,16},{1,17},{2,18},{3,19},{4,20},{5,21},{6,22},{7,23},{8,24},{9,... | collective-permute-start | bytes 3145736 | tf_op jit(solution)/shard_map/ppermute | solution.py:29
  124.9 29.3 %collective-permute-start.21 = (f32[2,512,256]{2,1,0:T(8,128)}, f32[2,512,256]{2,1,0:T(8,128)S(1)}, u32[]{:S(2)}, u32[]{:S(2)}) collective-permute-start(f32[2,512,256]{2,1,0:T(8,128)} %get-tuple-element.65), channel_id=1, source_target_pairs={{0,112},{1,113},{2,114},{3,115},{4,116},{5,117},{6,118},{7,119},{8... | collective-permute-start | bytes 3145736 | tf_op jit(solution)/shard_map/ppermute | solution.py:29
  130.5 23.6 %collective-permute-start.22 = (f32[2,512,256]{2,1,0:T(8,128)}, f32[2,512,256]{2,1,0:T(8,128)S(1)}, u32[]{:S(2)}, u32[]{:S(2)}) collective-permute-start(f32[2,512,256]{2,1,0:T(8,128)} %get-tuple-element.66.refs_2_), channel_id=1, source_target_pairs={{0,6},{1,3},{2,0},{3,5},{4,2},{5,7},{6,4},{7,1},{8,14},{9,11},{10,... | collective-permute-start | bytes 3145736 | tf_op jit(solution)/shard_map/ppermute | solution.py:29
  132.1 24.7 %collective-permute-start.23 = (f32[2,512,256]{2,1,0:T(8,128)}, f32[2,512,256]{2,1,0:T(8,128)S(1)}, u32[]{:S(2)}, u32[]{:S(2)}) collective-permute-start(f32[2,512,256]{2,1,0:T(8,128)} %get-tuple-element.67), channel_id=1, source_target_pairs={{0,7},{1,2},{2,1},{3,4},{4,3},{5,6},{6,5},{7,0},{8,15},{9,10},{10,... | collective-permute-start | bytes 3145736 | tf_op jit(solution)/shard_map/ppermute | solution.py:29
  132.9 23.9 %collective-permute-start.24 = (f32[2,512,256]{2,1,0:T(8,128)}, f32[2,512,256]{2,1,0:T(8,128)S(1)}, u32[]{:S(2)}, u32[]{:S(2)}) collective-permute-start(f32[2,512,256]{2,1,0:T(8,128)} %get-tuple-element.67), channel_id=1, source_target_pairs={{0,1},{1,0},{2,3},{3,2},{4,5},{5,4},{6,7},{7,6},{8,9},{9,8},{10,11... | collective-permute-start | bytes 3145736 | tf_op jit(solution)/shard_map/ppermute | solution.py:33
  158.4 28.8 %collective-permute-start.30 = (f32[2,512,256]{2,1,0:T(8,128)S(1)}, f32[2,512,256]{2,1,0:T(8,128)}, u32[]{:S(2)}, u32[]{:S(2)}) collective-permute-start(f32[2,512,256]{2,1,0:T(8,128)S(1)} %broadcast_select_fusion), channel_id=1, source_target_pairs={{0,8},{1,9},{14,6},{15,7},{16,24},{17,25},{30,22},{31,23},{32,40},... | collective-permute-start | bytes 3145736 | tf_op jit(solution)/shard_map/ppermute | solution.py:29
  160.8 31.0 %collective-permute-start.28 = (f32[2,512,256]{2,1,0:T(8,128)S(1)}, f32[2,512,256]{2,1,0:T(8,128)}, u32[]{:S(2)}, u32[]{:S(2)}) collective-permute-start(f32[2,512,256]{2,1,0:T(8,128)S(1)} %pad_maximum_fusion.4), channel_id=1, source_target_pairs={{0,1},{1,3},{2,0},{3,5},{4,2},{5,7},{6,4},{7,9},{8,6},{9,11},{10,8... | collective-permute-start | bytes 3145736 | tf_op jit(solution)/shard_map/ppermute | solution.py:29
  164.6 36.2 %collective-permute-start.29 = (f32[2,512,256]{2,1,0:T(8,128)S(1)}, f32[2,512,256]{2,1,0:T(8,128)}, u32[]{:S(2)}, u32[]{:S(2)}) collective-permute-start(f32[2,512,256]{2,1,0:T(8,128)S(1)} %pad_maximum_fusion.3.refs_4_), channel_id=1, source_target_pairs={{0,0},{1,2},{2,1},{3,4},{4,3},{5,6},{6,5},{7,8},{8,7},{9,10},{10,9... | collective-permute-start | bytes 3145736 | tf_op jit(solution)/shard_map/ppermute | solution.py:29
  169.3 41.3 %collective-permute-start.27 = (f32[2,512,256]{2,1,0:T(8,128)S(1)}, f32[2,512,256]{2,1,0:T(8,128)}, u32[]{:S(2)}, u32[]{:S(2)}) collective-permute-start(f32[2,512,256]{2,1,0:T(8,128)S(1)} %pad_maximum_fusion.2.refs_1_), channel_id=1, source_target_pairs={{16,0},{17,1},{18,2},{19,3},{20,4},{21,5},{22,6},{23,7},{24,8},{25... | collective-permute-start | bytes 3145736 | tf_op jit(solution)/shard_map/ppermute | solution.py:29
  174.3 39.1 %collective-permute-start.26 = (f32[2,512,256]{2,1,0:T(8,128)S(1)}, f32[2,512,256]{2,1,0:T(8,128)S(1)}, u32[]{:S(2)}, u32[]{:S(2)}) collective-permute-start(f32[2,512,256]{2,1,0:T(8,128)S(1)} %pad_maximum_fusion.1.refs_0_), channel_id=1, source_target_pairs={{0,16},{1,17},{2,18},{3,19},{4,20},{5,21},{6,22},{7,23},{8,24},{9,... | collective-permute-start | bytes 3145736 | tf_op jit(solution)/shard_map/ppermute | solution.py:29
  (37 other events, 256.6 us)
